TPU v7x, 32 devices: a whole 2x2x4 slice. The times are simulated.
32 devices in a mesh: fsdp: 8 (over y, x, core), tp: 4 (over z).
Axes of the slice: x: 2, y: 2, z: 4, core: 2. Of those that a mesh axis runs over, the one named last changes fastest.
Arguments:
- layer_input: bfloat16 [24576, 512], P(('fsdp', 'tp')), may hold values from -6 to 6
- segment_ids: int32 [24, 1024], P('fsdp'), may hold values from 0 to 15, never falling along the last dimension, each value on 1 to 512 neighbouring positions
- valid_mask: int32 [24576], P(('fsdp', 'tp')), may hold values from 0 to 1, as said below
- teacher: bfloat16 [24576, 512], P(('fsdp', 'tp')), may hold values from -6 to 6
- cotangent: bfloat16 [24576, 512], P(('fsdp', 'tp')), may hold values from -6 to 6
- ln1_gain: bfloat16 [512], P('fsdp'), may hold values from 0.099609375 to 1.8984375
- ln1_bias: bfloat16 [512], P('fsdp'), may hold values from -1.75 to 1.75
- w_q: bfloat16 [512, 512], P('fsdp', 'tp'), may hold values from -0.25 to 0.25
- w_k: bfloat16 [512, 512], P('fsdp', 'tp'), may hold values from -0.25 to 0.25
- w_v: bfloat16 [512, 512], P('fsdp', 'tp'), may hold values from -0.25 to 0.25
- b_q: bfloat16 [8, 64], P('tp', 'fsdp'), may hold values from -3 to 3
- b_v: bfloat16 [8, 64], P('tp', 'fsdp'), may hold values from -3 to 3
- w_o: bfloat16 [512, 512], P('tp', 'fsdp'), may hold values from -1 to 1
- b_o: bfloat16 [512], P('fsdp'), may hold values from -3 to 3
- ln2_gain: bfloat16 [512], P('fsdp'), may hold values from 0.099609375 to 1.8984375
- ln2_bias: bfloat16 [512], P('fsdp'), may hold values from -1.75 to 1.75
- w_up: bfloat16 [512, 2048], P('fsdp', 'tp'), may hold values from -0.25 to 0.25
- b_up: bfloat16 [32, 64], P('tp', 'fsdp'), may hold values from -3 to 3
- w_down: bfloat16 [2048, 512], P('tp', 'fsdp'), may hold values from -0.25 to 0.25
- b_down: bfloat16 [512], P('fsdp'), may hold values from -3 to 3
Outputs:
- layer_out: bfloat16 [24576, 512], P(('fsdp', 'tp'))
- loss: float32 [], replicated
- grad_layer_input: float32 [24576, 512], P(('fsdp', 'tp'))
- grad_ln1_gain: float32 [512], P('fsdp')
- grad_ln1_bias: float32 [512], P('fsdp')
- grad_w_q: float32 [512, 512], P('fsdp', 'tp')
- grad_w_k: float32 [512, 512], P('fsdp', 'tp')
- grad_w_v: float32 [512, 512], P('fsdp', 'tp')
- grad_b_q: float32 [8, 64], P('tp', 'fsdp')
- grad_b_v: float32 [8, 64], P('tp', 'fsdp')
- grad_w_o: float32 [512, 512], P('tp', 'fsdp')
- grad_b_o: float32 [512], P('fsdp')
- grad_ln2_gain: float32 [512], P('fsdp')
- grad_ln2_bias: float32 [512], P('fsdp')
- grad_w_up: float32 [512, 2048], P('fsdp', 'tp')
- grad_b_up: float32 [32, 64], P('tp', 'fsdp')
- grad_w_down: float32 [2048, 512], P('tp', 'fsdp')
- grad_b_down: float32 [512], P('fsdp')
Inputs may be any that keep to these rules, and one draw needn't show every extreme that they name: `segment_ids`: in each sequence the ids never fall, each document holds 1 to 512 positions, and one holds exactly 512. `valid_mask`: the first token of every sequence is 1.
All inputs are finite; a program needn't handle non-finite values.
Results may differ from a plain program's by a relative error of at most 0.014.
Values may be sent and summed in bfloat16 or wider, within the bound.
No kernel may reach another device: no remote copies, remote signals or barrier semaphores. Data moves between devices by JAX's collectives and lax.ppermute only.
A program may use at most 128 MiB of HBM per device.

v0:
```python
import jax
import jax.numpy as jnp
from jax import lax
from jax.sharding import PartitionSpec as P

D = 512
HD = 64
LEN = 1024


def layer_norm(values, gains, offsets):
    center = values - jnp.mean(values, axis=-1, keepdims=True)
    spread = jnp.mean(center * center, axis=-1, keepdims=True)
    return center * lax.rsqrt(spread + 1e-05) * gains + offsets


def quick_gelu(values):
    return values * jax.nn.sigmoid(1.702 * values)


def block_scores(query_block, key_seq, segment_seq, first_row):
    block_rows = query_block.shape[0]
    query_place = first_row + jnp.arange(block_rows, dtype=jnp.int32)
    key_place = jnp.arange(key_seq.shape[0], dtype=jnp.int32)
    query_segment = lax.dynamic_slice_in_dim(segment_seq, first_row, block_rows)
    allowed = (query_segment[:, None] == segment_seq[None, :]) & (
        key_place[None, :] <= query_place[:, None]
    )
    raw_scores = jnp.einsum(
        "qhd,khd->hqk", query_block, key_seq, preferred_element_type=jnp.float32
    ) * HD ** (-0.5)
    return jnp.where(allowed[None], raw_scores, -1e30)


def forward_sequence(inputs):
    query_seq, key_seq, value_seq, segment_seq = inputs

    def forward_one_block(element):
        block_index, query_block = element
        scores = block_scores(query_block, key_seq, segment_seq, block_index * query_block.shape[0])
        row_max = jnp.max(scores, axis=-1, keepdims=True)
        exponent = jnp.exp(scores - row_max)
        row_sum = jnp.sum(exponent, axis=-1, keepdims=True)
        weights = (exponent / row_sum).astype(jnp.bfloat16)
        attended = jnp.einsum(
            "hqk,khd->qhd", weights, value_seq, preferred_element_type=jnp.float32
        )
        return (attended.astype(jnp.bfloat16), (row_max + jnp.log(row_sum))[..., 0])

    return lax.map(forward_one_block, (jnp.arange(query_seq.shape[0], dtype=jnp.int32), query_seq))


def backward_sequence(inputs):
    query_seq, key_seq, value_seq, segment_seq, total_seq, grad_out_seq = inputs
    zero_grads = jnp.zeros(key_seq.shape, jnp.float32)

    def backward_one_block(carried, element):
        grad_keys, grad_values = carried
        block_index, query_block, total_block, grad_block = element
        scores = block_scores(query_block, key_seq, segment_seq, block_index * query_block.shape[0])
        weights = jnp.exp(scores - total_block[..., None])
        grad_values = grad_values + jnp.einsum(
            "hqk,qhd->khd",
            weights.astype(jnp.bfloat16),
            grad_block,
            preferred_element_type=jnp.float32,
        )
        grad_weights = jnp.einsum(
            "qhd,khd->hqk", grad_block, value_seq, preferred_element_type=jnp.float32
        )
        grad_scores = (
            weights * (grad_weights - jnp.sum(weights * grad_weights, axis=-1, keepdims=True))
        ).astype(jnp.bfloat16)
        grad_query = jnp.einsum(
            "hqk,khd->qhd", grad_scores, key_seq, preferred_element_type=jnp.float32
        ) * HD ** (-0.5)
        grad_keys = grad_keys + jnp.einsum(
            "hqk,qhd->khd", grad_scores, query_block, preferred_element_type=jnp.float32
        ) * HD ** (-0.5)
        return ((grad_keys, grad_values), grad_query.astype(jnp.bfloat16))

    (grad_keys, grad_values), grad_queries = lax.scan(
        backward_one_block,
        (zero_grads, zero_grads),
        (jnp.arange(query_seq.shape[0], dtype=jnp.int32), query_seq, total_seq, grad_out_seq),
    )
    return (grad_queries, grad_keys.astype(jnp.bfloat16), grad_values.astype(jnp.bfloat16))


def local(
    layer_input,
    segment_ids,
    valid_mask,
    teacher,
    cotangent,
    ln1_gain,
    ln1_bias,
    w_q,
    w_k,
    w_v,
    b_q,
    b_v,
    w_o,
    b_o,
    ln2_gain,
    ln2_bias,
    w_up,
    b_up,
    w_down,
    b_down,
):
    fsdp_size = lax.axis_size("fsdp")
    tensor_size = lax.axis_size("tp")
    local_rows = layer_input.shape[0]
    (
        gain_one,
        bias_one,
        query_w,
        key_w,
        value_w,
        query_b,
        value_b,
        out_w,
        out_b,
        gain_two,
        bias_two,
        upper_w,
        upper_b,
        lower_w,
        lower_b,
    ) = (
        lax.all_gather(ln1_gain, "fsdp", axis=0, tiled=True),
        lax.all_gather(ln1_bias, "fsdp", axis=0, tiled=True),
        lax.all_gather(w_q, "fsdp", axis=0, tiled=True),
        lax.all_gather(w_k, "fsdp", axis=0, tiled=True),
        lax.all_gather(w_v, "fsdp", axis=0, tiled=True),
        lax.all_gather(b_q, "fsdp", axis=1, tiled=True),
        lax.all_gather(b_v, "fsdp", axis=1, tiled=True),
        lax.all_gather(w_o, "fsdp", axis=1, tiled=True),
        lax.all_gather(b_o, "fsdp", axis=0, tiled=True),
        lax.all_gather(ln2_gain, "fsdp", axis=0, tiled=True),
        lax.all_gather(ln2_bias, "fsdp", axis=0, tiled=True),
        lax.all_gather(w_up, "fsdp", axis=0, tiled=True),
        lax.all_gather(b_up, "fsdp", axis=1, tiled=True),
        lax.all_gather(w_down, "fsdp", axis=1, tiled=True),
        lax.all_gather(b_down, "fsdp", axis=0, tiled=True),
    )
    mask_float = valid_mask.astype(jnp.float32)
    valid_total = lax.psum(jnp.sum(mask_float), ("fsdp", "tp"))
    tokens_all = local_rows * fsdp_size * tensor_size
    input_float = layer_input.astype(jnp.float32)
    gain_first = gain_one.astype(jnp.float32)
    bias_first = bias_one.astype(jnp.float32)
    gain_second = gain_two.astype(jnp.float32)
    bias_second = bias_two.astype(jnp.float32)
    normed_one = layer_norm(input_float, gain_first, bias_first).astype(jnp.bfloat16)
    head_count = query_w.shape[1] // HD
    rows_one = lax.all_gather(normed_one, "tp", axis=0, tiled=True)
    queries = (
        jnp.dot(rows_one, query_w, preferred_element_type=jnp.float32)
        + query_b.reshape(-1).astype(jnp.float32)
    ).astype(jnp.bfloat16)
    keys_all = jnp.dot(rows_one, key_w, preferred_element_type=jnp.float32).astype(jnp.bfloat16)
    values_all = (
        jnp.dot(rows_one, value_w, preferred_element_type=jnp.float32)
        + value_b.reshape(-1).astype(jnp.float32)
    ).astype(jnp.bfloat16)
    seq_count = segment_ids.shape[0]
    block_rows = min(512, LEN)
    block_count = LEN // block_rows
    shaped_queries = queries.reshape(seq_count, block_count, block_rows, head_count, HD)
    shaped_keys = keys_all.reshape(seq_count, LEN, head_count, HD)
    shaped_values = values_all.reshape(seq_count, LEN, head_count, HD)
    attended, log_totals = lax.map(
        forward_sequence, (shaped_queries, shaped_keys, shaped_values, segment_ids)
    )
    attended = attended.reshape(-1, head_count * HD)
    attention = lax.psum_scatter(
        jnp.dot(attended, out_w, preferred_element_type=jnp.float32).astype(jnp.bfloat16),
        "tp",
        scatter_dimension=0,
        tiled=True,
    ).astype(jnp.float32)
    hidden_one = input_float + attention + out_b.astype(jnp.float32)
    normed_two = layer_norm(hidden_one, gain_second, bias_second).astype(jnp.bfloat16)
    rows_two = lax.all_gather(normed_two, "tp", axis=0, tiled=True)
    pre_act = jnp.dot(rows_two, upper_w, preferred_element_type=jnp.float32) + upper_b.reshape(
        -1
    ).astype(jnp.float32)
    activated = quick_gelu(pre_act).astype(jnp.bfloat16)
    branch = lax.psum_scatter(
        jnp.dot(activated, lower_w, preferred_element_type=jnp.float32).astype(jnp.bfloat16),
        "tp",
        scatter_dimension=0,
        tiled=True,
    ).astype(jnp.float32)
    out_full = hidden_one + branch + lower_b.astype(jnp.float32)
    difference = out_full - teacher.astype(jnp.float32)
    square_part = jnp.sum(mask_float * jnp.mean(difference * difference, axis=-1))
    grad_out = (
        cotangent.astype(jnp.float32) + tokens_all / valid_total * mask_float[:, None] * difference
    )
    grad_lower_bias = jnp.sum(grad_out, axis=0)
    grad_out_low = grad_out.astype(jnp.bfloat16)
    grad_rows = lax.all_gather(grad_out_low, "tp", axis=0, tiled=True)
    grad_hidden_units = jnp.einsum(
        "nd,fd->nf", grad_rows, lower_w, preferred_element_type=jnp.float32
    )
    grad_lower = jnp.einsum("nf,nd->fd", activated, grad_rows, preferred_element_type=jnp.float32)
    gelu_value, gelu_pull = jax.vjp(quick_gelu, pre_act)
    grad_pre = gelu_pull(grad_hidden_units)[0].astype(jnp.bfloat16)
    grad_upper = jnp.einsum("nd,nf->df", rows_two, grad_pre, preferred_element_type=jnp.float32)
    grad_upper_bias = jnp.sum(grad_pre, axis=0, dtype=jnp.float32).reshape(upper_b.shape)
    grad_normed_two = lax.psum_scatter(
        jnp.einsum("nf,df->nd", grad_pre, upper_w, preferred_element_type=jnp.float32).astype(
            jnp.bfloat16
        ),
        "tp",
        scatter_dimension=0,
        tiled=True,
    ).astype(jnp.float32)
    norm_value, second_pull = jax.vjp(layer_norm, hidden_one, gain_second, bias_second)
    grad_hidden_norm, grad_gain_second, grad_bias_second = second_pull(grad_normed_two)
    grad_hidden = grad_out + grad_hidden_norm
    grad_out_bias = jnp.sum(grad_hidden, axis=0)
    grad_attn_low = grad_hidden.astype(jnp.bfloat16)
    grad_attn_rows = lax.all_gather(grad_attn_low, "tp", axis=0, tiled=True)
    grad_out_w = jnp.einsum(
        "nc,nd->cd", attended, grad_attn_rows, preferred_element_type=jnp.float32
    )
    grad_attended = jnp.einsum(
        "nd,cd->nc", grad_attn_rows, out_w, preferred_element_type=jnp.float32
    ).astype(jnp.bfloat16)
    grad_queries, grad_keys, grad_values = lax.map(
        backward_sequence,
        (
            shaped_queries,
            shaped_keys,
            shaped_values,
            segment_ids,
            log_totals,
            grad_attended.reshape(seq_count, block_count, block_rows, head_count, HD),
        ),
    )
    flat_queries = grad_queries.reshape(-1, head_count * HD)
    flat_keys = grad_keys.reshape(-1, head_count * HD)
    flat_values = grad_values.reshape(-1, head_count * HD)
    grad_query_w = jnp.einsum(
        "nd,nc->dc", rows_one, flat_queries, preferred_element_type=jnp.float32
    )
    grad_key_w = jnp.einsum("nd,nc->dc", rows_one, flat_keys, preferred_element_type=jnp.float32)
    grad_value_w = jnp.einsum(
        "nd,nc->dc", rows_one, flat_values, preferred_element_type=jnp.float32
    )
    grad_query_b = jnp.sum(flat_queries, axis=0, dtype=jnp.float32).reshape(query_b.shape)
    grad_value_b = jnp.sum(flat_values, axis=0, dtype=jnp.float32).reshape(value_b.shape)
    stacked_grads = jnp.concatenate((flat_queries, flat_keys, flat_values), axis=1)
    stacked_weights = jnp.concatenate((query_w, key_w, value_w), axis=1)
    grad_normed_one = lax.psum_scatter(
        jnp.einsum(
            "nc,dc->nd", stacked_grads, stacked_weights, preferred_element_type=jnp.float32
        ).astype(jnp.bfloat16),
        "tp",
        scatter_dimension=0,
        tiled=True,
    ).astype(jnp.float32)
    first_value, first_pull = jax.vjp(layer_norm, input_float, gain_first, bias_first)
    grad_input_norm, grad_gain_first, grad_bias_first = first_pull(grad_normed_one)
    grad_input = grad_hidden + grad_input_norm
    summed = lax.psum(
        (
            square_part,
            grad_gain_first,
            grad_bias_first,
            grad_out_bias,
            grad_gain_second,
            grad_bias_second,
            grad_lower_bias,
        ),
        ("fsdp", "tp"),
    )
    piece_size = D // fsdp_size
    piece_start = lax.axis_index("fsdp") * piece_size

    def own_piece(vector):
        return lax.dynamic_slice_in_dim(vector, piece_start, piece_size)

    loss = 0.5 * summed[0] / valid_total
    grad_wq, grad_wk, grad_wv, grad_bq, grad_bv, grad_wo, grad_wu, grad_bu, grad_wd = (
        lax.psum_scatter(
            grad_query_w.astype(jnp.bfloat16), "fsdp", scatter_dimension=0, tiled=True
        ).astype(jnp.float32),
        lax.psum_scatter(
            grad_key_w.astype(jnp.bfloat16), "fsdp", scatter_dimension=0, tiled=True
        ).astype(jnp.float32),
        lax.psum_scatter(
            grad_value_w.astype(jnp.bfloat16), "fsdp", scatter_dimension=0, tiled=True
        ).astype(jnp.float32),
        lax.psum_scatter(
            grad_query_b.astype(jnp.bfloat16), "fsdp", scatter_dimension=1, tiled=True
        ).astype(jnp.float32),
        lax.psum_scatter(
            grad_value_b.astype(jnp.bfloat16), "fsdp", scatter_dimension=1, tiled=True
        ).astype(jnp.float32),
        lax.psum_scatter(
            grad_out_w.astype(jnp.bfloat16), "fsdp", scatter_dimension=1, tiled=True
        ).astype(jnp.float32),
        lax.psum_scatter(
            grad_upper.astype(jnp.bfloat16), "fsdp", scatter_dimension=0, tiled=True
        ).astype(jnp.float32),
        lax.psum_scatter(
            grad_upper_bias.astype(jnp.bfloat16), "fsdp", scatter_dimension=1, tiled=True
        ).astype(jnp.float32),
        lax.psum_scatter(
            grad_lower.astype(jnp.bfloat16), "fsdp", scatter_dimension=1, tiled=True
        ).astype(jnp.float32),
    )
    return (
        out_full.astype(jnp.bfloat16),
        loss,
        grad_input,
        own_piece(summed[1]),
        own_piece(summed[2]),
        grad_wq,
        grad_wk,
        grad_wv,
        grad_bq,
        grad_bv,
        grad_wo,
        own_piece(summed[3]),
        own_piece(summed[4]),
        own_piece(summed[5]),
        grad_wu,
        grad_bu,
        grad_wd,
        own_piece(summed[6]),
    )


def solution(mesh):
    placed = (
        P(("fsdp", "tp"), None),
        P("fsdp", None),
        P(("fsdp", "tp")),
        P(("fsdp", "tp"), None),
        P(("fsdp", "tp"), None),
        P("fsdp"),
        P("fsdp"),
        P("fsdp", "tp"),
        P("fsdp", "tp"),
        P("fsdp", "tp"),
        P("tp", "fsdp"),
        P("tp", "fsdp"),
        P("tp", "fsdp"),
        P("fsdp"),
        P("fsdp"),
        P("fsdp"),
        P("fsdp", "tp"),
        P("tp", "fsdp"),
        P("tp", "fsdp"),
        P("fsdp"),
    )
    return jax.shard_map(
        local,
        mesh=mesh,
        in_specs=placed,
        out_specs=(
            P(("fsdp", "tp"), None),
            P(),
            P(("fsdp", "tp"), None),
            P("fsdp"),
            P("fsdp"),
            P("fsdp", "tp"),
            P("fsdp", "tp"),
            P("fsdp", "tp"),
            P("tp", "fsdp"),
            P("tp", "fsdp"),
            P("tp", "fsdp"),
            P("fsdp"),
            P("fsdp"),
            P("fsdp"),
            P("fsdp", "tp"),
            P("tp", "fsdp"),
            P("tp", "fsdp"),
            P("fsdp"),
        ),
        check_vma=False,
    )
```

profile of v0, /device:TPU:0, one launch (start us, length us, event | category | flops | bytes accessed | tf_op | source)
XLA Modules:
  0.0 948.7 jit_solution(11095047475518688719)
XLA Ops:
  14.4 16.0 %all-reduce.11 = (bf16[512]{0:T(512)(128)(2,1)}, bf16[512]{0:T(512)(128)(2,1)}, bf16[512]{0:T(512)(128)(2,1)}, bf16[512]{0:T(512)(128)(2,1)S(1)}, bf16[512]{0:T(512)(128)(2,1)S(1)}, /*index=5*/bf16[512]{0:T(512)(128)(2,1)}) all-reduce(bf16[512]{0:T(512)(128)(2,1)S(1)} %dynamic-update-slice.5, ...), channel_id=1, replica_groups=mesh['fsdp'=8,'tp'=4] {'fsdp'}, use_global_device_ids=true, to_apply=%add.5 | all-reduce | flops 3072 | bytes 12288
  43.7 8.8 all-gather.1
  52.6 8.2 all_gather.60
  60.8 9.3 all_gather.62
  70.1 8.2 all_gather.63
  78.2 10.2 %all_gather.65 = bf16[128,512]{0,1:T(8,128)(2,1)} all-gather(bf16[128,64]{0,1:T(8,128)(2,1)S(1)} %copy-done.51), channel_id=1, replica_groups=mesh['fsdp'=8,'tp'=4] {'fsdp'}, dimensions={1}, use_global_device_ids=true | all-gather | bytes 147456 | tf_op jit(solution)/shard_map/all_gather | solution.py:139
  88.5 10.3 %all-gather.7.cloned.1.call-done = bf16[3072,512]{1,0:T(8,128)(2,1)} async-done(((bf16[768,512]{1,0:T(8,128)(2,1)}), bf16[3072,512]{1,0:T(8,128)(2,1)}) %all-gather.7.cloned.1.call-update) | async-done | bytes 3145744 | tf_op jit(solution)/shard_map/all_gather | solution.py:158
  131.4 47.3 %while.54 = (s32[]{:T(128)}, bf16[3,2,512,2,64]{2,1,0,4,3:T(2,128)(2,1)}, f32[3,2,2,512]{3,2,1,0:T(2,128)}, bf16[3,2,512,2,64]{2,4,3,1,0:T(8,128)(2,1)S(1)}, s32...) while((s32[]{:T(128)}, ...), condition=%wide.region_7.8_spmd, body=%wide.region_2.7_spmd.sunk | while | flops 282656256 | bytes 17635796 | solution.py:174
  132.2 13.3 %while.57 = (s32[]{:T(128)}, bf16[2,512,2,64]{1,3,2,0:T(8,128)(2,1)S(1)}, f32[2,2,512]{2,1,0:T(2,128)S(1)}, s32[2]{0:T(128)S(1)}, s32[1024]{0:T(1024)S(1)}, /*in...) while((s32[]{:T(128)}, ...), condition=%wide.region_6.6_spmd, body=%wide.region_3.5_spmd.sunk | while | flops 282656256 | bytes 15513803 | solution.py:50
  148.0 13.3 %while.57 = (s32[]{:T(128)}, bf16[2,512,2,64]{1,3,2,0:T(8,128)(2,1)S(1)}, f32[2,2,512]{2,1,0:T(2,128)S(1)}, s32[2]{0:T(128)S(1)}, s32[1024]{0:T(1024)S(1)}, /*in...) while((s32[]{:T(128)}, ...), condition=%wide.region_6.6_spmd, body=%wide.region_3.5_spmd.sunk | while | flops 282656256 | bytes 15513803 | solution.py:50
  163.7 13.3 %while.57 = (s32[]{:T(128)}, bf16[2,512,2,64]{1,3,2,0:T(8,128)(2,1)S(1)}, f32[2,2,512]{2,1,0:T(2,128)S(1)}, s32[2]{0:T(128)S(1)}, s32[1024]{0:T(1024)S(1)}, /*in...) while((s32[]{:T(128)}, ...), condition=%wide.region_6.6_spmd, body=%wide.region_3.5_spmd.sunk | while | flops 282656256 | bytes 15513803 | solution.py:50
  184.9 58.4 %reduce-scatter.14.cloned.1.call-done = bf16[768,512]{1,0:T(8,128)(2,1)} async-done(((bf16[3072,512]{1,0:T(8,128)(2,1)}), bf16[768,512]{1,0:T(8,128)(2,1)}) %reduce-scatter.14.cloned.1.call-update) | async-done | bytes 786448 | tf_op jit(solution)/shard_map/reduce_scatter | solution.py:178
  246.8 8.9 all_gather.71
  255.8 10.8 %all_gather.70 = bf16[512,512]{1,0:T(8,128)(2,1)} all-gather(bf16[64,512]{1,0:T(8,128)(2,1)S(1)} %copy-done.38), channel_id=1, replica_groups=mesh['fsdp'=8,'tp'=4] {'fsdp'}, dimensions={0}, use_global_device_ids=true | all-gather | bytes 589824 | tf_op jit(solution)/shard_map/all_gather | solution.py:143
  266.6 9.9 %all_gather.72 = bf16[512,512]{0,1:T(8,128)(2,1)} all-gather(bf16[512,64]{0,1:T(8,128)(2,1)S(1)} %copy-done.39), channel_id=1, replica_groups=mesh['fsdp'=8,'tp'=4] {'fsdp'}, dimensions={1}, use_global_device_ids=true | all-gather | bytes 589824 | tf_op jit(solution)/shard_map/all_gather | solution.py:145
  276.6 33.8 %all-gather.9.cloned.1.call-done = bf16[3072,512]{1,0:T(8,128)(2,1)} async-done(((bf16[768,512]{1,0:T(8,128)(2,1)}), bf16[3072,512]{1,0:T(8,128)(2,1)}) %all-gather.9.cloned.1.call-update) | async-done | bytes 3145744 | tf_op jit(solution)/shard_map/all_gather | solution.py:186
  324.3 42.1 %psum.57 = f32[]{:T(128)} all-reduce(f32[]{:T(128)} %convert_reduce_fusion.3), channel_id=1, replica_groups=mesh['fsdp'=8,'tp'=4] {'fsdp','tp'}, use_global_device_ids=true, to_apply=%region_16.17 | all-reduce | flops 1 | bytes 8 | tf_op jit(solution)/shard_map/psum | solution.py:149
  367.1 15.9 %reduce-scatter.16.cloned.1.call-done = bf16[768,512]{1,0:T(8,128)(2,1)} async-done(((bf16[3072,512]{1,0:T(8,128)(2,1)}), bf16[768,512]{1,0:T(8,128)(2,1)}) %reduce-scatter.16.cloned.1.call-update) | async-done | bytes 786448 | tf_op jit(solution)/shard_map/reduce_scatter | solution.py:191
  388.3 63.5 %all-gather.11.cloned.1.call-done = bf16[3072,512]{1,0:T(8,128)(2,1)} async-done(((bf16[768,512]{1,0:T(8,128)(2,1)}), bf16[3072,512]{1,0:T(8,128)(2,1)}) %all-gather.11.cloned.1.call-update) | async-done | bytes 3145744 | tf_op jit(solution)/shard_map/all_gather | solution.py:205
  451.8 8.7 fusion.87
  465.9 59.0 %reduce-scatter.18.cloned.1.call-done = bf16[768,512]{1,0:T(8,128)(2,1)} async-done(((bf16[3072,512]{1,0:T(8,128)(2,1)}), bf16[768,512]{1,0:T(8,128)(2,1)}) %reduce-scatter.18.cloned.1.call-update) | async-done | bytes 786448 | tf_op jit(solution)/shard_map/reduce_scatter | solution.py:214
  546.0 52.0 %all-gather.13.cloned.1.call-done = bf16[3072,512]{1,0:T(8,128)(2,1)} async-done(((bf16[768,512]{1,0:T(8,128)(2,1)}), bf16[3072,512]{1,0:T(8,128)(2,1)}) %all-gather.13.cloned.1.call-update) | async-done | bytes 3145744 | tf_op jit(solution)/shard_map/all_gather | solution.py:227
  607.9 69.2 %while.56 = (s32[]{:T(128)}, bf16[3,2,512,2,64]{2,4,3,1,0:T(8,128)(2,1)}, bf16[3,1024,2,64]{1,3,2,0:T(8,128)(2,1)}, bf16[3,1024,2,64]{1,3,2,0:T(8,128)(2,1)}, bf...) while((s32[]{:T(128)}, ...), condition=%wide.region_24.25_spmd, body=%wide.region_20.24_spmd.sunk | while | flops 689438208 | bytes 45550196 | solution.py:234
  610.6 17.6 %while.58 = (s32[]{:T(128)}, f32[1024,2,64]{0,2,1:T(8,128)S(1)}, f32[1024,2,64]{0,2,1:T(8,128)}, bf16[2,512,2,64]{1,3,2,0:T(8,128)(2,1)S(1)}, bf16[2,512,2,64]{1...) while((s32[]{:T(128)}, f32[1024,2,64]{0,2,1:T(8,128)S(1)}, ...), condition=%wide.region_23.23_spmd.clone, body=%wide.region_21.22_spmd.clone.sunk | while | flops 689176064 | bytes 41330992 | solution.py:82
  633.7 17.6 %while.58 = (s32[]{:T(128)}, f32[1024,2,64]{0,2,1:T(8,128)S(1)}, f32[1024,2,64]{0,2,1:T(8,128)}, bf16[2,512,2,64]{1,3,2,0:T(8,128)(2,1)S(1)}, bf16[2,512,2,64]{1...) while((s32[]{:T(128)}, f32[1024,2,64]{0,2,1:T(8,128)S(1)}, ...), condition=%wide.region_23.23_spmd.clone, body=%wide.region_21.22_spmd.clone.sunk | while | flops 689176064 | bytes 41330992 | solution.py:82
  656.8 17.6 %while.58 = (s32[]{:T(128)}, f32[1024,2,64]{0,2,1:T(8,128)S(1)}, f32[1024,2,64]{0,2,1:T(8,128)}, bf16[2,512,2,64]{1,3,2,0:T(8,128)(2,1)S(1)}, bf16[2,512,2,64]{1...) while((s32[]{:T(128)}, f32[1024,2,64]{0,2,1:T(8,128)S(1)}, ...), condition=%wide.region_23.23_spmd.clone, body=%wide.region_21.22_spmd.clone.sunk | while | flops 689176064 | bytes 41330992 | solution.py:82
  705.8 13.7 %all-reduce.10 = (bf16[2,64]{1,0:T(2,128)(2,1)S(1)}, bf16[2,64]{1,0:T(2,128)(2,1)S(1)}, bf16[8,64]{1,0:T(8,128)(2,1)S(1)}) all-reduce(bf16[2,64]{1,0:T(2,128)(2,1)S(1)} %reduce_sum.233, bf16[2,64]{1,0:T(2,128)(2,1)S(1)} %reduce_sum.234, bf16[8,64]{1,0:T(8,128)(2,1)S(1)} %convert_element_type.247), channel_id=9, replica_groups=mesh['fsdp'=8,'tp'=4] {'fsdp'}, use_global_device_ids=true, to_apply=%region_36.37.clone | all-reduce | flops 768 | bytes 3072
  722.1 33.2 %reduce-scatter.22.cloned.1.call-done = bf16[64,128]{1,0:T(8,128)(2,1)} async-done(((bf16[512,128]{1,0:T(8,128)(2,1)}), bf16[64,128]{1,0:T(8,128)(2,1)}) %reduce-scatter.22.cloned.1.call-update) | async-done | bytes 16400 | tf_op jit(solution)/shard_map/reduce_scatter | solution.py:290
  756.6 34.9 %reduce-scatter.26.cloned.1.call-done = bf16[64,128]{1,0:T(8,128)(2,1)} async-done(((bf16[512,128]{1,0:T(8,128)(2,1)}), bf16[64,128]{1,0:T(8,128)(2,1)}) %reduce-scatter.26.cloned.1.call-update) | async-done | bytes 16400 | tf_op jit(solution)/shard_map/reduce_scatter | solution.py:296
  792.9 35.3 %reduce-scatter.24.cloned.1.call-done = bf16[64,128]{1,0:T(8,128)(2,1)} async-done(((bf16[512,128]{1,0:T(8,128)(2,1)}), bf16[64,128]{1,0:T(8,128)(2,1)}) %reduce-scatter.24.cloned.1.call-update) | async-done | bytes 16400 | tf_op jit(solution)/shard_map/reduce_scatter | solution.py:293
  829.6 61.1 %reduce-scatter.20.cloned.1.call-done = bf16[768,512]{1,0:T(8,128)(2,1)} async-done(((bf16[3072,512]{1,0:T(8,128)(2,1)}), bf16[768,512]{1,0:T(8,128)(2,1)}) %reduce-scatter.20.cloned.1.call-update) | async-done | bytes 786448 | tf_op jit(solution)/shard_map/reduce_scatter | solution.py:259
  893.4 40.6 %all-reduce.9 = (f32[]{:T(128)}, f32[512]{0:T(512)S(1)}, f32[512]{0:T(512)S(1)}, f32[512]{0:T(512)S(1)}, f32[512]{0:T(512)S(1)}, /*index=5*/f32[512]{0:T(512)S(1)}, f32[512]{0:T(512)S(1)}) all-reduce(f32[]{:T(128)} %multiply_reduce_fusion.3, f32[512]{0:T(512)S(1)} %get-tuple-element.340, ...), channel_id=1, replica_groups=mesh['fsdp'=8,'tp'=4] {'fsdp','tp'}, use_global_device_ids=true, to_apply=%region_14.15 | all-reduce | flops 3073 | bytes 24584 | tf_op jit(solution)/shard_map/psum | solution.py:270
  (466 shorter events, 267.4 us)
Async XLA Ops:
  7.2 45.4 %copy-start.48 = (bf16[64,128]{1,0:T(8,128)(2,1)S(1)}, bf16[64,128]{1,0:T(8,128)(2,1)}, u32[]{:S(2)}) copy-start(bf16[64,128]{1,0:T(8,128)(2,1)} %param.35) | copy-start | bytes 49156
  7.2 91.5 %all-gather.7.cloned.1.call-start = ((), (), s32[]{:S(2)}) async-start(), calls=%async_computation.10 | async-start | bytes 3932160 | tf_op jit(solution)/shard_map/all_gather | solution.py:158
  30.4 39.7 %copy-start.50 = (bf16[64,128]{1,0:T(8,128)(2,1)S(1)}, bf16[64,128]{1,0:T(8,128)(2,1)}, u32[]{:S(2)}) copy-start(bf16[64,128]{1,0:T(8,128)(2,1)} %param.37) | copy-start | bytes 49156
  30.4 47.8 %copy-start.51 = (bf16[128,64]{0,1:T(8,128)(2,1)S(1)}, bf16[128,64]{0,1:T(8,128)(2,1)}, u32[]{:S(2)}) copy-start(bf16[128,64]{0,1:T(8,128)(2,1)} %param.40) | copy-start | bytes 49156
  35.7 207.5 %reduce-scatter.14.cloned.1.call-start = ((), (), s32[]{:S(2)}) async-start(), calls=%async_computation.11 | async-start | bytes 3932160 | tf_op jit(solution)/shard_map/reduce_scatter | solution.py:178
  60.8 38.0 %copy-start.27 = (bf16[512,128]{1,0:T(8,128)(2,1)}, bf16[512,128]{1,0:T(8,128)(2,1)S(1)}, u32[]{:S(2)}) copy-start(bf16[512,128]{1,0:T(8,128)(2,1)S(1)} %all_gather.60) | copy-start | bytes 393220
  70.1 51.9 %copy-start.29 = (bf16[512,128]{1,0:T(8,128)(2,1)}, bf16[512,128]{1,0:T(8,128)(2,1)S(1)}, u32[]{:S(2)}) copy-start(bf16[512,128]{1,0:T(8,128)(2,1)S(1)} %all_gather.62) | copy-start | bytes 393220
  131.4 50.1 %copy-start.25 = (bf16[128,512]{0,1:T(8,128)(2,1)S(1)}, bf16[128,512]{0,1:T(8,128)(2,1)}, u32[]{:S(2)}) copy-start(bf16[128,512]{0,1:T(8,128)(2,1)} %all_gather.65) | copy-start | bytes 393220
  184.2 59.1 %copy-start.1 = (bf16[768,512]{1,0:T(8,128)(2,1)S(1)}, bf16[768,512]{1,0:T(8,128)(2,1)}, u32[]{:S(2)}) copy-start(bf16[768,512]{1,0:T(8,128)(2,1)} %param.28) | copy-start | bytes 2359300
  184.2 126.2 %all-gather.9.cloned.1.call-start = ((), (), s32[]{:S(2)}) async-start(), calls=%async_computation.12 | async-start | bytes 3932160 | tf_op jit(solution)/shard_map/all_gather | solution.py:186
  246.7 136.3 %reduce-scatter.16.cloned.1.call-start = ((), (), s32[]{:S(2)}) async-start(), calls=%async_computation.13 | async-start | bytes 3932160 | tf_op jit(solution)/shard_map/reduce_scatter | solution.py:191
  323.0 43.4 %copy-start.59 = (bf16[512]{0:T(512)(128)(2,1)S(1)}, bf16[512]{0:T(512)(128)(2,1)}, u32[]{:S(2)}) copy-start(bf16[512]{0:T(512)(128)(2,1)} %get-tuple-element.429) | copy-start | bytes 3076
  323.0 128.8 %all-gather.11.cloned.1.call-start = ((), (), s32[]{:S(2)}) async-start(), calls=%async_computation.14 | async-start | bytes 3932160 | tf_op jit(solution)/shard_map/all_gather | solution.py:205
  388.1 136.9 %reduce-scatter.18.cloned.1.call-start = ((), (), s32[]{:S(2)}) async-start(), calls=%async_computation.15 | async-start | bytes 3932160 | tf_op jit(solution)/shard_map/reduce_scatter | solution.py:214
  465.9 132.1 %all-gather.13.cloned.1.call-start = ((), (), s32[]{:S(2)}) async-start(), calls=%async_computation.16 | async-start | bytes 3932160 | tf_op jit(solution)/shard_map/all_gather | solution.py:227
  534.3 167.4 %reduce-scatter.32.cloned.1.call-start = ((), (), s32[]{:S(2)}) async-start(), calls=%async_computation.23 | async-start | bytes 589824 | tf_op jit(solution)/shard_map/reduce_scatter | solution.py:314
  539.9 163.3 %reduce-scatter.30.cloned.1.call-start = ((), (), s32[]{:S(2)}) async-start(), calls=%async_computation.22 | async-start | bytes 589824 | tf_op jit(solution)/shard_map/reduce_scatter | solution.py:308
  546.0 174.8 %reduce-scatter.28.cloned.1.call-start = ((), (), s32[]{:S(2)}) async-start(), calls=%async_computation.21 | async-start | bytes 147456 | tf_op jit(solution)/shard_map/reduce_scatter | solution.py:305
  686.5 68.8 %reduce-scatter.22.cloned.1.call-start = ((), (), s32[]{:S(2)}) async-start(), calls=%async_computation.18 | async-start | bytes 147456 | tf_op jit(solution)/shard_map/reduce_scatter | solution.py:290
  689.6 101.9 %reduce-scatter.26.cloned.1.call-start = ((), (), s32[]{:S(2)}) async-start(), calls=%async_computation.20 | async-start | bytes 147456 | tf_op jit(solution)/shard_map/reduce_scatter | solution.py:296
  692.5 135.7 %reduce-scatter.24.cloned.1.call-start = ((), (), s32[]{:S(2)}) async-start(), calls=%async_computation.19 | async-start | bytes 147456 | tf_op jit(solution)/shard_map/reduce_scatter | solution.py:293
  695.5 195.2 %reduce-scatter.20.cloned.1.call-start = ((), (), s32[]{:S(2)}) async-start(), calls=%async_computation.17 | async-start | bytes 3932160 | tf_op jit(solution)/shard_map/reduce_scatter | solution.py:259
  700.7 190.0 %copy-start.2 = (bf16[768,512]{1,0:T(8,128)(2,1)S(1)}, bf16[768,512]{1,0:T(8,128)(2,1)}, u32[]{:S(2)}) copy-start(bf16[768,512]{1,0:T(8,128)(2,1)} %param.28) | copy-start | bytes 2359300
  700.7 189.9 %copy-start.36 = (f32[768]{0:T(1024)S(1)}, f32[768]{0:T(1024)}, u32[]{:S(2)}) copy-start(f32[768]{0:T(1024)} %copy-done.35) | copy-start | bytes 9220
  700.7 189.9 %copy-start.43 = (f32[512]{0:T(512)S(1)}, f32[512]{0:T(512)}, u32[]{:S(2)}) copy-start(f32[512]{0:T(512)} %copy-done.42) | copy-start | bytes 6148
  700.8 191.7 %copy-start.45 = (f32[768]{0:T(1024)S(1)}, f32[768]{0:T(1024)}, u32[]{:S(2)}) copy-start(f32[768]{0:T(1024)} %copy-done.44) | copy-start | bytes 9220
  700.8 191.7 %copy-start.41 = (f32[768]{0:T(1024)S(1)}, f32[768]{0:T(1024)}, u32[]{:S(2)}) copy-start(f32[768]{0:T(1024)} %copy-done.40) | copy-start | bytes 9220
  705.5 187.9 %copy-start.53 = (f32[512]{0:T(512)S(1)}, f32[512]{0:T(512)}, u32[]{:S(2)}) copy-start(f32[512]{0:T(512)} %get-tuple-element.437) | copy-start | bytes 6148
  705.5 187.9 %copy-start.54 = (f32[512]{0:T(512)S(1)}, f32[512]{0:T(512)}, u32[]{:S(2)}) copy-start(f32[512]{0:T(512)} %get-tuple-element.338) | copy-start | bytes 6148
  705.5 187.9 %copy-start.55 = (f32[512]{0:T(512)S(1)}, f32[512]{0:T(512)}, u32[]{:S(2)}) copy-start(f32[512]{0:T(512)} %get-tuple-element.439) | copy-start | bytes 6148
  705.5 187.9 %copy-start.56 = (f32[512]{0:T(512)S(1)}, f32[512]{0:T(512)}, u32[]{:S(2)}) copy-start(f32[512]{0:T(512)} %get-tuple-element.343) | copy-start | bytes 6148
  705.5 233.4 %copy-start.11 = (f32[768,512]{1,0:T(8,128)S(1)}, f32[768,512]{1,0:T(8,128)}, u32[]{:S(2)}) copy-start(f32[768,512]{1,0:T(8,128)} %copy-done.10) | copy-start | bytes 4718596
  (59 other events, 333.3 us)
Sparse Core Ops, SparseCore 0:
  35.8 62.8 all-gather.6
  184.3 58.8 reduce-scatter.13
  246.8 63.5 all-gather.8
  323.2 59.8 reduce-scatter.15
  388.2 63.5 all-gather.10
  466.0 58.8 reduce-scatter.17
  534.4 63.5 all-gather.12
  601.1 32.8 reduce-scatter.31
  637.4 34.1 reduce-scatter.29
  686.6 31.9 reduce-scatter.27
  721.9 33.3 reduce-scatter.21
  758.2 33.3 reduce-scatter.25
  794.8 33.3 reduce-scatter.23
  830.4 60.2 reduce-scatter.19
where the time goes:
time: 957 us; the launch traced here: 949 us
  waiting for transfers between devices  458 us (48%)
  blocking collectives  194 us (20%)
  matrix products  117 us (12%)
  local copies, waits for them, and re-layouts  86.9 us (9%)
  other arithmetic  63 us (7%)
  between operations  19.7 us (2%)
    all_gather x1, waiting for transfers between devices, local(): grad_rows = lax.all_gather(grad_out_low, 'tp', axis=0, tiled=True)  63.5 us
    reduce_scatter x1, waiting for transfers between devices, local(): lax.psum_scatter(jnp.einsum('nc,dc->nd', stacked_grads, stacked_weights,...  61.1 us
    reduce_scatter x1, waiting for transfers between devices, local(): lax.psum_scatter(jnp.einsum('nf,df->nd', grad_pre, upper_w, preferred_ele...  59 us
    reduce_scatter x1, waiting for transfers between devices, local(): lax.psum_scatter(jnp.dot(attended, out_w, preferred_element_type=jnp.floa...  58.4 us
    all_gather x1, waiting for transfers between devices, local(): grad_attn_rows = lax.all_gather(grad_attn_low, 'tp', axis=0, tiled=True)  52 us
    psum x1, blocking collectives, local(): valid_total = lax.psum(jnp.sum(mask_float), ('fsdp', 'tp'))  42.1 us
    psum x1, blocking collectives, local(): lax.psum((square_part, grad_gain_first, grad_bias_first, grad_out_bias, g...  40.6 us
    reduce_scatter x1, waiting for transfers between devices, local(): lax.psum_scatter(grad_key_w.astype(jnp.bfloat16), 'fsdp', scatter_dimensi...  35.3 us
  transfers between devices with their start and end apart: 14, of which 11 were waited for; matrix products, arithmetic and copies ran while one was open for 13% of the time, Pallas kernels for 0%

commit v1 on v0

v1 whole, which is shorter than its diff:
```python
import functools

import jax
import jax.numpy as jnp
from jax import lax
from jax.experimental import pallas as pl
from jax.experimental.pallas import tpu as pltpu
from jax.sharding import PartitionSpec as P

D = 512
H = 8
HD = 64
LEN = 1024
HALO = 512
PAIR = 2 * HD
NEG = -1e30
SCALE = HD ** (-0.5)
F32 = jnp.float32
BF16 = jnp.bfloat16
MIB = 1 << 20

CONTRACT_LAST = (((1,), (1,)), ((), ()))


def dot(a, b):
    return jnp.dot(a, b, preferred_element_type=F32)


def dot_t(a, b):
    return lax.dot_general(a, b, CONTRACT_LAST, preferred_element_type=F32)


def normalize(x):
    center = x - jnp.mean(x, axis=-1, keepdims=True)
    rstd = lax.rsqrt(jnp.mean(center * center, axis=-1, keepdims=True) + 1e-05)
    return center * rstd, rstd


def norm_pull(g, gain, xhat, rstd):
    gx = g * gain
    return rstd * (
        gx
        - jnp.mean(gx, axis=-1, keepdims=True)
        - xhat * jnp.mean(gx * xhat, axis=-1, keepdims=True)
    )


def fold(x):
    return jnp.sum(x.reshape(x.shape[0] // 8, 8, x.shape[1]), axis=0)


def rows_of(start, size, unit=128):
    return pl.ds(pl.multiple_of(start, unit), size)


def forward_kernel(
    qb, x_ref, vec_ref, w_ref, idr_ref, idc_ref, n_ref, q_ref, k_ref, v_ref, o_ref, lse_ref, bias_ref, stat_ref
):
    ext, own = x_ref.shape[0], o_ref.shape[0]
    window = HALO + qb

    def project(i, carry):
        rows = rows_of(i * 128, 128)
        xhat, _ = normalize(x_ref[rows, :].astype(F32))
        n1 = (xhat * vec_ref[0:1, :] + vec_ref[1:2, :]).astype(BF16)
        n_ref[rows, :] = n1
        k_ref[rows, :] = dot(n1, w_ref[:, D : 2 * D]).astype(BF16)
        v_ref[rows, :] = (dot(n1, w_ref[:, 2 * D : 3 * D]) + vec_ref[3:4, :]).astype(BF16)
        return carry

    lax.fori_loop(0, ext // 128, project, 0)

    def project_q(i, carry):
        rows = rows_of(i * 128, 128)
        q = dot(n_ref[rows_of(HALO + i * 128, 128), :], w_ref[:, 0:D]) + vec_ref[2:3, :]
        q_ref[rows, :] = q.astype(BF16) * jnp.asarray(SCALE, BF16)
        return carry

    lax.fori_loop(0, own // 128, project_q, 0)

    def query_block(i, carry):
        first = i * qb
        key = lax.broadcasted_iota(jnp.int32, (qb, window), 1)
        query = lax.broadcasted_iota(jnp.int32, (qb, window), 0)
        same = idc_ref[rows_of(HALO + first, qb), :] == idr_ref[:, rows_of(first, window)]
        bias_ref[...] = jnp.where(same & (key <= query + HALO), 0.0, NEG)

        def pair(g, inner):
            lanes = rows_of(g * PAIR, PAIR)
            lane = lax.broadcasted_iota(jnp.int32, (qb, PAIR), 1)
            keys = k_ref[rows_of(first, window), lanes]
            values = v_ref[rows_of(first, window), lanes]
            both = q_ref[rows_of(first, qb), lanes]
            got = None
            for h in range(2):
                mine = (lane < HD) if h == 0 else (lane >= HD)
                s = dot_t(jnp.where(mine, both, jnp.zeros_like(both)), keys) + bias_ref[...]
                top = jnp.max(s, axis=-1, keepdims=True)
                p = jnp.exp(s - top)
                total = jnp.sum(p, axis=-1, keepdims=True)
                o = dot(p.astype(BF16), values) / total
                got = o if h == 0 else jnp.where(mine, o, got)
                stat_ref[...] = jnp.where(lane == 2 * g + h, top + jnp.log(total), stat_ref[...])
            o_ref[rows_of(first, qb), lanes] = got.astype(BF16)
            return inner

        lax.fori_loop(0, D // PAIR, pair, 0)
        lse_ref[:, rows_of(first, qb)] = jnp.transpose(stat_ref[...])[0:H, :]
        return carry

    stat_ref[...] = jnp.zeros_like(stat_ref)
    lax.fori_loop(0, own // qb, query_block, 0)


def attention_forward(x_ext, vecs, w_qkv, id_row, id_col, own):
    ext = x_ext.shape[0]
    qb = 256 if own % 256 == 0 else 128
    shapes = (
        jax.ShapeDtypeStruct((ext, D), BF16),
        jax.ShapeDtypeStruct((own, D), BF16),
        jax.ShapeDtypeStruct((ext, D), BF16),
        jax.ShapeDtypeStruct((ext, D), BF16),
        jax.ShapeDtypeStruct((own, D), BF16),
        jax.ShapeDtypeStruct((H, own), F32),
    )
    return pl.pallas_call(
        functools.partial(forward_kernel, qb),
        out_shape=shapes,
        scratch_shapes=[pltpu.VMEM((qb, HALO + qb), F32), pltpu.VMEM((qb, 128), F32)],
        compiler_params=pltpu.CompilerParams(vmem_limit_bytes=48 * MIB),
        name="attention_forward",
    )(x_ext, vecs, w_qkv, id_row, id_col)


def middle_kernel(
    rb,
    scale_ref,
    x_ref,
    o_ref,
    teacher_ref,
    cot_ref,
    mask_ref,
    vec_ref,
    bup_ref,
    wo_ref,
    wup_ref,
    wdn_ref,
    out_ref,
    gh_ref,
    go_ref,
    delta_ref,
    gwo_ref,
    gwup_ref,
    gwdn_ref,
    small_ref,
    gbup_ref,
    slope_ref,
    hid_ref,
    gpre_ref,
    n2t_ref,
    gmlpt_ref,
    gattnt_ref,
):
    own = x_ref.shape[0]
    ff = wup_ref.shape[1]
    chunk = 512
    small_ref[...] = jnp.zeros_like(small_ref)
    head_of = lax.broadcasted_iota(jnp.int32, (D, 128), 0) // HD
    pick = (head_of == lax.broadcasted_iota(jnp.int32, (D, 128), 1)).astype(BF16)

    def block(i, carry):
        rows = rows_of(i * rb, rb)
        out_bias, gain, offset, down_bias = (vec_ref[j : j + 1, :] for j in range(4))
        h1 = x_ref[rows, :].astype(F32) + dot_t(o_ref[rows, :], wo_ref[...]) + out_bias
        xhat, rstd = normalize(h1)
        n2 = xhat * gain + offset
        n2_low = n2.astype(BF16)
        n2t_ref[:, rows] = jnp.transpose(n2).astype(BF16)
        for c in range(0, ff, chunk):
            pre = dot(n2_low, wup_ref[:, c : c + chunk]) + bup_ref[:, c : c + chunk]
            s = jax.nn.sigmoid(1.702 * pre)
            value = pre * s
            hid_ref[rows, c : c + chunk] = value.astype(BF16)
            slope_ref[:, c : c + chunk] = s + 1.702 * value * (1.0 - s)
        out = h1 + dot_t(hid_ref[rows, :], wdn_ref[...]) + down_bias
        out_ref[rows, :] = out.astype(BF16)
        valid = mask_ref[rows, :]
        diff = (out - teacher_ref[rows, :].astype(F32)) * valid
        g_out = cot_ref[rows, :].astype(F32) + scale_ref[0, 0] * diff
        small_ref[0:8, :] += fold(g_out)
        small_ref[8:16, :] += fold(diff * diff)
        g_mlp = g_out.astype(BF16)
        gmlpt_ref[:, rows] = jnp.transpose(g_out).astype(BF16)
        for c in range(0, ff, chunk):
            g_hid = dot(g_mlp, wdn_ref[:, c : c + chunk])
            gpre_ref[rows, c : c + chunk] = (g_hid * slope_ref[:, c : c + chunk]).astype(BF16)
        g_n2 = dot_t(gpre_ref[rows, :], wup_ref[...])
        small_ref[16:24, :] += fold(g_n2 * xhat)
        small_ref[24:32, :] += fold(g_n2)
        g_h1 = g_out + norm_pull(g_n2, gain, xhat, rstd)
        gh_ref[rows, :] = g_h1
        small_ref[32:40, :] += fold(g_h1)
        gattnt_ref[:, rows] = jnp.transpose(g_h1).astype(BF16)
        g_o = dot(g_h1.astype(BF16), wo_ref[...]).astype(BF16)
        go_ref[rows, :] = g_o
        product = g_o.astype(F32) * o_ref[rows, :].astype(F32)
        high = product.astype(BF16)
        low = (product - high.astype(F32)).astype(BF16)
        delta_ref[:, rows] = jnp.transpose(dot(high, pick) + dot(low, pick))[0:H, :]
        return carry

    lax.fori_loop(0, own // rb, block, 0)
    ones = jnp.ones((8, own), BF16)

    def grads(i, carry):
        cols = rows_of(i * chunk, chunk)
        gwdn_ref[:, cols] = dot(gmlpt_ref[...], hid_ref[:, cols]).astype(BF16)
        gwup_ref[:, cols] = dot(n2t_ref[...], gpre_ref[:, cols]).astype(BF16)
        gbup_ref[:, cols] = dot(ones, gpre_ref[:, cols])
        return carry

    lax.fori_loop(0, ff // chunk, grads, 0)
    gwo_ref[...] = dot(gattnt_ref[...], o_ref[...]).astype(BF16)


def middle(scale, x, o, teacher, cot, mask, vecs, b_up, w_o, w_up, w_dn):
    own, ff = x.shape[0], w_up.shape[1]
    rb = 256 if own % 256 == 0 else 128
    shapes = (
        jax.ShapeDtypeStruct((own, D), BF16),
        jax.ShapeDtypeStruct((own, D), F32),
        jax.ShapeDtypeStruct((own, D), BF16),
        jax.ShapeDtypeStruct((H, own), F32),
        jax.ShapeDtypeStruct((D, D), BF16),
        jax.ShapeDtypeStruct((D, ff), BF16),
        jax.ShapeDtypeStruct((D, ff), BF16),
        jax.ShapeDtypeStruct((40, D), F32),
        jax.ShapeDtypeStruct((8, ff), F32),
    )
    whole = pl.BlockSpec(memory_space=pltpu.VMEM)
    return pl.pallas_call(
        functools.partial(middle_kernel, rb),
        out_shape=shapes,
        in_specs=[pl.BlockSpec(memory_space=pltpu.SMEM)] + [whole] * 10,
        out_specs=[whole] * len(shapes),
        scratch_shapes=[
            pltpu.VMEM((rb, ff), F32),
            pltpu.VMEM((own, ff), BF16),
            pltpu.VMEM((own, ff), BF16),
            pltpu.VMEM((D, own), BF16),
            pltpu.VMEM((D, own), BF16),
            pltpu.VMEM((D, own), BF16),
        ],
        compiler_params=pltpu.CompilerParams(vmem_limit_bytes=56 * MIB),
        name="middle",
    )(scale, x, o, teacher, cot, mask, vecs, b_up, w_o, w_up, w_dn)


def backward_kernel(
    qb,
    q_ref,
    k_ref,
    v_ref,
    go_ref,
    lse_ref,
    delta_ref,
    idr_ref,
    idc_ref,
    n_ref,
    x_ref,
    w_ref,
    gn_halo_ref,
    gn_ref,
    gw_ref,
    small_ref,
    bias_ref,
    kt_ref,
    nt_ref,
    dqt_ref,
    dk_ref,
    dv_ref,
    g_ref,
):
    ext, own = k_ref.shape[0], q_ref.shape[0]
    window = HALO + qb
    dk_ref[...] = jnp.zeros_like(dk_ref)
    dv_ref[...] = jnp.zeros_like(dv_ref)
    small_ref[...] = jnp.zeros_like(small_ref)

    def turn(i, carry):
        rows = rows_of(i * 128, 128)
        kt_ref[:, rows] = jnp.transpose(k_ref[rows, :].astype(F32)).astype(BF16)
        nt_ref[:, rows] = jnp.transpose(n_ref[rows, :].astype(F32)).astype(BF16)
        return carry

    lax.fori_loop(0, ext // 128, turn, 0)

    def query_block(i, carry):
        first = i * qb
        key = lax.broadcasted_iota(jnp.int32, (window, qb), 0)
        query = lax.broadcasted_iota(jnp.int32, (window, qb), 1)
        same = idc_ref[rows_of(first, window), :] == idr_ref[:, rows_of(HALO + first, qb)]
        bias_ref[...] = jnp.where(same & (key <= query + HALO), 0.0, NEG)

        def pair(g, inner):
            lanes = rows_of(g * PAIR, PAIR)
            lane = lax.broadcasted_iota(jnp.int32, (qb, PAIR), 1)
            keys = k_ref[rows_of(first, window), lanes]
            values = v_ref[rows_of(first, window), lanes]
            both_q = q_ref[rows_of(first, qb), lanes]
            both_g = go_ref[rows_of(first, qb), lanes]
            all_lse = lse_ref[:, rows_of(first, qb)]
            all_delta = delta_ref[:, rows_of(first, qb)]
            line = lax.broadcasted_iota(jnp.int32, (H, qb), 0)
            dk, dv = None, None
            for h in range(2):
                head = 2 * g + h
                mine = (lane < HD) if h == 0 else (lane >= HD)
                q = jnp.where(mine, both_q, jnp.zeros_like(both_q))
                g_o = jnp.where(mine, both_g, jnp.zeros_like(both_g))
                lse = jnp.sum(jnp.where(line == head, all_lse, 0.0), axis=0, keepdims=True)
                delta = jnp.sum(jnp.where(line == head, all_delta, 0.0), axis=0, keepdims=True)
                p = jnp.exp(dot_t(keys, q) + bias_ref[...] - lse)
                ds = (p * (dot_t(values, g_o) - delta)).astype(BF16)
                dv_h = dot(p.astype(BF16), g_o)
                dk_h = dot(ds, q)
                dk, dv = (dk_h, dv_h) if h == 0 else (dk + dk_h, dv + dv_h)
                dqt_ref[rows_of(head * HD, HD, HD), rows_of(first, qb)] = dot(
                    kt_ref[rows_of(head * HD, HD, HD), rows_of(first, window)], ds
                )
            dk_ref[rows_of(first, window), lanes] += dk
            dv_ref[rows_of(first, window), lanes] += dv
            return inner

        lax.fori_loop(0, D // PAIR, pair, 0)
        return carry

    lax.fori_loop(0, own // qb, query_block, 0)

    def gather(i, carry):
        rows = rows_of(i * 128, 128)
        g_ref[rows, D : 2 * D] = dk_ref[rows, :].astype(BF16)
        g_ref[rows, 2 * D : 3 * D] = dv_ref[rows, :].astype(BF16)
        return carry

    lax.fori_loop(0, ext // 128, gather, 0)

    def gather_q(i, carry):
        cols = rows_of(i * 128, 128)
        g_ref[rows_of(HALO + i * 128, 128), 0:D] = (jnp.transpose(dqt_ref[:, cols]) * SCALE).astype(BF16)
        return carry

    lax.fori_loop(0, own // 128, gather_q, 0)

    def norms(rows, g_n1):
        xhat, _ = normalize(x_ref[rows, :].astype(F32))
        small_ref[0:8, :] += fold(g_n1 * xhat)
        small_ref[8:16, :] += fold(g_n1)

    def pull_halo(i, carry):
        rows = rows_of(i * 128, 128)
        g_n1 = dot_t(g_ref[rows, D : 3 * D], w_ref[:, D : 3 * D])
        gn_halo_ref[rows, :] = g_n1.astype(BF16)
        norms(rows, g_n1)
        return carry

    lax.fori_loop(0, HALO // 128, pull_halo, 0)

    def pull_own(i, carry):
        rows = rows_of(HALO + i * 128, 128)
        g_n1 = dot_t(g_ref[rows, :], w_ref[...])
        gn_ref[rows_of(i * 128, 128), :] = g_n1
        norms(rows, g_n1)
        return carry

    lax.fori_loop(0, own // 128, pull_own, 0)
    gw_ref[:, 0:D] = dot(nt_ref[:, HALO:], g_ref[HALO:, 0:D]).astype(BF16)
    gw_ref[:, D : 2 * D] = dot(nt_ref[...], g_ref[:, D : 2 * D]).astype(BF16)
    gw_ref[:, 2 * D : 3 * D] = dot(nt_ref[...], g_ref[:, 2 * D : 3 * D]).astype(BF16)
    small_ref[16:24, :] = dot(jnp.ones((8, own), BF16), g_ref[HALO:, 0:D])
    small_ref[24:32, :] = dot(jnp.ones((8, ext), BF16), g_ref[:, 2 * D : 3 * D])


def attention_backward(q, k, v, g_o, lse, delta, id_row, id_col, n1, x_ext, w_qkv):
    ext, own = k.shape[0], q.shape[0]
    qb = 256 if own % 256 == 0 else 128
    shapes = (
        jax.ShapeDtypeStruct((HALO, D), BF16),
        jax.ShapeDtypeStruct((own, D), F32),
        jax.ShapeDtypeStruct((D, 3 * D), BF16),
        jax.ShapeDtypeStruct((32, D), F32),
    )
    return pl.pallas_call(
        functools.partial(backward_kernel, qb),
        out_shape=shapes,
        scratch_shapes=[
            pltpu.VMEM((HALO + qb, qb), F32),
            pltpu.VMEM((D, ext), BF16),
            pltpu.VMEM((D, ext), BF16),
            pltpu.VMEM((D, own), F32),
            pltpu.VMEM((ext, D), F32),
            pltpu.VMEM((ext, D), F32),
            pltpu.VMEM((ext, 3 * D), BF16),
        ],
        compiler_params=pltpu.CompilerParams(vmem_limit_bytes=56 * MIB),
        name="attention_backward",
    )(q, k, v, g_o, lse, delta, id_row, id_col, n1, x_ext, w_qkv)


def finish_kernel(x_ref, gn_ref, gh_ref, vec_ref, out_ref):
    def block(i, carry):
        rows = rows_of(i * 128, 128)
        xhat, rstd = normalize(x_ref[rows, :].astype(F32))
        out_ref[rows, :] = gh_ref[rows, :] + norm_pull(gn_ref[rows, :], vec_ref[0:1, :], xhat, rstd)
        return carry

    lax.fori_loop(0, x_ref.shape[0] // 128, block, 0)


def finish(x, g_n1, g_h1, vecs):
    return pl.pallas_call(
        finish_kernel,
        out_shape=jax.ShapeDtypeStruct(x.shape, F32),
        compiler_params=pltpu.CompilerParams(vmem_limit_bytes=32 * MIB),
        name="finish",
    )(x, g_n1, g_h1, vecs)


def hops(rows):
    plan, left, step = [], HALO, 1
    while left > 0:
        take = min(rows, left)
        plan.append((step, take))
        left, step = left - take, step + 1
    return plan


def local(
    layer_input,
    segment_ids,
    valid_mask,
    teacher,
    cotangent,
    ln1_gain,
    ln1_bias,
    w_q,
    w_k,
    w_v,
    b_q,
    b_v,
    w_o,
    b_o,
    ln2_gain,
    ln2_bias,
    w_up,
    b_up,
    w_down,
    b_down,
):
    fsdp_size = lax.axis_size("fsdp")
    tensor_size = lax.axis_size("tp")
    place = lax.axis_index("tp")
    own = layer_input.shape[0]
    tokens_all = own * fsdp_size * tensor_size
    rows_d = w_q.shape[0]
    cols_h, cols_f = w_q.shape[1], w_up.shape[1]

    parts = []
    for step, take in hops(own):
        route = [(i, i + step) for i in range(tensor_size - step)]
        parts.insert(0, lax.ppermute(layer_input[own - take :], "tp", route))
    x_ext = jnp.concatenate(parts + [layer_input], axis=0)
    ids = segment_ids + LEN * jnp.arange(segment_ids.shape[0], dtype=jnp.int32)[:, None]
    ids = jnp.concatenate([jnp.full((HALO,), -1, jnp.int32), ids.reshape(-1)])
    ids = lax.dynamic_slice_in_dim(ids, place * own, HALO + own)
    id_row, id_col = ids[None, :], ids[:, None]

    pack = jnp.concatenate([w_q, w_k, w_v, w_o.T, w_up, w_down.T], axis=1)
    count = jnp.sum(valid_mask)
    count_high = count // 256
    vectors = jnp.concatenate([ln1_gain, ln1_bias, b_o, ln2_gain, ln2_bias, b_down])
    heads = jnp.concatenate([b_q.reshape(-1), b_v.reshape(-1), b_up.reshape(-1)])
    digits = jnp.stack([count_high, count - 256 * count_high]).astype(BF16)
    small = jnp.concatenate([vectors, heads, digits])
    width = pack.shape[1]
    lines = -(-small.shape[0] // width)
    small = jnp.pad(small, (0, lines * width - small.shape[0])).reshape(lines, width)
    shard = jnp.concatenate([pack, small], axis=0)
    every = lax.all_gather(lax.all_gather(shard, "tp", axis=0), "fsdp", axis=0)
    big = every[:, :, :rows_d, :]

    def columns(start, size):
        part = big[:, :, :, start : start + size]
        return part.transpose(0, 2, 1, 3).reshape(fsdp_size * rows_d, tensor_size * size)

    w_qkv = jnp.concatenate([columns(j * cols_h, cols_h) for j in range(3)], axis=1)
    w_ot = columns(3 * cols_h, cols_h)
    w_up_all = columns(4 * cols_h, cols_f)
    w_dn_all = columns(4 * cols_h + cols_f, cols_f)
    few = every[:, :, rows_d:, :].reshape(fsdp_size, tensor_size, -1).astype(F32)
    six = few[:, 0, : 6 * rows_d].reshape(fsdp_size, 6, rows_d).transpose(1, 0, 2).reshape(6, D)
    at = 6 * rows_d

    def by_head(start, shape):
        size = shape[0] * shape[1]
        part = few[:, :, start : start + size].reshape((fsdp_size, tensor_size) + shape)
        return part.transpose(1, 2, 0, 3).reshape(1, -1)

    bq_all = by_head(at, b_q.shape)
    at += b_q.size
    bv_all = by_head(at, b_v.shape)
    at += b_v.size
    bup_all = by_head(at, b_up.shape)
    at += b_up.size
    valid_total = 256.0 * jnp.sum(few[:, :, at]) + jnp.sum(few[:, :, at + 1])

    vec_one = jnp.concatenate([six[0:2], bq_all, bv_all], axis=0)
    vec_two = jnp.stack([six[2], six[3], six[4], six[5]])
    n1, q, k, v, o, lse = attention_forward(x_ext, vec_one, w_qkv, id_row, id_col, own)
    scale = (tokens_all / valid_total).reshape(1, 1)
    mask = valid_mask.astype(F32)[:, None]
    layer_out, g_h1, g_o, delta, g_wo, g_wup, g_wdn, small_two, g_bup = middle(
        scale, layer_input, o, teacher, cotangent, mask, vec_two, bup_all, w_ot, w_up_all, w_dn_all
    )
    gn_halo, gn_own, g_qkv, small_one = attention_backward(
        q, k, v, g_o, lse, delta, id_row, id_col, n1, x_ext, w_qkv
    )

    total = gn_own
    left = HALO
    for step, take in hops(own):
        route = [(i + step, i) for i in range(tensor_size - step)]
        part = lax.ppermute(gn_halo[left - take : left], "tp", route).astype(F32)
        total = total + jnp.pad(part, ((own - take, 0), (0, 0)))
        left -= take
    grad_input = finish(layer_input, total, g_h1, vec_one)

    def split(grad, size):
        return grad.reshape(fsdp_size, rows_d, tensor_size, size).transpose(0, 2, 1, 3)

    g_pack = jnp.concatenate(
        [split(g_qkv[:, j * D : (j + 1) * D], cols_h) for j in range(3)]
        + [split(g_wo, cols_h), split(g_wup, cols_f), split(g_wdn, cols_f)],
        axis=3,
    )
    ones = [small_one[8 * j : 8 * j + 8].sum(0) for j in range(2)] + [small_one[16], small_one[24]]
    twos = [small_two[8 * j : 8 * j + 8].sum(0) for j in range(5)]
    loss_part = 0.5 / D * jnp.sum(twos[1]) / valid_total
    six_grads = jnp.stack([ones[0], ones[1], twos[4], twos[2], twos[3], twos[0]])
    six_grads = six_grads.reshape(6, fsdp_size, 1, rows_d).transpose(1, 2, 0, 3)
    six_grads = jnp.broadcast_to(
        six_grads.reshape(fsdp_size, 1, -1), (fsdp_size, tensor_size, 6 * rows_d)
    )

    def heads_of(grad, shape):
        part = grad.reshape((tensor_size, shape[0], fsdp_size, shape[1]))
        return part.transpose(2, 0, 1, 3).reshape(fsdp_size, tensor_size, -1)

    loss_high = loss_part.astype(BF16).astype(F32)
    losses = jnp.broadcast_to(
        jnp.stack([loss_high, loss_part - loss_high]), (fsdp_size, tensor_size, 2)
    )
    g_small = jnp.concatenate(
        [
            six_grads,
            heads_of(ones[2], b_q.shape),
            heads_of(ones[3], b_v.shape),
            heads_of(g_bup[0], b_up.shape),
            losses,
        ],
        axis=2,
    ).astype(BF16)
    g_small = jnp.pad(g_small, ((0, 0), (0, 0), (0, lines * width - g_small.shape[2])))
    g_all = jnp.concatenate([g_pack, g_small.reshape(fsdp_size, tensor_size, lines, width)], axis=2)
    mine = lax.psum_scatter(g_all, "fsdp", scatter_dimension=0, tiled=False)
    mine = lax.psum_scatter(mine, "tp", scatter_dimension=0, tiled=False).astype(F32)
    g_mat, g_vec = mine[:rows_d], mine[rows_d:].reshape(-1)
    c3, c4 = 3 * cols_h, 4 * cols_h
    six_out = g_vec[: 6 * rows_d].reshape(6, rows_d)
    at = 6 * rows_d
    grad_bq = g_vec[at : at + b_q.size].reshape(b_q.shape)
    at += b_q.size
    grad_bv = g_vec[at : at + b_v.size].reshape(b_v.shape)
    at += b_v.size
    grad_bup = g_vec[at : at + b_up.size].reshape(b_up.shape)
    at += b_up.size
    loss = g_vec[at] + g_vec[at + 1]
    return (
        layer_out,
        loss,
        grad_input,
        six_out[0],
        six_out[1],
        g_mat[:, 0:cols_h],
        g_mat[:, cols_h : 2 * cols_h],
        g_mat[:, 2 * cols_h : c3],
        grad_bq,
        grad_bv,
        g_mat[:, c3:c4].T,
        six_out[2],
        six_out[3],
        six_out[4],
        g_mat[:, c4 : c4 + cols_f],
        grad_bup,
        g_mat[:, c4 + cols_f :].T,
        six_out[5],
    )


def solution(mesh):
    tokens = P(("fsdp", "tp"), None)
    rows, crossed, heads = P("fsdp"), P("fsdp", "tp"), P("tp", "fsdp")
    placed = (
        tokens,
        P("fsdp", None),
        P(("fsdp", "tp")),
        tokens,
        tokens,
        rows,
        rows,
        crossed,
        crossed,
        crossed,
        heads,
        heads,
        heads,
        rows,
        rows,
        rows,
        crossed,
        heads,
        heads,
        rows,
    )
    given = (
        tokens,
        P(),
        tokens,
        rows,
        rows,
        crossed,
        crossed,
        crossed,
        heads,
        heads,
        heads,
        rows,
        rows,
        rows,
        crossed,
        heads,
        heads,
        rows,
    )
    return jax.shard_map(local, mesh=mesh, in_specs=placed, out_specs=given, check_vma=False)
```

time: 957 us -> 345 us (0.36)
  waiting for transfers between devices: 458 us -> 135 us
  blocking collectives: 194 us -> 23 us
  matrix products: 117 us -> 0 us
  Pallas kernels: 0 us -> 76.3 us
  other arithmetic: 63 us -> 11.5 us
  local copies, waits for them, and re-layouts: 86.9 us -> 72.6 us
    reduce_scatter x10 -> x2, waiting for transfers between devices: 298 us -> 66.3 us  [the longest x1 65.6 us: local(): mine = lax.psum_scatter(g_all, 'fsdp', scatter_dimension=0, tiled=False)]
    all_gather x4 -> x1, waiting for transfers between devices: 160 us -> 35.2 us  [local(): every = lax.all_gather(lax.all_gather(shard, 'tp', axis=0), 'fsdp', axis=0)]
    dot_general x58 -> x0, matrix products: 117 us -> none  [the longest x12 16.8 us: block_scores(): jnp.einsum('qhd,khd->hqk', query_block, key_seq, preferred_element_type=j...]
    psum x2 -> x0, blocking collectives: 82.8 us -> none  [the longest x1 42.1 us: local(): valid_total = lax.psum(jnp.sum(mask_float), ('fsdp', 'tp'))]
    pallas_call x0 -> x4, Pallas kernels: none -> 76.3 us  [the longest x1 30.2 us: attention_backward(): pl.pallas_call(functools.partial(backward_kernel, qb), out_shape=shapes,...]
    all_gather x9 -> x1, blocking collectives: 81.9 us -> 23 us  [local(): every = lax.all_gather(lax.all_gather(shard, 'tp', axis=0), 'fsdp', axis=0)]
    ppermute x0 -> x2, waiting for transfers between devices: none -> 33.6 us  [the longest x1 25.3 us: local(): part = lax.ppermute(gn_halo[left - take:left], 'tp', route).astype(F32)]
    unnamed x2 -> x0, blocking collectives: 29.7 us -> none
  transfers between devices with their start and end apart: 14 -> 5, of which waited for: 11 -> 5; matrix products, arithmetic and copies ran while one was open for 13% -> 1% of each run, Pallas kernels for 0% -> 1%
where the time goes in v1:
time: 345 us; the launch traced here: 344 us
  waiting for transfers between devices  135 us (39%)
  Pallas kernels  76.3 us (22%)
  local copies, waits for them, and re-layouts  72.6 us (21%)
  blocking collectives  23 us (7%)
  between operations  22.1 us (6%)
  other arithmetic  11.5 us (3%)
    reduce_scatter x1, waiting for transfers between devices, local(): mine = lax.psum_scatter(g_all, 'fsdp', scatter_dimension=0, tiled=False)  65.6 us
    all_gather x1, waiting for transfers between devices, local(): every = lax.all_gather(lax.all_gather(shard, 'tp', axis=0), 'fsdp', axis=0)  35.2 us
    pallas_call x1, Pallas kernels, attention_backward(): pl.pallas_call(functools.partial(backward_kernel, qb), out_shape=shapes,...  30.2 us
    unnamed x76, local copies, waits for them, and re-layouts  27.7 us
    ppermute x1, waiting for transfers between devices, local(): part = lax.ppermute(gn_halo[left - take:left], 'tp', route).astype(F32)  25.3 us
    all_gather x1, blocking collectives, local(): every = lax.all_gather(lax.all_gather(shard, 'tp', axis=0), 'fsdp', axis=0)  23 us
    pallas_call x1, Pallas kernels, middle(): pl.pallas_call(functools.partial(middle_kernel, rb), out_shape=shapes, in...  22.4 us
    pallas_call x1, Pallas kernels, attention_forward(): pl.pallas_call(functools.partial(forward_kernel, qb), out_shape=shapes, s...  20.7 us
  transfers between devices with their start and end apart: 5, of which 5 were waited for; matrix products, arithmetic and copies ran while one was open for 1% of the time, Pallas kernels for 1%

profile of v1, /device:TPU:0, one launch (start us, length us, event | category | flops | bytes accessed | tf_op | source)
XLA Modules:
  0.0 343.6 jit_solution(4805214136657932766)
XLA Ops:
  7.3 1.4 fusion.7
  14.2 4.1 %concatenate.34 = bf16[482]{0:T(512)(128)(2,1)S(1)} concatenate(bf16[64]{0:T(256)(128)(2,1)} %param.25, bf16[64]{0:T(256)(128)(2,1)} %param.26, bf16[64]{0:T(256)(128)(2,1)} %param.33, bf16[64]{0:T(256)(128)(2,1)} %param.34, bf16[64]{0:T(256)(128)(2,1)} %param.35, bf16[64]{0:T(256)(128)(2,1)} %param.39, bf16[16]{0:T(256)(128)(2,1)S(1)} %reshape.190, bf16[16]{0:T(256)(128)(2,1)S(1)} %reshape.191, ...), dimensions={0} | concatenate | bytes 1928 | tf_op jit(solution)/shard_map/concatenate | solution.py:484
  22.9 23.0 %all-gather.2 = bf16[4,65,1536]{2,1,0:T(8,128)(2,1)} all-gather(bf16[1,65,1536]{2,1,0:T(8,128)(2,1)S(1)} %maximum_bitcast_fusion), channel_id=2, replica_groups=mesh['fsdp'=8,'tp'=4] {'tp'}, dimensions={0}, use_global_device_ids=true | all-gather | bytes 998400 | tf_op jit(solution)/shard_map/all_gather | solution.py:489
  46.0 1.4 collective-permute-start
  48.8 8.3 %collective-permute-done = bf16[512,512]{1,0:T(8,128)(2,1)S(1)} collective-permute-done((bf16[512,512]{1,0:T(8,128)(2,1)S(1)}, bf16[512,512]{1,0:T(8,128)(2,1)S(1)}, u32[]{:S(2)}, u32[]{:S(2)}) %collective-permute-start) | collective-permute-done | bytes 524320 | tf_op jit(solution)/shard_map/ppermute | solution.py:471
  58.9 35.2 %all-gather.5.cloned.1.call-done = bf16[32,65,1536]{2,1,0:T(8,128)(2,1)} async-done(((bf16[4,65,1536]{2,1,0:T(8,128)(2,1)}), bf16[32,65,1536]{2,1,0:T(8,128)(2,1)}) %all-gather.5.cloned.1.call-update) | async-done | bytes 6389776 | tf_op jit(solution)/shard_map/all_gather | solution.py:489
  94.1 1.2 slice.259
  96.4 2.8 fusion.3
  99.2 4.1 %fusion.2 = (bf16[8,4,64,512]{3,2,1,0:T(8,128)(2,1)}, bf16[8,4,64,512]{3,2,1,0:T(8,128)(2,1)S(1)}) fusion(bf16[8,4,65,1536]{3,2,1,0:T(8,128)(2,1)} %bitcast.121), kind=kLoop, calls=%fused_computation.60 | loop fusion | bytes 8388608 | tf_op jit(solution)/shard_map/slice | solution.py:493
  109.0 3.2 copy.107
  112.2 2.0 copy.113
  115.9 1.2 copy.103
  118.4 1.6 copy.106
  120.1 2.0 copy.112
  125.9 20.7 %attention_forward.1 = (bf16[1280,512]{1,0:T(8,128)(2,1)S(1)}, bf16[768,512]{1,0:T(8,128)(2,1)S(1)}, bf16[1280,512]{1,0:T(8,128)(2,1)S(1)}, bf16[1280,512]{1,0:T...) custom-call(bf16[1280,512]{1,0:T(8,128)(2,1)} %constant_dynamic-update-slice_fusion.5.x_ref, ...), custom_call_target="tpu_custom_call" | custom-call | tf_op jit(solution)/shard_map/attention_forward/pallas_call | solution.py:126
  146.6 1.1 copy-done.4
  148.8 1.1 copy-done.6
  152.3 22.4 %middle.1 = (bf16[768,512]{1,0:T(8,128)(2,1)}, f32[768,512]{1,0:T(8,128)}, bf16[768,512]{1,0:T(8,128)(2,1)}, f32[8,768]{1,0:T(8,128)}, bf16[512,512]{1,0:T(8,128...) custom-call(f32[1,1]{1,0:T(1,128)} %bitcast.8.scale_ref, ...), custom_call_target="tpu_custom_call" | custom-call | tf_op jit(solution)/shard_map/middle/pallas_call | solution.py:241
  174.7 30.2 %attention_backward.1 = (bf16[512,512]{1,0:T(8,128)(2,1)}, f32[768,512]{1,0:T(8,128)}, bf16[512,1536]{1,0:T(8,128)(2,1)}, f32[32,512]{1,0:T(8,128)}) custom-call(bf16[768,512]{1,0:T(8,128)(2,1)} %copy-done.7, bf16[1280,512]{1,0:T(8,128)(2,1)} %copy-done.5, bf16[1280,512]{1,0:T(8,128)(2,1)} %copy-done.6, bf16[768,512]{1,0:T(8,128)(2,1)} %get-tuple-element.42.go_ref, ...), custom_call_target="tpu_custom_call" | custom-call | tf_op jit(solution)/shard_map/attention_backward/pallas_call | solution.py:393
  206.6 2.3 fusion.4
  212.9 2.0 reshape.209
  215.8 1.2 reshape.211
  217.0 2.8 reshape.212
  219.8 3.5 %reshape.213 = bf16[8,64,4,512]{3,2,1,0:T(4,128)(2,1)S(1)} reshape(bf16[512,2048]{1,0:T(8,128)(2,1)} %get-tuple-element.49) | data formatting | bytes 4194304 | tf_op jit(solution)/shard_map/reshape | solution.py:539
  223.3 1.3 bitcast_dynamic-update-slice_fusion.8
  224.6 1.3 bitcast_dynamic-update-slice_fusion.7
  227.4 3.8 %pad_maximum_fusion = bf16[8,4,65,1536]{3,2,1,0:T(8,128)(2,1)} fusion(bf16[8,4,1,1536]{3,2,1,0:T(2,128)(2,1)S(1)} %copy.100, bf16[8,4,64,1536]{3,2,1,0:T(8,128)(2,1)S(1)} %bitcast_dynamic-update-slice_fusion), kind=kLoop, calls=%fused_computation | loop fusion | flops 12779520 | bytes 12779520 | tf_op jit(solution)/shard_map/concatenate | solution.py:574
  231.2 65.6 %reduce-scatter.3.cloned.1.call-done = bf16[1,4,65,1536]{3,2,1,0:T(8,128)(2,1)} async-done(((bf16[8,4,65,1536]{3,2,1,0:T(8,128)(2,1)}), bf16[1,4,65,1536]{3,2,1,0:T(8,128)(2,1)}) %reduce-scatter.3.cloned.1.call-update) | async-done | bytes 798736 | tf_op jit(solution)/shard_map/reduce_scatter | solution.py:575
  296.9 1.4 collective-permute-start.1
  298.3 25.3 %collective-permute-done.1 = bf16[512,512]{1,0:T(8,128)(2,1)S(1)} collective-permute-done((bf16[512,512]{1,0:T(8,128)(2,1)S(1)}, bf16[512,512]{1,0:T(8,128)(2,1)S(1)}, u32[]{:S(2)}, u32[]{:S(2)}) %collective-permute-start.1) | collective-permute-done | bytes 524320 | tf_op jit(solution)/shard_map/ppermute | solution.py:533
  323.6 1.6 convert_add_fusion.gn_ref
  325.3 3.0 finish.1
  (156 shorter events, 39.4 us)
Async XLA Ops:
  7.2 38.8 %copy-start = (bf16[768,512]{1,0:T(8,128)(2,1)S(1)}, bf16[768,512]{1,0:T(8,128)(2,1)}, u32[]{:S(2)}) copy-start(bf16[768,512]{1,0:T(8,128)(2,1)} %x_ref.3) | copy-start | bytes 2359300
  7.2 40.2 %copy-start.18 = (s32[3,1024]{1,0:T(4,128)S(1)}, s32[3,1024]{1,0:T(4,128)}, u32[]{:S(2)}) copy-start(s32[3,1024]{1,0:T(4,128)} %param.21) | copy-start | bytes 36868
  7.2 86.9 %all-gather.5.cloned.1.call-start = ((), (), s32[]{:S(2)}) async-start(), calls=%async_computation.4 | async-start | bytes 7962624 | tf_op jit(solution)/shard_map/all_gather | solution.py:489
  45.9 250.9 %reduce-scatter.3.cloned.1.call-start = ((), (), s32[]{:S(2)}) async-start(), calls=%async_computation.2 | async-start | bytes 7962624 | tf_op jit(solution)/shard_map/reduce_scatter | solution.py:575
  46.0 11.1 %collective-permute-start = (bf16[512,512]{1,0:T(8,128)(2,1)S(1)}, bf16[512,512]{1,0:T(8,128)(2,1)S(1)}, u32[]{:S(2)}, u32[]{:S(2)}) collective-permute-start(bf16[512,512]{1,0:T(8,128)(2,1)S(1)} %slice.208), channel_id=1, source_target_pairs={{0,1},{1,2},{2,3},{4,5},{5,6},{6,7},{8,9},{9,10},{10,11},{12,13},{... | collective-permute-start | bytes 1572872 | tf_op jit(solution)/shard_map/ppermute | solution.py:471
  47.6 78.3 %copy-start.9 = (s32[1,1280]{1,0:T(1,128)}, s32[1,1280]{1,0:T(1,128)S(1)}, u32[]{:S(2)}) copy-start(s32[1,1280]{1,0:T(1,128)S(1)} %broadcast_in_dim.21.idr_ref) | copy-start | bytes 15364
  47.8 78.1 %copy-start.2 = (s32[1280,1]{1,0:T(8,128)}, s32[1280,1]{1,0:T(8,128)S(1)}, u32[]{:S(2)}) copy-start(s32[1280,1]{1,0:T(8,128)S(1)} %broadcast_in_dim.27.idc_ref) | copy-start | bytes 15364
  114.2 1.3 copy-start.16
  114.2 1.7 copy-start.15
  114.2 2.9 copy-start.14
  120.1 3.4 %copy-start.13 = (bf16[8,4,64,128]{3,1,2,0:T(4,128)(2,1)S(1)}, bf16[8,4,64,128]{3,1,2,0:T(4,128)(2,1)}, u32[]{:S(2)}) copy-start(bf16[8,4,64,128]{3,1,2,0:T(4,128)(2,1)} %copy.103) | copy-start | bytes 1572868
  122.1 3.2 copy-start.19
  122.1 3.2 copy-start.21
  122.1 3.2 copy-start.25
  122.1 3.2 copy-start.20
  122.1 3.2 copy-start.22
  122.1 3.2 copy-start.23
  122.1 3.2 copy-start.24
  146.6 1.1 copy-start.4
  147.7 1.1 copy-start.5
  148.8 1.1 copy-start.6
  149.9 0.9 copy-start.7
  150.8 0.9 copy-start.8
  151.7 0.6 copy-start.10
  206.6 3.5 %copy-start.17 = (f32[40,512]{1,0:T(8,128)S(1)}, f32[40,512]{1,0:T(8,128)}, u32[]{:S(2)}) copy-start(f32[40,512]{1,0:T(8,128)} %get-tuple-element.51) | copy-start | bytes 245764
  211.8 5.2 %copy-start.12 = (bf16[512,2048]{1,0:T(8,128)(2,1)S(1)}, bf16[512,2048]{1,0:T(8,128)(2,1)}, u32[]{:S(2)}) copy-start(bf16[512,2048]{1,0:T(8,128)(2,1)} %get-tuple-element.48) | copy-start | bytes 6291460
  223.3 3.0 copy-start.11
  231.1 65.7 %copy-start.26 = (bf16[512,512]{1,0:T(8,128)(2,1)S(1)}, bf16[512,512]{1,0:T(8,128)(2,1)}, u32[]{:S(2)}) copy-start(bf16[512,512]{1,0:T(8,128)(2,1)} %get-tuple-element.54) | copy-start | bytes 1572868
  231.2 97.8 %reduce-scatter.5.cloned.1.call-start = ((), (), s32[]{:S(2)}) async-start(), calls=%async_computation.3 | async-start | bytes 1105920 | tf_op jit(solution)/shard_map/reduce_scatter | solution.py:576
  296.8 28.4 %copy-start.1 = (bf16[768,512]{1,0:T(8,128)(2,1)S(1)}, bf16[768,512]{1,0:T(8,128)(2,1)}, u32[]{:S(2)}) copy-start(bf16[768,512]{1,0:T(8,128)(2,1)} %x_ref.3) | copy-start | bytes 2359300
  296.8 28.5 %copy-start.3 = (f32[768,512]{1,0:T(8,128)S(1)}, f32[768,512]{1,0:T(8,128)}, u32[]{:S(2)}) copy-start(f32[768,512]{1,0:T(8,128)} %get-tuple-element.55.gh_ref) | copy-start | bytes 4718596
  296.9 26.8 %collective-permute-start.1 = (bf16[512,512]{1,0:T(8,128)(2,1)S(1)}, bf16[512,512]{1,0:T(8,128)(2,1)S(1)}, u32[]{:S(2)}, u32[]{:S(2)}) collective-permute-start(bf16[512,512]{1,0:T(8,128)(2,1)S(1)} %copy-done.26), channel_id=1, source_target_pairs={{1,0},{2,1},{3,2},{5,4},{6,5},{7,6},{9,8},{10,9},{11,10},{13,12},{... | collective-permute-start | bytes 1572872 | tf_op jit(solution)/shard_map/ppermute | solution.py:533
Sparse Core Ops, SparseCore 0:
  46.0 48.0 all-gather.4
  231.3 65.5 reduce-scatter.2
  299.3 29.6 reduce-scatter.4

commit v2 on v1

--- a/solution.py
+++ b/solution.py
@@ -607,6 +607,791 @@
     )
 
 
+ROWS = D // 8
+EXTRA = 8
+COLS = D // 4
+FFC = 512
+WA = 3 * COLS
+WF = COLS + 2 * FFC
+MASKS_A = (0, 2, 4, 6, 1, 3, 5, 7)
+SMALL = pl.CostEstimate(flops=1, bytes_accessed=1, transcendentals=0)
+ANY = pl.BlockSpec(memory_space=pl.ANY)
+VMEM = pl.BlockSpec(memory_space=pltpu.VMEM)
+
+
+def params(mib):
+    return pltpu.CompilerParams(vmem_limit_bytes=mib * MIB)
+
+
+def lane_of(shape):
+    return lax.broadcasted_iota(jnp.int32, shape, len(shape) - 1)
+
+
+def pack_kernel(
+    wq_ref, wk_ref, wv_ref, wo_ref, wup_ref, wdn_ref, g1, b1, bo, g2, b2, bd, bq, bv, bup, mask_ref, a_ref, f_ref
+):
+    me = lax.axis_index("fsdp")
+    a_ref[0:ROWS, 0:COLS] = wq_ref[...]
+    a_ref[0:ROWS, COLS : 2 * COLS] = wk_ref[...]
+    a_ref[0:ROWS, 2 * COLS : 3 * COLS] = wv_ref[...]
+    f_ref[:, 0:COLS] = wo_ref[...]
+    f_ref[:, COLS : COLS + FFC] = wup_ref[...]
+    f_ref[:, COLS + FFC :] = wdn_ref[...]
+    count = jnp.sum(mask_ref[...].astype(F32)).reshape(1, 1)
+    high = jnp.floor(count / 256.0)
+    lane = lane_of((1, 128))
+    digits = jnp.where(lane == 0, high, jnp.where(lane == 1, count - 256.0 * high, 0.0))
+    vectors = [r[...].astype(F32).reshape(1, ROWS) for r in (g1, b1, bo, g2, b2, bd)]
+    rows = [jnp.concatenate([v, v], axis=1) for v in vectors] + [digits, jnp.zeros((1, 128), F32)]
+    a_ref[ROWS:, 0:128] = jnp.concatenate(rows, axis=0).astype(BF16)
+
+    def spread(ref):
+        block = ref[...].astype(F32)
+        count, piece = block.shape
+        lanes = count * HD
+        lane = lane_of((1, lanes))
+        row = jnp.zeros((1, lanes), F32)
+        for i in range(count):
+            for j in range(piece):
+                at = i * HD + me * piece + j
+                row = jnp.where(lane == at, block[i : i + 1, j : j + 1], row)
+        return row
+
+    ups = spread(bup)
+    rows = [spread(bq), spread(bv)] + [ups[:, 128 * j : 128 * j + 128] for j in range(4)]
+    rows.append(jnp.zeros((2, 128), F32))
+    a_ref[ROWS:, 128:256] = jnp.concatenate(rows, axis=0).astype(BF16)
+    a_ref[ROWS:, 256:384] = jnp.zeros((EXTRA, 128), BF16)
+
+
+def pack_weights(args):
+    return pl.pallas_call(
+        pack_kernel,
+        out_shape=(
+            jax.ShapeDtypeStruct((ROWS + EXTRA, WA), BF16),
+            jax.ShapeDtypeStruct((ROWS, WF), BF16),
+        ),
+        compiler_params=params(60),
+        name="pack_weights",
+    )(*args)
+
+
+def project_kernel(
+    tokens_all, x_ref, halo_ref, p0, p1, p2, p3, p4, p5, p6, p7,
+    q_ref, k_ref, v_ref, kt_ref, nt_ref, w_ref, vec_ref, bup_ref, scale_ref, ext_ref, head_ref, sem
+):
+    me, place = lax.axis_index("fsdp"), lax.axis_index("tp")
+    pieces = (p0, p1, p2, p3, p4, p5, p6, p7)
+
+    def each(act):
+        for j, (ref, mask) in enumerate(zip(pieces, MASKS_A)):
+            owner = lax.bitwise_xor(me, mask)
+            for s in range(4):
+                tp = lax.bitwise_and(place - s + 4, 3)
+                act(j, ref, owner, s, tp)
+
+    def start_ext(j, ref, owner, s, tp):
+        pltpu.make_async_copy(ref.at[s, pl.ds(ROWS, EXTRA), :], ext_ref.at[4 * j + s], sem.at[0]).start()
+
+    def start_w(j, ref, owner, s, tp):
+        pltpu.make_async_copy(
+            ref.at[s, pl.ds(0, ROWS), :],
+            w_ref.at[rows_of(owner * ROWS, ROWS, ROWS), rows_of(tp * WA, WA)],
+            sem.at[1],
+        ).start()
+
+    each(start_ext)
+    each(start_w)
+    pltpu.make_async_copy(ext_ref, ext_ref, sem.at[0]).wait()
+    lane = lane_of((EXTRA, D))
+    vectors = jnp.zeros((EXTRA, D), F32)
+    total = jnp.zeros((EXTRA, 128), F32)
+    for j, mask in enumerate(MASKS_A):
+        block = ext_ref[4 * j, :, 0:128].astype(F32)
+        wide = jnp.concatenate([block] * 4, axis=1)
+        vectors = jnp.where(lane // ROWS == lax.bitwise_xor(me, mask), wide, vectors)
+        for s in range(4):
+            total += ext_ref[4 * j + s, :, 0:128].astype(F32)
+    vec_ref[...] = vectors
+    valid = 256.0 * total[6:7, 0:1] + total[6:7, 1:2]
+    scale_ref[...] = jnp.concatenate(
+        [jnp.broadcast_to(tokens_all / valid, (4, 128)), jnp.broadcast_to(0.5 / D / valid, (4, 128))], axis=0
+    )
+    for s in range(4):
+        tp = lax.bitwise_and(place - s + 4, 3)
+        block = jnp.zeros((EXTRA, 128), F32)
+        for j in range(8):
+            block += ext_ref[4 * j + s, :, 128:256].astype(F32)
+        head_ref[:, rows_of(tp * COLS, COLS)] = block
+        for i in range(4):
+            bup_ref[:, rows_of(tp * FFC + 128 * i, 128)] = jnp.broadcast_to(block[2 + i : 3 + i], (8, 128))
+    pltpu.make_async_copy(w_ref, w_ref, sem.at[1]).wait()
+    gain, offset = vectors[0:1], vectors[1:2]
+
+    def rows_done(x, at):
+        xhat, _ = normalize(x.astype(F32))
+        n1 = xhat * gain + offset
+        turned = jnp.transpose(n1).astype(BF16)
+        for i in range(8):
+            slot = lax.bitwise_xor(me, i)
+            nt_ref[rows_of(slot * ROWS, ROWS, ROWS), rows_of(at, 128)] = turned[ROWS * i : ROWS * (i + 1)]
+        made = dot(n1.astype(BF16), w_ref[...])
+        for t in range(4):
+            lanes = slice(t * COLS, (t + 1) * COLS)
+            k = made[:, t * WA + COLS : t * WA + 2 * COLS]
+            k_ref[rows_of(at, 128), lanes] = k.astype(BF16)
+            kt_ref[lanes, rows_of(at, 128)] = jnp.transpose(k).astype(BF16)
+            v = made[:, t * WA + 2 * COLS : (t + 1) * WA] + head_ref[1:2, lanes]
+            v_ref[rows_of(at, 128), lanes] = v.astype(BF16)
+        return made
+
+    def halo_rows(i, carry):
+        rows_done(halo_ref[rows_of(i * 128, 128), :], i * 128)
+        return carry
+
+    lax.fori_loop(0, HALO // 128, halo_rows, 0)
+
+    def own_rows(i, carry):
+        rows = rows_of(i * 128, 128)
+        made = rows_done(x_ref[rows, :], HALO + i * 128)
+        for t in range(4):
+            lanes = slice(t * COLS, (t + 1) * COLS)
+            q = (made[:, t * WA : t * WA + COLS] + head_ref[0:1, lanes]).astype(BF16)
+            q_ref[rows, lanes] = q * jnp.asarray(SCALE, BF16)
+        return carry
+
+    lax.fori_loop(0, x_ref.shape[0] // 128, own_rows, 0)
+
+
+def project(x, halo, pieces, tokens_all):
+    own = x.shape[0]
+    ext = HALO + own
+    shapes = (
+        jax.ShapeDtypeStruct((own, D), BF16),
+        jax.ShapeDtypeStruct((ext, D), BF16),
+        jax.ShapeDtypeStruct((ext, D), BF16),
+        jax.ShapeDtypeStruct((D, ext), BF16),
+        jax.ShapeDtypeStruct((D, ext), BF16),
+        jax.ShapeDtypeStruct((D, 4 * WA), BF16),
+        jax.ShapeDtypeStruct((EXTRA, D), F32),
+        jax.ShapeDtypeStruct((8, 4 * FFC), F32),
+        jax.ShapeDtypeStruct((8, 128), F32),
+    )
+    return pl.pallas_call(
+        functools.partial(project_kernel, float(tokens_all)),
+        out_shape=shapes,
+        in_specs=[VMEM, VMEM] + [ANY] * 8,
+        out_specs=[VMEM] * len(shapes),
+        scratch_shapes=[
+            pltpu.VMEM((32, EXTRA, WA), BF16),
+            pltpu.VMEM((EXTRA, D), F32),
+            pltpu.SemaphoreType.DMA((2,)),
+        ],
+        compiler_params=params(20),
+        cost_estimate=SMALL,
+        name="project",
+    )(x, halo, *pieces)
+
+
+def attend_kernel(q_ref, k_ref, v_ref, idr_ref, idc_ref, o_ref, lse_ref, bias_ref, stat_ref):
+    own = o_ref.shape[0]
+    qb, window = bias_ref.shape[1:]
+
+    @pl.when(pl.program_id(0) == 0)
+    def _():
+        stat_ref[...] = jnp.zeros_like(stat_ref)
+
+        def mask(i, carry):
+            first = i * qb
+            key = lax.broadcasted_iota(jnp.int32, (qb, window), 1)
+            query = lax.broadcasted_iota(jnp.int32, (qb, window), 0)
+            same = idc_ref[rows_of(HALO + first, qb), :] == idr_ref[:, rows_of(first, window)]
+            bias_ref[i] = jnp.where(same & (key <= query + HALO), 0.0, NEG)
+            return carry
+
+        lax.fori_loop(0, own // qb, mask, 0)
+
+    def query_block(i, carry):
+        first = i * qb
+        lane = lane_of((qb, PAIR))
+        keys, values = k_ref[rows_of(first, window), :], v_ref[rows_of(first, window), :]
+        both = q_ref[rows_of(first, qb), :]
+        got = None
+        for h in range(2):
+            mine = (lane < HD) if h == 0 else (lane >= HD)
+            s = dot_t(jnp.where(mine, both, jnp.zeros_like(both)), keys) + bias_ref[i]
+            top = jnp.max(s, axis=-1, keepdims=True)
+            p = jnp.exp(s - top)
+            total = jnp.sum(p, axis=-1, keepdims=True)
+            o = dot(p.astype(BF16), values) / total
+            got = o if h == 0 else jnp.where(mine, o, got)
+            stat_ref[:, h : h + 1] = top + jnp.log(total)
+        o_ref[rows_of(first, qb), :] = got.astype(BF16)
+        lse_ref[0, :, rows_of(first, qb)] = jnp.transpose(stat_ref[...])[0:8, :]
+        return carry
+
+    lax.fori_loop(0, own // qb, query_block, 0)
+
+
+def attend(q, k, v, id_row, id_col, first_pair, pairs):
+    own, ext = q.shape[0], k.shape[0]
+    qb = 256
+    at = lambda i: (0, first_pair + i)
+    flat = lambda i: (0, 0)
+    return pl.pallas_call(
+        attend_kernel,
+        grid=(pairs,),
+        out_shape=(
+            jax.ShapeDtypeStruct((own, pairs * PAIR), BF16),
+            jax.ShapeDtypeStruct((pairs, 8, own), F32),
+        ),
+        in_specs=[
+            pl.BlockSpec((own, PAIR), at),
+            pl.BlockSpec((ext, PAIR), at),
+            pl.BlockSpec((ext, PAIR), at),
+            pl.BlockSpec((1, ext), flat),
+            pl.BlockSpec((ext, 1), flat),
+        ],
+        out_specs=[pl.BlockSpec((own, PAIR), lambda i: (0, i)), pl.BlockSpec((1, 8, own), lambda i: (i, 0, 0))],
+        scratch_shapes=[pltpu.VMEM((own // qb, qb, HALO + qb), F32), pltpu.VMEM((qb, 128), F32)],
+        compiler_params=params(14),
+        cost_estimate=SMALL,
+        name="attend",
+    )(q, k, v, id_row, id_col)
+
+
+PIECES_F = ((0, (0, 1, 2, 3)), (2, (0, 1, 2, 3)), (4, (0, 1, 2, 3)), (6, (0, 1)), (6, (2, 3)))
+
+
+def central_kernel(
+    rb, x_ref, oa_ref, ob_ref, teacher_ref, cot_ref, mask_ref, vec_ref, bup_ref, scale_ref,
+    p0, p1, p2, p3, p4, p5, p6, p7, p8, p9,
+    out_ref, gh_ref, go_ref, delta_ref, theirs_ref, mine_ref, small_ref, gbup_ref,
+    wo_ref, wup_ref, wdn_ref, o_ref, slope_ref, hid_ref, gpre_ref, n2t_ref, gmlpt_ref, gattnt_ref, sem
+):
+    me, place = lax.axis_index("fsdp"), lax.axis_index("tp")
+    own, ff = x_ref.shape[0], 4 * FFC
+    pieces = (p0, p1, p2, p3, p4, p5, p6, p7, p8, p9)
+    parts = ((wo_ref, 0, COLS), (wup_ref, COLS, FFC), (wdn_ref, COLS + FFC, FFC))
+    for n, (dst, start, size) in enumerate(parts):
+        for j, ref in enumerate(pieces):
+            mask, steps = PIECES_F[j % 5]
+            owner = lax.bitwise_xor(me, mask + j // 5)
+            for i, s in enumerate(steps):
+                tp = lax.bitwise_and(place - s + 4, 3)
+                pltpu.make_async_copy(
+                    ref.at[i, :, pl.ds(start, size)],
+                    dst.at[rows_of(owner * ROWS, ROWS, ROWS), rows_of(tp * size, size)],
+                    sem.at[n],
+                ).start()
+    small_ref[...] = jnp.zeros_like(small_ref)
+    o_ref[:, 0 : D // 2] = oa_ref[...]
+    o_ref[:, D // 2 :] = ob_ref[...]
+    head_of = lax.broadcasted_iota(jnp.int32, (D, 128), 0) // HD
+    pick = (head_of == lax.broadcasted_iota(jnp.int32, (D, 128), 1)).astype(BF16)
+    out_bias, gain, offset, down_bias = (vec_ref[j : j + 1, :] for j in range(2, 6))
+
+    def turn(dst, rows, value):
+        turned = jnp.transpose(value).astype(BF16)
+        for i in range(8):
+            slot = lax.bitwise_xor(me, i)
+            dst[rows_of(slot * ROWS, ROWS, ROWS), rows] = turned[ROWS * i : ROWS * (i + 1)]
+
+    for n, (dst, _, _) in enumerate(parts):
+        pltpu.make_async_copy(dst, dst, sem.at[n]).wait()
+
+    def block(i, carry):
+        rows = rows_of(i * rb, rb)
+        h1 = x_ref[rows, :].astype(F32) + dot_t(o_ref[rows, :], wo_ref[...]) + out_bias
+        xhat, rstd = normalize(h1)
+        n2 = xhat * gain + offset
+        n2_low = n2.astype(BF16)
+        turn(n2t_ref, rows, n2)
+        for c in range(0, ff, FFC):
+            pre = dot(n2_low, wup_ref[:, c : c + FFC]) + bup_ref[0:1, c : c + FFC]
+            s = jax.nn.sigmoid(1.702 * pre)
+            value = pre * s
+            hid_ref[rows, c : c + FFC] = value.astype(BF16)
+            slope_ref[:, c : c + FFC] = s + 1.702 * value * (1.0 - s)
+        out = h1 + dot_t(hid_ref[rows, :], wdn_ref[...]) + down_bias
+        out_ref[rows, :] = out.astype(BF16)
+        diff = (out - teacher_ref[rows, :].astype(F32)) * mask_ref[rows, :]
+        g_out = cot_ref[rows, :].astype(F32) + scale_ref[0:1, 0:1] * diff
+        small_ref[0:8, :] += fold(g_out)
+        small_ref[8:16, :] += fold(diff * diff)
+        g_mlp = g_out.astype(BF16)
+        turn(gmlpt_ref, rows, g_out)
+        for c in range(0, ff, FFC):
+            g_hid = dot(g_mlp, wdn_ref[:, c : c + FFC])
+            gpre_ref[rows, c : c + FFC] = (g_hid * slope_ref[:, c : c + FFC]).astype(BF16)
+        g_n2 = dot_t(gpre_ref[rows, :], wup_ref[...])
+        small_ref[16:24, :] += fold(g_n2 * xhat)
+        small_ref[24:32, :] += fold(g_n2)
+        g_h1 = g_out + norm_pull(g_n2, gain, xhat, rstd)
+        gh_ref[rows, :] = g_h1
+        small_ref[32:40, :] += fold(g_h1)
+        turn(gattnt_ref, rows, g_h1)
+        g_o = dot(g_h1.astype(BF16), wo_ref[...]).astype(BF16)
+        go_ref[rows, :] = g_o
+        product = g_o.astype(F32) * o_ref[rows, :].astype(F32)
+        high = product.astype(BF16)
+        low = (product - high.astype(F32)).astype(BF16)
+        turned = jnp.transpose(dot(high, pick) + dot(low, pick))
+        for g in range(4):
+            delta_ref[g, 0:2, rows] = turned[2 * g : 2 * g + 2, :]
+        return carry
+
+    lax.fori_loop(0, own // rb, block, 0)
+    ones = jnp.ones((8, own), BF16)
+
+    def keep(grad, s, start, size):
+        low = grad.astype(BF16)
+        for r in range(8):
+            dst = theirs_ref if r % 2 else mine_ref
+            dst[r // 2, s, :, start : start + size] = low[ROWS * r : ROWS * (r + 1)]
+
+    def grads(s, carry):
+        tp = lax.bitwise_and(place + s, 3)
+        cols = rows_of(tp * FFC, FFC)
+        keep(dot(gattnt_ref[...], o_ref[:, rows_of(tp * COLS, COLS)]), s, 0, COLS)
+        keep(dot(n2t_ref[...], gpre_ref[:, cols]), s, COLS, FFC)
+        keep(dot(gmlpt_ref[...], hid_ref[:, cols]), s, COLS + FFC, FFC)
+        gbup_ref[:, cols] = dot(ones, gpre_ref[:, cols])
+        return carry
+
+    lax.fori_loop(0, 4, grads, 0)
+
+
+def central(x, o_a, o_b, teacher, cot, mask, vec, bup, scale, pieces):
+    own = x.shape[0]
+    rb = 256
+    shapes = (
+        jax.ShapeDtypeStruct((own, D), BF16),
+        jax.ShapeDtypeStruct((own, D), F32),
+        jax.ShapeDtypeStruct((own, D), BF16),
+        jax.ShapeDtypeStruct((4, 8, own), F32),
+        jax.ShapeDtypeStruct((4, 4, ROWS, WF), BF16),
+        jax.ShapeDtypeStruct((4, 4, ROWS, WF), BF16),
+        jax.ShapeDtypeStruct((40, D), F32),
+        jax.ShapeDtypeStruct((8, 4 * FFC), F32),
+    )
+    return pl.pallas_call(
+        functools.partial(central_kernel, rb),
+        out_shape=shapes,
+        in_specs=[VMEM] * 9 + [ANY] * 10,
+        out_specs=[VMEM] * len(shapes),
+        scratch_shapes=[
+            pltpu.VMEM((D, D), BF16),
+            pltpu.VMEM((D, 4 * FFC), BF16),
+            pltpu.VMEM((D, 4 * FFC), BF16),
+            pltpu.VMEM((own, D), BF16),
+            pltpu.VMEM((rb, 4 * FFC), F32),
+            pltpu.VMEM((own, 4 * FFC), BF16),
+            pltpu.VMEM((own, 4 * FFC), BF16),
+            pltpu.VMEM((D, own), BF16),
+            pltpu.VMEM((D, own), BF16),
+            pltpu.VMEM((D, own), BF16),
+            pltpu.SemaphoreType.DMA((3,)),
+        ],
+        compiler_params=params(36),
+        cost_estimate=SMALL,
+        name="central",
+    )(x, o_a, o_b, teacher, cot, mask, vec, bup, scale, *pieces)
+
+
+def pair_core(q_ref, k_ref, v_ref, go_ref, lse_ref, delta_ref, idr_ref, idc_ref, kt_ref, nt_ref,
+              g_ref, theirs_ref, mine_ref, bias_ref, dqt_ref, dk_ref, dv_ref):
+    ext, own = k_ref.shape[0], q_ref.shape[0]
+    window, qb = bias_ref.shape
+    dk_ref[...] = jnp.zeros_like(dk_ref)
+    dv_ref[...] = jnp.zeros_like(dv_ref)
+
+    def query_block(i, carry):
+        first = i * qb
+        key = lax.broadcasted_iota(jnp.int32, (window, qb), 0)
+        query = lax.broadcasted_iota(jnp.int32, (window, qb), 1)
+        same = idc_ref[rows_of(first, window), :] == idr_ref[:, rows_of(HALO + first, qb)]
+        bias_ref[...] = jnp.where(same & (key <= query + HALO), 0.0, NEG)
+        lane = lane_of((qb, PAIR))
+        keys, values = k_ref[rows_of(first, window), :], v_ref[rows_of(first, window), :]
+        both_q, both_g = q_ref[rows_of(first, qb), :], go_ref[rows_of(first, qb), :]
+        all_lse, all_delta = lse_ref[0, :, rows_of(first, qb)], delta_ref[0, :, rows_of(first, qb)]
+        for h in range(2):
+            mine = (lane < HD) if h == 0 else (lane >= HD)
+            q = jnp.where(mine, both_q, jnp.zeros_like(both_q))
+            g_o = jnp.where(mine, both_g, jnp.zeros_like(both_g))
+            p = jnp.exp(dot_t(keys, q) + bias_ref[...] - all_lse[h : h + 1])
+            ds = (p * (dot_t(values, g_o) - all_delta[h : h + 1])).astype(BF16)
+            dv_ref[rows_of(first, window), :] += dot(p.astype(BF16), g_o)
+            dk_ref[rows_of(first, window), :] += dot(ds, q)
+            dqt_ref[h * HD : (h + 1) * HD, rows_of(first, qb)] = dot(
+                kt_ref[h * HD : (h + 1) * HD, rows_of(first, window)], ds
+            )
+        return carry
+
+    lax.fori_loop(0, own // qb, query_block, 0)
+    g_ref[0:HALO, 0:COLS] = jnp.zeros((HALO, COLS), BF16)
+
+    def gather(i, carry):
+        rows = rows_of(i * 128, 128)
+        g_ref[rows, COLS : 2 * COLS] = dk_ref[rows, :].astype(BF16)
+        g_ref[rows, 2 * COLS :] = dv_ref[rows, :].astype(BF16)
+        return carry
+
+    lax.fori_loop(0, ext // 128, gather, 0)
+
+    def gather_q(i, carry):
+        cols = rows_of(i * 128, 128)
+        g_ref[rows_of(HALO + i * 128, 128), 0:COLS] = (jnp.transpose(dqt_ref[:, cols]) * SCALE).astype(BF16)
+        return carry
+
+    lax.fori_loop(0, own // 128, gather_q, 0)
+    low = dot(nt_ref[...], g_ref[...]).astype(BF16)
+    for r in range(8):
+        dst = theirs_ref if r % 2 else mine_ref
+        dst[r // 2, 0, 0:ROWS, :] = low[ROWS * r : ROWS * (r + 1)]
+
+
+def pair_kernel(sc_ref, q_ref, k_ref, v_ref, go_ref, lse_ref, delta_ref, idr_ref, idc_ref, kt_ref, nt_ref, *rest):
+    g_ref, theirs_ref, mine_ref, *scratch = rest[-7:]
+    pair_core(q_ref, k_ref, v_ref, go_ref, lse_ref, delta_ref, idr_ref, idc_ref, kt_ref, nt_ref,
+              g_ref, theirs_ref, mine_ref, *scratch)
+
+
+def pair_backward(step, where, q, k, v, g_o, lse, delta, id_row, id_col, kt, nt, before):
+    own, ext = q.shape[0], k.shape[0]
+    qb = 256
+
+    def at(i, sc):
+        return (0, lax.bitwise_and(sc[0] + step, 3))
+
+    def deep(i, sc):
+        return (lax.bitwise_and(sc[0] + step, 3), 0, 0)
+
+    def down(i, sc):
+        return (lax.bitwise_and(sc[0] + step, 3), 0)
+
+    flat = lambda i, sc: (0, 0)
+    send = jax.ShapeDtypeStruct((4, 4, ROWS + EXTRA, WA), BF16)
+    block = pl.BlockSpec((4, 1, ROWS + EXTRA, WA), lambda i, sc: (0, step, 0, 0))
+    return pl.pallas_call(
+        pair_kernel,
+        grid_spec=pltpu.PrefetchScalarGridSpec(
+            num_scalar_prefetch=1,
+            grid=(1,),
+            in_specs=[
+                pl.BlockSpec((own, PAIR), at),
+                pl.BlockSpec((ext, PAIR), at),
+                pl.BlockSpec((ext, PAIR), at),
+                pl.BlockSpec((own, PAIR), at),
+                pl.BlockSpec((1, 8, own), deep),
+                pl.BlockSpec((1, 8, own), deep),
+                pl.BlockSpec((1, ext), flat),
+                pl.BlockSpec((ext, 1), flat),
+                pl.BlockSpec((PAIR, ext), down),
+                pl.BlockSpec((D, ext), flat),
+            ]
+            + [ANY] * len(before),
+            out_specs=[pl.BlockSpec((ext, WA), flat), block, block],
+            scratch_shapes=[
+                pltpu.VMEM((HALO + qb, qb), F32),
+                pltpu.VMEM((PAIR, own), F32),
+                pltpu.VMEM((ext, PAIR), F32),
+                pltpu.VMEM((ext, PAIR), F32),
+            ],
+        ),
+        out_shape=(jax.ShapeDtypeStruct((ext, WA), BF16), send, send),
+        input_output_aliases={11: 1, 12: 2} if before else {},
+        compiler_params=params(14),
+        cost_estimate=SMALL,
+        name="pair_backward",
+    )(where, q, k, v, g_o, lse, delta, id_row, id_col, kt, nt, *before)
+
+
+def pull_kernel(x_ref, halo_ref, g0, g1, g2, g3, w_ref, small_in, gbup_ref, scale_ref, theirs_in, mine_in,
+                gn_halo_ref, gn_ref, theirs_ref, mine_ref, small_ref, bias_ref):
+    me, place = lax.axis_index("fsdp"), lax.axis_index("tp")
+    own, ext = x_ref.shape[0], g0.shape[0]
+    grads = (g0, g1, g2, g3)
+    small_ref[...] = jnp.zeros_like(small_ref)
+
+    def pull(at, skip):
+        total = None
+        for s, ref in enumerate(grads):
+            tp = lax.bitwise_and(place + s, 3)
+            part = dot_t(
+                ref[rows_of(at, 128), skip:], w_ref[:, rows_of(tp * WA + skip, WA - skip)]
+            )
+            total = part if total is None else total + part
+        return total
+
+    def norms(x, g_n1):
+        xhat, _ = normalize(x.astype(F32))
+        small_ref[0:8, :] += fold(g_n1 * xhat)
+        small_ref[8:16, :] += fold(g_n1)
+
+    def pull_halo(i, carry):
+        rows = rows_of(i * 128, 128)
+        g_n1 = pull(i * 128, COLS)
+        gn_halo_ref[rows, :] = g_n1.astype(BF16)
+        norms(halo_ref[rows, :], g_n1)
+        return carry
+
+    lax.fori_loop(0, HALO // 128, pull_halo, 0)
+
+    def pull_own(i, carry):
+        rows = rows_of(i * 128, 128)
+        g_n1 = pull(HALO + i * 128, 0)
+        gn_ref[rows, :] = g_n1
+        norms(x_ref[rows, :], g_n1)
+        return carry
+
+    lax.fori_loop(0, own // 128, pull_own, 0)
+
+    ones = jnp.ones((8, ext), BF16)
+    for s, ref in enumerate(grads):
+        bias_ref[s] = dot(ones, ref[...])[0:1]
+    sums = lambda ref, j: jnp.sum(ref[8 * j : 8 * j + 8, :], axis=0, keepdims=True)
+    loss = jnp.sum(sums(small_in, 1), axis=1, keepdims=True) * scale_ref[4:5, 0:1]
+    vectors = jnp.concatenate(
+        [sums(small_ref, 0), sums(small_ref, 1), sums(small_in, 4), sums(small_in, 2), sums(small_in, 3),
+         sums(small_in, 0), jnp.zeros((2, D), F32)],
+        axis=0,
+    )
+    high = loss.astype(BF16).astype(F32)
+    row, lane = lax.broadcasted_iota(jnp.int32, (EXTRA, 128), 0), lane_of((EXTRA, 128))
+    for r in range(8):
+        owner = lax.bitwise_xor(me, r)
+        block = pltpu.roll(vectors, lax.rem(D - owner * ROWS, D), 1)[:, 0:128]
+        block = jnp.where((row == 6) & (lane == 0), high, block)
+        block = jnp.where((row == 6) & (lane == 1), loss - high, block)
+        dst = theirs_ref if r % 2 else mine_ref
+        for s in range(4):
+            tp = lax.bitwise_and(place + s, 3)
+            ups = gbup_ref[0:1, rows_of(tp * FFC, FFC)]
+            mids = jnp.concatenate(
+                [bias_ref[s][:, 0:COLS], bias_ref[s][:, 2 * COLS :]]
+                + [ups[:, 128 * j : 128 * j + 128] for j in range(4)]
+                + [jnp.zeros((2, 128), F32)],
+                axis=0,
+            )
+            dst[r // 2, s, :, 0:128] = block.astype(BF16)
+            dst[r // 2, s, :, 128:256] = mids.astype(BF16)
+            dst[r // 2, s, :, 256:384] = jnp.zeros((EXTRA, 128), BF16)
+
+
+def pull_back(x, halo, grads, w, small_two, gbup, scale, theirs, mine):
+    own, ext = x.shape[0], grads[0].shape[0]
+    full = lambda a: pl.BlockSpec(a.shape, lambda i: (0,) * a.ndim)
+    send = jax.ShapeDtypeStruct(theirs.shape, BF16)
+    tail = pl.BlockSpec((4, 4, EXTRA, WA), lambda i: (0, 0, ROWS // EXTRA, 0))
+    given = (x, halo, *grads, w, small_two, gbup, scale)
+    return pl.pallas_call(
+        pull_kernel,
+        grid=(1,),
+        in_specs=[full(a) for a in given] + [ANY, ANY],
+        out_specs=[
+            pl.BlockSpec((HALO, D), lambda i: (0, 0)),
+            pl.BlockSpec((own, D), lambda i: (0, 0)),
+            tail,
+            tail,
+        ],
+        out_shape=(
+            jax.ShapeDtypeStruct((HALO, D), BF16),
+            jax.ShapeDtypeStruct((own, D), F32),
+            send,
+            send,
+        ),
+        scratch_shapes=[pltpu.VMEM((16, D), F32), pltpu.VMEM((4, 1, WA), F32)],
+        input_output_aliases={10: 2, 11: 3},
+        compiler_params=params(20),
+        cost_estimate=SMALL,
+        name="pull_back",
+    )(*given, theirs, mine)
+
+
+def close_kernel(x_ref, gn_ref, back_ref, gh_ref, vec_ref, out_ref):
+    own = x_ref.shape[0]
+
+    def block(at, extra):
+        rows = rows_of(at, 128)
+        xhat, rstd = normalize(x_ref[rows, :].astype(F32))
+        g_n1 = gn_ref[rows, :] + extra
+        out_ref[rows, :] = gh_ref[rows, :] + norm_pull(g_n1, vec_ref[0:1, :], xhat, rstd)
+
+    def first(i, carry):
+        block(i * 128, 0.0)
+        return carry
+
+    def second(i, carry):
+        block(own - HALO + i * 128, back_ref[rows_of(i * 128, 128), :].astype(F32))
+        return carry
+
+    lax.fori_loop(0, (own - HALO) // 128, first, 0)
+    lax.fori_loop(0, HALO // 128, second, 0)
+
+
+def close(x, g_n1, back, g_h1, vec):
+    return pl.pallas_call(
+        close_kernel,
+        out_shape=jax.ShapeDtypeStruct(x.shape, F32),
+        compiler_params=params(12),
+        cost_estimate=SMALL,
+        name="close",
+    )(x, g_n1, back, g_h1, vec)
+
+
+def unpack_f_kernel(k_ref, r1, r2, r3, wo_ref, wup_ref, wdn_ref):
+    total = (k_ref[0].astype(F32) + r1[...].astype(F32)) + (r2[...].astype(F32) + r3[...].astype(F32))
+    wo_ref[...] = total[:, 0:COLS]
+    wup_ref[...] = total[:, COLS : COLS + FFC]
+    wdn_ref[...] = total[:, COLS + FFC :]
+
+
+def unpack_f(k, r1, r2, r3):
+    return pl.pallas_call(
+        unpack_f_kernel,
+        out_shape=(
+            jax.ShapeDtypeStruct((ROWS, COLS), F32),
+            jax.ShapeDtypeStruct((ROWS, FFC), F32),
+            jax.ShapeDtypeStruct((ROWS, FFC), F32),
+        ),
+        compiler_params=params(8),
+        name="unpack_f",
+    )(k, r1, r2, r3)
+
+
+def unpack_a_kernel(k_ref, r1, r2, r3, wq_ref, wk_ref, wv_ref, bq_ref, bv_ref, bup_ref, vec_ref):
+    me = lax.axis_index("fsdp")
+    total = (k_ref[0].astype(F32) + r1[...].astype(F32)) + (r2[...].astype(F32) + r3[...].astype(F32))
+    wq_ref[...] = total[0:ROWS, 0:COLS]
+    wk_ref[...] = total[0:ROWS, COLS : 2 * COLS]
+    wv_ref[...] = total[0:ROWS, 2 * COLS :]
+    vec_ref[...] = total[ROWS:, 0:128]
+    mids = pltpu.roll(total[ROWS:, 128:256], lax.rem(128 - me * 8, 128), 1)
+    for i in range(2):
+        bq_ref[i : i + 1, :] = mids[0:1, i * HD : i * HD + 8]
+        bv_ref[i : i + 1, :] = mids[1:2, i * HD : i * HD + 8]
+    for i in range(8):
+        at = (i % 2) * HD
+        bup_ref[i : i + 1, :] = mids[2 + i // 2 : 3 + i // 2, at : at + 8]
+
+
+def unpack_a(k, r1, r2, r3):
+    small = jax.ShapeDtypeStruct((ROWS, COLS), F32)
+    return pl.pallas_call(
+        unpack_a_kernel,
+        out_shape=(
+            small,
+            small,
+            small,
+            jax.ShapeDtypeStruct((2, 8), F32),
+            jax.ShapeDtypeStruct((2, 8), F32),
+            jax.ShapeDtypeStruct((8, 8), F32),
+            jax.ShapeDtypeStruct((EXTRA, 128), F32),
+        ),
+        compiler_params=params(8),
+        name="unpack_a",
+    )(k, r1, r2, r3)
+
+
+def to_mask(x, mask):
+    return lax.ppermute(x, "fsdp", [(i, i ^ mask) for i in range(8)])
+
+
+def to_step(x, step):
+    return lax.ppermute(x, "tp", [(i, (i + step) % 4) for i in range(4)])
+
+
+def add(a, b):
+    return (a.astype(F32) + b.astype(F32)).astype(BF16)
+
+
+def after(values, others):
+    return lax.optimization_barrier((values, others))[0]
+
+
+def local_fast(
+    layer_input, segment_ids, valid_mask, teacher, cotangent, ln1_gain, ln1_bias, w_q, w_k, w_v, b_q, b_v,
+    w_o, b_o, ln2_gain, ln2_bias, w_up, b_up, w_down, b_down
+):
+    place = lax.axis_index("tp")
+    own = layer_input.shape[0]
+    tokens_all = own * lax.axis_size("fsdp") * lax.axis_size("tp")
+
+    shard_a, shard_f = pack_weights(
+        (w_q, w_k, w_v, w_o.T, w_up, w_down.T, ln1_gain, ln1_bias, b_o, ln2_gain, ln2_bias, b_down, b_q, b_v, b_up,
+         valid_mask)
+    )
+    halo = lax.ppermute(layer_input[own - HALO :], "tp", [(i, i + 1) for i in range(3)])
+    line_a = jnp.stack([shard_a] + [to_step(shard_a, s) for s in (1, 2, 3)])
+    near_a = [line_a] + [to_mask(line_a, m) for m in (2, 4, 6)]
+    pieces_a = near_a + [to_mask(a, 1) for a in near_a]
+    shard_f = after(shard_f, pieces_a[4])
+    steps_f = [shard_f] + [to_step(shard_f, s) for s in (1, 2, 3)]
+
+    ids = segment_ids + LEN * jnp.arange(segment_ids.shape[0], dtype=jnp.int32)[:, None]
+    ids = jnp.concatenate([jnp.full((HALO,), -1, jnp.int32), ids.reshape(-1)])
+    ids = lax.dynamic_slice_in_dim(ids, place * own, HALO + own)
+    id_row, id_col = ids[None, :], ids[:, None]
+    mask = valid_mask.astype(F32)[:, None]
+    where = place.reshape(1).astype(jnp.int32)
+
+    q, k, v, kt, nt, w_all, vec, bup, scale = project(layer_input, halo, pieces_a, tokens_all)
+    line_f = jnp.stack(after(steps_f, q))
+    q_a = after(q, line_f)
+    f_x, f_y = to_mask(line_f, 2), to_mask(line_f, 4)
+    o_a, lse_a = attend(q_a, k, v, id_row, id_col, 0, 2)
+    q_b = after(q, o_a)
+    o_b, lse_b = attend(q_b, k, v, id_row, id_col, 2, 2)
+    f_x, f_y = after((f_x, f_y), o_b)
+    near_f = [line_f, f_x, f_y, to_mask(f_y[0:2], 2), to_mask(f_x[2:4], 4)]
+    pieces_f = near_f + [to_mask(a, 1) for a in near_f]
+    layer_out, g_h1, g_o, delta, theirs_f, mine_f, small_two, gbup = central(
+        layer_input, o_a, o_b, teacher, cotangent, mask, vec, bup, scale, pieces_f
+    )
+    lse = jnp.concatenate([lse_a, lse_b])
+
+    def backward(step, before):
+        return pair_backward(step, where, q, k, v, g_o, lse, delta, id_row, id_col, kt, nt, before)
+
+    g0, *sums = backward(0, ())
+    half = add(after(mine_f, g0), to_mask(theirs_f, 1))
+    from_x, from_y = to_mask(half[3, 0:2], 2), to_mask(half[3, 2:4], 4)
+    sums = after(sums, half)
+    g1, *sums = backward(1, sums)
+    from_x, from_y = after((from_x, from_y), g1)
+    for_x = jnp.concatenate([half[1, 0:2], add(half[1, 2:4], from_y)])
+    for_y = jnp.concatenate([add(half[2, 0:2], from_x), half[2, 2:4]])
+    got_x, got_y = to_mask(for_x, 2), to_mask(for_y, 4)
+    sums = after(sums, (for_x, for_y))
+    g2, *sums = backward(2, sums)
+    g3, *sums = backward(3, sums)
+    got_x, got_y = after((got_x, got_y), g3)
+    line = (half[0].astype(F32) + got_x.astype(F32) + got_y.astype(F32)).astype(BF16)
+    line_up = [line[s] for s in (1, 2, 3)]
+    sums = after(sums, line_up)
+    grad_wo, grad_wup, grad_wdn = unpack_f(line, *[to_step(line_up[s - 1], s) for s in (1, 2, 3)])
+
+    gn_halo, gn_own, theirs_a, mine_a = pull_back(
+        layer_input, halo, (g0, g1, g2, g3), w_all, small_two, gbup, scale, *sums
+    )
+    back = lax.ppermute(gn_halo, "tp", [(i + 1, i) for i in range(3)])
+    half = add(mine_a, to_mask(theirs_a, 1))
+    from_x, from_y, from_xy = (to_mask(half[m], 2 * m) for m in (1, 2, 3))
+    line = (half[0].astype(F32) + from_x.astype(F32) + from_y.astype(F32) + from_xy.astype(F32)).astype(BF16)
+    grad_wq, grad_wk, grad_wv, grad_bq, grad_bv, grad_bup, few = unpack_a(
+        line, *[to_step(line[s], s) for s in (1, 2, 3)]
+    )
+    grad_input = close(layer_input, gn_own, back, g_h1, vec)
+    six = [few[j, 0:ROWS] for j in range(6)]
+    loss = few[6, 0] + few[6, 1]
+    return (
+        layer_out, loss, grad_input, six[0], six[1], grad_wq, grad_wk, grad_wv, grad_bq, grad_bv, grad_wo.T, six[2],
+        six[3], six[4], grad_wup, grad_bup, grad_wdn.T, six[5]
+    )
+
+
 def solution(mesh):
     tokens = P(("fsdp", "tp"), None)
     rows, crossed, heads = P("fsdp"), P("fsdp", "tp"), P("tp", "fsdp")
@@ -652,4 +1437,6 @@
         heads,
         rows,
     )
-    return jax.shard_map(local, mesh=mesh, in_specs=placed, out_specs=given, check_vma=False)
+    sizes = (mesh.shape["fsdp"], mesh.shape["tp"])
+    body = local_fast if sizes == (8, 4) else local
+    return jax.shard_map(body, mesh=mesh, in_specs=placed, out_specs=given, check_vma=False)

time: 345 us -> 183 us (0.53)
  waiting for transfers between devices: 135 us -> 42.4 us
  local copies, waits for them, and re-layouts: 72.6 us -> 8.34 us
  starting transfers between devices: 2.95 us -> 50.7 us
  blocking collectives: 23 us -> 0 us
  between operations: 22.1 us -> 3.48 us
  other arithmetic: 11.5 us -> 3.4 us
    reduce_scatter x2 -> x0, waiting for transfers between devices: 66.3 us -> none  [the longest x1 65.6 us: local(): mine = lax.psum_scatter(g_all, 'fsdp', scatter_dimension=0, tiled=False)]
    ppermute x2 -> x39, starting transfers between devices: 2.83 us -> 50.7 us  [the longest x12 31.5 us: to_step(): return lax.ppermute(x, 'tp', [(i, (i + step) % 4) for i in range(4)])]
    all_gather x1 -> x0, waiting for transfers between devices: 35.2 us -> none  [local(): every = lax.all_gather(lax.all_gather(shard, 'tp', axis=0), 'fsdp', axis=0)]
    unnamed x76 -> x31, local copies, waits for them, and re-layouts: 27.7 us -> 3.36 us
    all_gather x1 -> x0, blocking collectives: 23 us -> none  [local(): every = lax.all_gather(lax.all_gather(shard, 'tp', axis=0), 'fsdp', axis=0)]
    reshape x25 -> x1, local copies, waits for them, and re-layouts: 17.4 us -> 0.01 us  [local_fast(): ids = jnp.concatenate([jnp.full((HALO,), -1, jnp.int32), ids.reshape(-1)])]
    slice x20 -> x4, local copies, waits for them, and re-layouts: 15.7 us -> 3.74 us  [the longest x2 2.08 us: local_fast(): near_f = [line_f, f_x, f_y, to_mask(f_y[0:2], 2), to_mask(f_x[2:4], 4)]]
    ppermute x2 -> x39, waiting for transfers between devices: 33.6 us -> 42.4 us  [the longest x25 22.4 us: to_mask(): return lax.ppermute(x, 'fsdp', [(i, i ^ mask) for i in range(8)])]
  transfers between devices with their start and end apart: 5 -> 39, of which waited for: 5 -> 19; matrix products, arithmetic and copies ran while one was open for 1% -> 2% of each run, Pallas kernels for 1% -> 25%
where the time goes in v2:
time: 183 us; the launch traced here: 182 us
  Pallas kernels  74.1 us (40%)
  starting transfers between devices  50.7 us (28%)
  waiting for transfers between devices  42.4 us (23%)
  local copies, waits for them, and re-layouts  8.34 us (5%)
  between operations  3.48 us (2%)
  other arithmetic  3.4 us (2%)
    ppermute x12, starting transfers between devices, to_step(): return lax.ppermute(x, 'tp', [(i, (i + step) % 4) for i in range(4)])  31.5 us
    ppermute x25, waiting for transfers between devices, to_mask(): return lax.ppermute(x, 'fsdp', [(i, i ^ mask) for i in range(8)])  22.4 us
    pallas_call x4, Pallas kernels, pair_backward(): pl.pallas_call(pair_kernel, grid_spec=pltpu.PrefetchScalarGridSpec(num_sc...  21.4 us
    pallas_call x1, Pallas kernels, central(): pl.pallas_call(functools.partial(central_kernel, rb), out_shape=shapes, i...  19.5 us
    ppermute x25, starting transfers between devices, to_mask(): return lax.ppermute(x, 'fsdp', [(i, i ^ mask) for i in range(8)])  15.9 us
    pallas_call x2, Pallas kernels, attend(): pl.pallas_call(attend_kernel, grid=(pairs,), out_shape=(jax.ShapeDtypeStr...  13.9 us
    ppermute x12, waiting for transfers between devices, to_step(): return lax.ppermute(x, 'tp', [(i, (i + step) % 4) for i in range(4)])  9.43 us
    ppermute x1, waiting for transfers between devices, local_fast(): back = lax.ppermute(gn_halo, 'tp', [(i + 1, i) for i in range(3)])  9.33 us
  transfers between devices with their start and end apart: 39, of which 19 were waited for; matrix products, arithmetic and copies ran while one was open for 2% of the time, Pallas kernels for 25%

profile of v2, /device:TPU:0, one launch (start us, length us, event | category | flops | bytes accessed | tf_op | source)
XLA Modules:
  0.0 182.4 jit_solution(12008837084842246222)
XLA Ops:
  0.7 1.9 %pack_weights.1 = (bf16[72,384]{1,0:T(8,128)(2,1)}, bf16[64,1152]{1,0:T(8,128)(2,1)}) custom-call(bf16[64,128]{1,0:T(8,128)(2,1)} %wq_ref.1, bf16[64,128]{1,0:T(8,128)(2,1)} %wk_ref.1, bf16[64,128]{1,0:T(8,128)(2,1)} %wv_ref.1, bf16[64,128]{1,0:T(8,128)(2,1)} %bitcast.81, bf16[64,512]{1,0:T(8,128)(2,1)} %wup_ref.1, bf16[64,512]{1,0:T(8,128)(2,1)} %bitcast.76, ...), custom_call_target="tpu_custom_call" | custom-call | tf_op jit(solution)/shard_map/pack_weights/pallas_call | solution.py:668
  2.5 5.1 %collective-permute-start.3 = (bf16[72,384]{1,0:T(8,128)(2,1)}, bf16[72,384]{1,0:T(8,128)(2,1)S(1)}, u32[]{:S(2)}, u32[]{:S(2)}) collective-permute-start(bf16[72,384]{1,0:T(8,128)(2,1)} %get-tuple-element.87), channel_id=1, source_target_pairs={{0,3},{1,0},{2,1},{3,2},{4,7},{5,4},{6,5},{7,6},{8,11},{9,8},{10,9... | collective-permute-start | bytes 165896 | tf_op jit(solution)/shard_map/ppermute | solution.py:1303
  8.6 1.6 collective-permute-done.3
  10.2 2.8 %collective-permute-done.2 = bf16[72,384]{1,0:T(8,128)(2,1)S(1)} collective-permute-done((bf16[72,384]{1,0:T(8,128)(2,1)}, bf16[72,384]{1,0:T(8,128)(2,1)S(1)}, u32[]{:S(2)}, u32[]{:S(2)}) %collective-permute-start.2) | collective-permute-done | bytes 55328 | tf_op jit(solution)/shard_map/ppermute | solution.py:1303
  14.6 2.5 %collective-permute-start.6 = (bf16[4,72,384]{2,1,0:T(8,128)(2,1)S(1)}, bf16[4,72,384]{2,1,0:T(8,128)(2,1)S(1)}, u32[]{:S(2)}, u32[]{:S(2)}) collective-permute-start(bf16[4,72,384]{2,1,0:T(8,128)(2,1)S(1)} %pad_maximum_fusion.3.p0), channel_id=1, source_target_pairs={{0,24},{4,28},{8,16},{12,20},{16,8},{20,12},{24,0},{28,4},{1,25},{... | collective-permute-start | bytes 663560 | tf_op jit(solution)/shard_map/ppermute | solution.py:1299
  18.8 2.1 %collective-permute-start = (bf16[512,512]{1,0:T(8,128)(2,1)S(1)}, bf16[512,512]{1,0:T(8,128)(2,1)S(1)}, u32[]{:S(2)}, u32[]{:S(2)}) collective-permute-start(bf16[512,512]{1,0:T(8,128)(2,1)S(1)} %slice.84), channel_id=1, source_target_pairs={{0,1},{1,2},{2,3},{4,5},{5,6},{6,7},{8,9},{9,10},{10,11},{12,13},{... | collective-permute-start | bytes 1572872 | tf_op jit(solution)/shard_map/ppermute | solution.py:1326
  22.0 4.1 %collective-permute-done.5.p2 = bf16[4,72,384]{2,1,0:T(8,128)(2,1)S(1)} collective-permute-done((bf16[4,72,384]{2,1,0:T(8,128)(2,1)S(1)}, bf16[4,72,384]{2,1,0:T(8,128)(2,1)S(1)}, u32[]{:S(2)}, u32[]{:S(2)}) %collective-permute-start.5) | collective-permute-done | bytes 221216 | tf_op jit(solution)/shard_map/ppermute | solution.py:1299
  28.2 2.5 %collective-permute-start.12 = (bf16[64,1152]{1,0:T(8,128)(2,1)}, bf16[64,1152]{1,0:T(8,128)(2,1)S(1)}, u32[]{:S(2)}, u32[]{:S(2)}) collective-permute-start(bf16[64,1152]{1,0:T(8,128)(2,1)} %get-tuple-element.91), channel_id=1, source_target_pairs={{0,2},{1,3},{2,0},{3,1},{4,6},{5,7},{6,4},{7,5},{8,10},{9,11},{10,... | collective-permute-start | bytes 442376 | tf_op jit(solution)/shard_map/ppermute | solution.py:1303
  32.7 6.5 %project.1 = (bf16[768,512]{1,0:T(8,128)(2,1)S(1)}, bf16[1280,512]{1,0:T(8,128)(2,1)S(1)}, bf16[1280,512]{1,0:T(8,128)(2,1)S(1)}, bf16[512,1280]{1,0:T(8,128)(2,...) custom-call(bf16[768,512]{1,0:T(8,128)(2,1)S(1)} %copy-done.4, ...), custom_call_target="tpu_custom_call" | custom-call | flops 1 | bytes 1 | tf_op jit(solution)/shard_map/project/pallas_call | solution.py:780
  42.5 2.0 %collective-permute-done.12 = bf16[64,1152]{1,0:T(8,128)(2,1)S(1)} collective-permute-done((bf16[64,1152]{1,0:T(8,128)(2,1)}, bf16[64,1152]{1,0:T(8,128)(2,1)S(1)}, u32[]{:S(2)}, u32[]{:S(2)}) %collective-permute-start.12) | collective-permute-done | bytes 147488 | tf_op jit(solution)/shard_map/ppermute | solution.py:1303
  47.9 7.0 %attend.2 = (bf16[768,256]{1,0:T(8,128)(2,1)S(1)}, f32[2,8,768]{2,1,0:T(8,128)S(1)}) custom-call(bf16[768,512]{1,0:T(8,128)(2,1)S(1)} %get-tuple-element.99.q_ref, bf16[1280,512]{1,0:T(8,128)(2,1)S(1)} %get-tuple-element.96.k_ref, bf16[1280,512]{1,0:T(8,128)(2,1)S(1)} %get-tuple-element.97.v_ref, s32[1,1280]{1,0:T(1,128)S(1)} %broadcast_in_dim.11.idr_ref, ...), custom_call_target="tpu_custom_call" | custom-call | flops 1 | bytes 1 | tf_op jit(solution)/shard_map/attend/pallas_call | solution.py:841
  54.9 7.0 %attend.3 = (bf16[768,256]{1,0:T(8,128)(2,1)S(1)}, f32[2,8,768]{2,1,0:T(8,128)S(1)}) custom-call(bf16[768,512]{1,0:T(8,128)(2,1)S(1)} %get-tuple-element.99.q_ref, bf16[1280,512]{1,0:T(8,128)(2,1)S(1)} %get-tuple-element.96.k_ref, bf16[1280,512]{1,0:T(8,128)(2,1)S(1)} %get-tuple-element.97.v_ref, s32[1,1280]{1,0:T(1,128)S(1)} %broadcast_in_dim.11.idr_ref, ...), custom_call_target="tpu_custom_call" | custom-call | flops 1 | bytes 1 | tf_op jit(solution)/shard_map/attend/pallas_call | solution.py:841
  63.1 1.5 collective-permute-start.16
  66.7 5.8 %collective-permute-done.16.p3 = bf16[2,64,1152]{2,1,0:T(8,128)(2,1)S(1)} collective-permute-done((bf16[2,64,1152]{2,1,0:T(8,128)(2,1)S(1)}, bf16[2,64,1152]{2,1,0:T(8,128)(2,1)S(1)}, u32[]{:S(2)}, u32[]{:S(2)}) %collective-permute-start.16) | collective-permute-done | bytes 294944 | tf_op jit(solution)/shard_map/ppermute | solution.py:1299
  72.5 2.3 %collective-permute-done.17.p4 = bf16[2,64,1152]{2,1,0:T(8,128)(2,1)S(1)} collective-permute-done((bf16[2,64,1152]{2,1,0:T(8,128)(2,1)S(1)}, bf16[2,64,1152]{2,1,0:T(8,128)(2,1)S(1)}, u32[]{:S(2)}, u32[]{:S(2)}) %collective-permute-start.17) | collective-permute-done | bytes 294944 | tf_op jit(solution)/shard_map/ppermute | solution.py:1299
  76.4 19.5 %central.1 = (bf16[768,512]{1,0:T(8,128)(2,1)}, f32[768,512]{1,0:T(8,128)S(1)}, bf16[768,512]{1,0:T(8,128)(2,1)S(1)}, f32[4,8,768]{2,1,0:T(8,128)S(1)}, bf16[4,4...) custom-call(bf16[768,512]{1,0:T(8,128)(2,1)S(1)} %copy-done.5, ...), custom_call_target="tpu_custom_call" | custom-call | flops 1 | bytes 1 | tf_op jit(solution)/shard_map/central/pallas_call | solution.py:978
  96.2 5.5 %pair_backward.4 = (bf16[1280,384]{1,0:T(8,128)(2,1)S(1)}, bf16[4,4,72,384]{3,2,1,0:T(8,128)(2,1)S(1)}, bf16[4,4,72,384]{3,2,1,0:T(8,128)(2,1)S(1)}) custom-call(s32[1]{0:T(128)} %bitcast.10.sc_ref, bf16[768,512]{1,0:T(8,128)(2,1)S(1)} %get-tuple-element.99.q_ref, bf16[1280,512]{1,0:T(8,128)(2,1)S(1)} %get-tuple-element.96.k_ref, ...), custom_call_target="tpu_custom_call" | custom-call | flops 1 | bytes 1 | tf_op jit(solution)/shard_map/pair_backward/pallas_call | solution.py:1077
  103.6 5.3 %pair_backward.5 = (bf16[1280,384]{1,0:T(8,128)(2,1)S(1)}, bf16[4,4,72,384]{3,2,1,0:T(8,128)(2,1)S(1)}, bf16[4,4,72,384]{3,2,1,0:T(8,128)(2,1)S(1)}) custom-call(s32[1]{0:T(128)} %bitcast.10.sc_ref, bf16[768,512]{1,0:T(8,128)(2,1)S(1)} %get-tuple-element.99.q_ref, ...), custom_call_target="tpu_custom_call", output_to_operand_aliasing={{1}: (11, {}), {2}: (12, {})} | custom-call | flops 1 | bytes 1 | tf_op jit(solution)/shard_map/pair_backward/pallas_call | solution.py:1077
  108.9 3.0 %collective-permute-done.25 = bf16[2,64,1152]{2,1,0:T(8,128)(2,1)S(1)} collective-permute-done((bf16[2,64,1152]{2,1,0:T(8,128)(2,1)S(1)}, bf16[2,64,1152]{2,1,0:T(8,128)(2,1)S(1)}, u32[]{:S(2)}, u32[]{:S(2)}) %collective-permute-start.25) | collective-permute-done | bytes 294944 | tf_op jit(solution)/shard_map/ppermute | solution.py:1299
  113.0 1.6 collective-permute-start.27
  114.6 5.3 %pair_backward.6 = (bf16[1280,384]{1,0:T(8,128)(2,1)S(1)}, bf16[4,4,72,384]{3,2,1,0:T(8,128)(2,1)S(1)}, bf16[4,4,72,384]{3,2,1,0:T(8,128)(2,1)S(1)}) custom-call(s32[1]{0:T(128)} %bitcast.10.sc_ref, bf16[768,512]{1,0:T(8,128)(2,1)S(1)} %get-tuple-element.99.q_ref, ...), custom_call_target="tpu_custom_call", output_to_operand_aliasing={{1}: (11, {}), {2}: (12, {})} | custom-call | flops 1 | bytes 1 | tf_op jit(solution)/shard_map/pair_backward/pallas_call | solution.py:1077
  119.9 5.3 %pair_backward.7 = (bf16[1280,384]{1,0:T(8,128)(2,1)S(1)}, bf16[4,4,72,384]{3,2,1,0:T(8,128)(2,1)S(1)}, bf16[4,4,72,384]{3,2,1,0:T(8,128)(2,1)S(1)}) custom-call(s32[1]{0:T(128)} %bitcast.10.sc_ref, bf16[768,512]{1,0:T(8,128)(2,1)S(1)} %get-tuple-element.99.q_ref, ...), custom_call_target="tpu_custom_call", output_to_operand_aliasing={{1}: (11, {}), {2}: (12, {})} | custom-call | flops 1 | bytes 1 | tf_op jit(solution)/shard_map/pair_backward/pallas_call | solution.py:1077
  125.2 1.7 collective-permute-done.26
  127.7 6.4 %pull_back.1 = (bf16[512,512]{1,0:T(8,128)(2,1)S(1)}, f32[768,512]{1,0:T(8,128)S(1)}, bf16[4,4,72,384]{3,2,1,0:T(8,128)(2,1)S(1)}, bf16[4,4,72,384]{3,2,1,0:T(8,128)(2,1)S(1)}) custom-call(bf16[768,512]{1,0:T(8,128)(2,1)S(1)} %copy-done.5, bf16[512,512]{1,0:T(8,128)(2,1)S(1)} %copy-done.7, ...), custom_call_target="tpu_custom_call", output_to_operand_aliasing={{2}: (10, {}), {3}: (11, {})} | custom-call | flops 1 | bytes 1 | tf_op jit(solution)/shard_map/pull_back/pallas_call | solution.py:1189
  134.2 2.4 %collective-permute-done.28 = bf16[4,4,72,384]{3,2,1,0:T(8,128)(2,1)S(1)} collective-permute-done((bf16[4,4,72,384]{3,2,1,0:T(8,128)(2,1)S(1)}, bf16[4,4,72,384]{3,2,1,0:T(8,128)(2,1)S(1)}, u32[]{:S(2)}, u32[]{:S(2)}) %collective-permute-start.28) | collective-permute-done | bytes 884768 | tf_op jit(solution)/shard_map/ppermute | solution.py:1299
  140.5 4.2 %collective-permute-start.38 = (bf16[64,1152]{1,0:T(8,128)(2,1)S(1)}, bf16[64,1152]{1,0:T(8,128)(2,1)S(1)}, u32[]{:S(2)}, u32[]{:S(2)}) collective-permute-start(bf16[64,1152]{1,0:T(8,128)(2,1)S(1)} %get-tuple-element.165), channel_id=1, source_target_pairs={{0,3},{1,0},{2,1},{3,2},{4,7},{5,4},{6,5},{7,6},{8,11},{9,8},{10,9... | collective-permute-start | bytes 442376 | tf_op jit(solution)/shard_map/ppermute | solution.py:1303
  144.7 4.7 %collective-permute-start.37 = (bf16[64,1152]{1,0:T(8,128)(2,1)S(1)}, bf16[64,1152]{1,0:T(8,128)(2,1)S(1)}, u32[]{:S(2)}, u32[]{:S(2)}) collective-permute-start(bf16[64,1152]{1,0:T(8,128)(2,1)S(1)} %get-tuple-element.166), channel_id=1, source_target_pairs={{0,2},{1,3},{2,0},{3,1},{4,6},{5,7},{6,4},{7,5},{8,10},{9,11},{10,... | collective-permute-start | bytes 442376 | tf_op jit(solution)/shard_map/ppermute | solution.py:1303
  149.4 2.8 %collective-permute-start.36 = (bf16[64,1152]{1,0:T(8,128)(2,1)S(1)}, bf16[64,1152]{1,0:T(8,128)(2,1)S(1)}, u32[]{:S(2)}, u32[]{:S(2)}) collective-permute-start(bf16[64,1152]{1,0:T(8,128)(2,1)S(1)} %get-tuple-element.167), channel_id=1, source_target_pairs={{0,1},{1,2},{2,3},{3,0},{4,5},{5,6},{6,7},{7,4},{8,9},{9,10},{10,1... | collective-permute-start | bytes 442376 | tf_op jit(solution)/shard_map/ppermute | solution.py:1303
  153.7 9.0 %collective-permute-start.34 = (bf16[72,384]{1,0:T(8,128)(2,1)S(1)}, bf16[72,384]{1,0:T(8,128)(2,1)S(1)}, u32[]{:S(2)}, u32[]{:S(2)}) collective-permute-start(bf16[72,384]{1,0:T(8,128)(2,1)S(1)} %get-tuple-element.168), channel_id=1, source_target_pairs={{0,3},{1,0},{2,1},{3,2},{4,7},{5,4},{6,5},{7,6},{8,11},{9,8},{10,9... | collective-permute-start | bytes 165896 | tf_op jit(solution)/shard_map/ppermute | solution.py:1303
  164.1 9.3 %collective-permute-done.35.back_ref = bf16[512,512]{1,0:T(8,128)(2,1)S(1)} collective-permute-done((bf16[512,512]{1,0:T(8,128)(2,1)S(1)}, bf16[512,512]{1,0:T(8,128)(2,1)S(1)}, u32[]{:S(2)}, u32[]{:S(2)}) %collective-permute-start.35) | collective-permute-done | bytes 524320 | tf_op jit(solution)/shard_map/ppermute | solution.py:1379
  173.4 3.0 %close.1 = f32[768,512]{1,0:T(8,128)} custom-call(bf16[768,512]{1,0:T(8,128)(2,1)S(1)} %copy-done.5, f32[768,512]{1,0:T(8,128)S(1)} %get-tuple-element.144.gn_ref, bf16[512,512]{1,0:T(8,128)(2,1)S(1)} %collective-permute-done.35.back_ref, f32[768,512]{1,0:T(8,128)S(1)} %get-tuple-element.146.gh_ref, f32[8,512]{1,0:T(8,128)S(1)} %get-tuple-element.101.vec_ref), custom_call_target="tpu_custom_call" | custom-call | flops 1 | bytes 1 | tf_op jit(solution)/shard_map/close/pallas_call | solution.py:1235
  176.4 1.8 collective-permute-done.33.r2
  (117 shorter events, 33.6 us)
Async XLA Ops:
  2.5 7.7 %collective-permute-start.3 = (bf16[72,384]{1,0:T(8,128)(2,1)}, bf16[72,384]{1,0:T(8,128)(2,1)S(1)}, u32[]{:S(2)}, u32[]{:S(2)}) collective-permute-start(bf16[72,384]{1,0:T(8,128)(2,1)} %get-tuple-element.87), channel_id=1, source_target_pairs={{0,3},{1,0},{2,1},{3,2},{4,7},{5,4},{6,5},{7,6},{8,11},{9,8},{10,9... | collective-permute-start | bytes 165896 | tf_op jit(solution)/shard_map/ppermute | solution.py:1303
  7.6 6.2 %collective-permute-start.1 = (bf16[72,384]{1,0:T(8,128)(2,1)}, bf16[72,384]{1,0:T(8,128)(2,1)S(1)}, u32[]{:S(2)}, u32[]{:S(2)}) collective-permute-start(bf16[72,384]{1,0:T(8,128)(2,1)} %get-tuple-element.87), channel_id=1, source_target_pairs={{0,1},{1,2},{2,3},{3,0},{4,5},{5,6},{6,7},{7,4},{8,9},{9,10},{10,1... | collective-permute-start | bytes 165896 | tf_op jit(solution)/shard_map/ppermute | solution.py:1303
  14.6 7.0 %collective-permute-start.6 = (bf16[4,72,384]{2,1,0:T(8,128)(2,1)S(1)}, bf16[4,72,384]{2,1,0:T(8,128)(2,1)S(1)}, u32[]{:S(2)}, u32[]{:S(2)}) collective-permute-start(bf16[4,72,384]{2,1,0:T(8,128)(2,1)S(1)} %pad_maximum_fusion.3.p0), channel_id=1, source_target_pairs={{0,24},{4,28},{8,16},{12,20},{16,8},{20,12},{24,0},{28,4},{1,25},{... | collective-permute-start | bytes 663560 | tf_op jit(solution)/shard_map/ppermute | solution.py:1299
  17.2 8.9 %collective-permute-start.5 = (bf16[4,72,384]{2,1,0:T(8,128)(2,1)S(1)}, bf16[4,72,384]{2,1,0:T(8,128)(2,1)S(1)}, u32[]{:S(2)}, u32[]{:S(2)}) collective-permute-start(bf16[4,72,384]{2,1,0:T(8,128)(2,1)S(1)} %pad_maximum_fusion.3.p0), channel_id=1, source_target_pairs={{0,16},{4,20},{8,24},{12,28},{16,0},{20,4},{24,8},{28,12},{1,17},{... | collective-permute-start | bytes 663560 | tf_op jit(solution)/shard_map/ppermute | solution.py:1299
  18.8 13.9 %collective-permute-start = (bf16[512,512]{1,0:T(8,128)(2,1)S(1)}, bf16[512,512]{1,0:T(8,128)(2,1)S(1)}, u32[]{:S(2)}, u32[]{:S(2)}) collective-permute-start(bf16[512,512]{1,0:T(8,128)(2,1)S(1)} %slice.84), channel_id=1, source_target_pairs={{0,1},{1,2},{2,3},{4,5},{5,6},{6,7},{8,9},{9,10},{10,11},{12,13},{... | collective-permute-start | bytes 1572872 | tf_op jit(solution)/shard_map/ppermute | solution.py:1326
  20.9 6.0 %collective-permute-start.4 = (bf16[4,72,384]{2,1,0:T(8,128)(2,1)S(1)}, bf16[4,72,384]{2,1,0:T(8,128)(2,1)S(1)}, u32[]{:S(2)}, u32[]{:S(2)}) collective-permute-start(bf16[4,72,384]{2,1,0:T(8,128)(2,1)S(1)} %pad_maximum_fusion.3.p0), channel_id=1, source_target_pairs={{0,8},{4,12},{8,0},{12,4},{16,24},{20,28},{24,16},{28,20},{1,9},{5... | collective-permute-start | bytes 663560 | tf_op jit(solution)/shard_map/ppermute | solution.py:1299
  21.6 6.6 %collective-permute-start.10 = (bf16[4,72,384]{2,1,0:T(8,128)(2,1)S(1)}, bf16[4,72,384]{2,1,0:T(8,128)(2,1)S(1)}, u32[]{:S(2)}, u32[]{:S(2)}) collective-permute-start(bf16[4,72,384]{2,1,0:T(8,128)(2,1)S(1)} %collective-permute-done.6.p3), channel_id=1, source_target_pairs={{0,4},{4,0},{8,12},{12,8},{16,20},{20,16},{24,28},{28,24},{1,5},{5... | collective-permute-start | bytes 663560 | tf_op jit(solution)/shard_map/ppermute | solution.py:1299
  26.9 15.7 %collective-permute-start.13 = (bf16[64,1152]{1,0:T(8,128)(2,1)}, bf16[64,1152]{1,0:T(8,128)(2,1)S(1)}, u32[]{:S(2)}, u32[]{:S(2)}) collective-permute-start(bf16[64,1152]{1,0:T(8,128)(2,1)} %get-tuple-element.91), channel_id=1, source_target_pairs={{0,3},{1,0},{2,1},{3,2},{4,7},{5,4},{6,5},{7,6},{8,11},{9,8},{10,9... | collective-permute-start | bytes 442376 | tf_op jit(solution)/shard_map/ppermute | solution.py:1303
  28.2 16.3 %collective-permute-start.12 = (bf16[64,1152]{1,0:T(8,128)(2,1)}, bf16[64,1152]{1,0:T(8,128)(2,1)S(1)}, u32[]{:S(2)}, u32[]{:S(2)}) collective-permute-start(bf16[64,1152]{1,0:T(8,128)(2,1)} %get-tuple-element.91), channel_id=1, source_target_pairs={{0,2},{1,3},{2,0},{3,1},{4,6},{5,7},{6,4},{7,5},{8,10},{9,11},{10,... | collective-permute-start | bytes 442376 | tf_op jit(solution)/shard_map/ppermute | solution.py:1303
  30.6 13.9 %collective-permute-start.11 = (bf16[64,1152]{1,0:T(8,128)(2,1)}, bf16[64,1152]{1,0:T(8,128)(2,1)S(1)}, u32[]{:S(2)}, u32[]{:S(2)}) collective-permute-start(bf16[64,1152]{1,0:T(8,128)(2,1)} %get-tuple-element.91), channel_id=1, source_target_pairs={{0,1},{1,2},{2,3},{3,0},{4,5},{5,6},{6,7},{7,4},{8,9},{9,10},{10,1... | collective-permute-start | bytes 442376 | tf_op jit(solution)/shard_map/ppermute | solution.py:1303
  45.4 16.6 %collective-permute-start.15 = (bf16[4,64,1152]{2,1,0:T(8,128)(2,1)}, bf16[4,64,1152]{2,1,0:T(8,128)(2,1)}, u32[]{:S(2)}, u32[]{:S(2)}) collective-permute-start(bf16[4,64,1152]{2,1,0:T(8,128)(2,1)} %pad_maximum_fusion.p0), channel_id=1, source_target_pairs={{0,16},{4,20},{8,24},{12,28},{16,0},{20,4},{24,8},{28,12},{1,17},{... | collective-permute-start | bytes 1769480 | tf_op jit(solution)/shard_map/ppermute | solution.py:1299
  46.9 15.0 %collective-permute-start.14 = (bf16[4,64,1152]{2,1,0:T(8,128)(2,1)}, bf16[4,64,1152]{2,1,0:T(8,128)(2,1)}, u32[]{:S(2)}, u32[]{:S(2)}) collective-permute-start(bf16[4,64,1152]{2,1,0:T(8,128)(2,1)} %pad_maximum_fusion.p0), channel_id=1, source_target_pairs={{0,8},{4,12},{8,0},{12,4},{16,24},{20,28},{24,16},{28,20},{1,9},{5... | collective-permute-start | bytes 1769480 | tf_op jit(solution)/shard_map/ppermute | solution.py:1299
  47.9 27.1 %collective-permute-start.18 = (bf16[4,64,1152]{2,1,0:T(8,128)(2,1)}, bf16[4,64,1152]{2,1,0:T(8,128)(2,1)S(1)}, u32[]{:S(2)}, u32[]{:S(2)}) collective-permute-start(bf16[4,64,1152]{2,1,0:T(8,128)(2,1)} %pad_maximum_fusion.p0), channel_id=1, source_target_pairs={{0,4},{4,0},{8,12},{12,8},{16,20},{20,16},{24,28},{28,24},{1,5},{5... | collective-permute-start | bytes 1769480 | tf_op jit(solution)/shard_map/ppermute | solution.py:1299
  63.1 9.5 %collective-permute-start.16 = (bf16[2,64,1152]{2,1,0:T(8,128)(2,1)S(1)}, bf16[2,64,1152]{2,1,0:T(8,128)(2,1)S(1)}, u32[]{:S(2)}, u32[]{:S(2)}) collective-permute-start(bf16[2,64,1152]{2,1,0:T(8,128)(2,1)S(1)} %slice.85), channel_id=1, source_target_pairs={{0,8},{4,12},{8,0},{12,4},{16,24},{20,28},{24,16},{28,20},{1,9},{5... | collective-permute-start | bytes 884744 | tf_op jit(solution)/shard_map/ppermute | solution.py:1299
  65.6 9.2 %collective-permute-start.17 = (bf16[2,64,1152]{2,1,0:T(8,128)(2,1)S(1)}, bf16[2,64,1152]{2,1,0:T(8,128)(2,1)S(1)}, u32[]{:S(2)}, u32[]{:S(2)}) collective-permute-start(bf16[2,64,1152]{2,1,0:T(8,128)(2,1)S(1)} %slice.86), channel_id=1, source_target_pairs={{0,16},{4,20},{8,24},{12,28},{16,0},{20,4},{24,8},{28,12},{1,17},{... | collective-permute-start | bytes 884744 | tf_op jit(solution)/shard_map/ppermute | solution.py:1299
  66.2 10.2 %collective-permute-start.19 = (bf16[4,64,1152]{2,1,0:T(8,128)(2,1)}, bf16[4,64,1152]{2,1,0:T(8,128)(2,1)S(1)}, u32[]{:S(2)}, u32[]{:S(2)}) collective-permute-start(bf16[4,64,1152]{2,1,0:T(8,128)(2,1)} %collective-permute-done.14.p1), channel_id=1, source_target_pairs={{0,4},{4,0},{8,12},{12,8},{16,20},{20,16},{24,28},{28,24},{1,5},{5... | collective-permute-start | bytes 1769480 | tf_op jit(solution)/shard_map/ppermute | solution.py:1299
  66.2 10.2 %collective-permute-start.20 = (bf16[4,64,1152]{2,1,0:T(8,128)(2,1)}, bf16[4,64,1152]{2,1,0:T(8,128)(2,1)S(1)}, u32[]{:S(2)}, u32[]{:S(2)}) collective-permute-start(bf16[4,64,1152]{2,1,0:T(8,128)(2,1)} %collective-permute-done.15.p2), channel_id=1, source_target_pairs={{0,4},{4,0},{8,12},{12,8},{16,20},{20,16},{24,28},{28,24},{1,5},{5... | collective-permute-start | bytes 1769480 | tf_op jit(solution)/shard_map/ppermute | solution.py:1299
  95.9 5.7 %collective-permute-start.23 = (bf16[4,4,64,1152]{3,2,1,0:T(8,128)(2,1)S(1)}, bf16[4,4,64,1152]{3,2,1,0:T(8,128)(2,1)S(1)}, u32[]{:S(2)}, u32[]{:S(2)}) collective-permute-start(bf16[4,4,64,1152]{3,2,1,0:T(8,128)(2,1)S(1)} %get-tuple-element.118), channel_id=1, source_target_pairs={{0,4},{4,0},{8,12},{12,8},{16,20},{20,16},{24,28},{28,24},{1,5},{5... | collective-permute-start | bytes 7077896 | tf_op jit(solution)/shard_map/ppermute | solution.py:1299
  102.5 9.3 %collective-permute-start.25 = (bf16[2,64,1152]{2,1,0:T(8,128)(2,1)S(1)}, bf16[2,64,1152]{2,1,0:T(8,128)(2,1)S(1)}, u32[]{:S(2)}, u32[]{:S(2)}) collective-permute-start(bf16[2,64,1152]{2,1,0:T(8,128)(2,1)S(1)} %get-tuple-element.159), channel_id=1, source_target_pairs={{0,16},{4,20},{8,24},{12,28},{16,0},{20,4},{24,8},{28,12},{1,17},{... | collective-permute-start | bytes 884744 | tf_op jit(solution)/shard_map/ppermute | solution.py:1299
  103.1 9.0 %collective-permute-start.24 = (bf16[2,64,1152]{2,1,0:T(8,128)(2,1)S(1)}, bf16[2,64,1152]{2,1,0:T(8,128)(2,1)S(1)}, u32[]{:S(2)}, u32[]{:S(2)}) collective-permute-start(bf16[2,64,1152]{2,1,0:T(8,128)(2,1)S(1)} %get-tuple-element.160), channel_id=1, source_target_pairs={{0,8},{4,12},{8,0},{12,4},{16,24},{20,28},{24,16},{28,20},{1,9},{5... | collective-permute-start | bytes 884744 | tf_op jit(solution)/shard_map/ppermute | solution.py:1299
  112.3 14.6 %collective-permute-start.26 = (bf16[4,64,1152]{2,1,0:T(8,128)(2,1)S(1)}, bf16[4,64,1152]{2,1,0:T(8,128)(2,1)S(1)}, u32[]{:S(2)}, u32[]{:S(2)}) collective-permute-start(bf16[4,64,1152]{2,1,0:T(8,128)(2,1)S(1)} %pad_maximum_fusion.1), channel_id=1, source_target_pairs={{0,8},{4,12},{8,0},{12,4},{16,24},{20,28},{24,16},{28,20},{1,9},{5... | collective-permute-start | bytes 1769480 | tf_op jit(solution)/shard_map/ppermute | solution.py:1299
  113.0 14.4 %collective-permute-start.27 = (bf16[4,64,1152]{2,1,0:T(8,128)(2,1)S(1)}, bf16[4,64,1152]{2,1,0:T(8,128)(2,1)S(1)}, u32[]{:S(2)}, u32[]{:S(2)}) collective-permute-start(bf16[4,64,1152]{2,1,0:T(8,128)(2,1)S(1)} %pad_maximum_fusion.2), channel_id=1, source_target_pairs={{0,16},{4,20},{8,24},{12,28},{16,0},{20,4},{24,8},{28,12},{1,17},{... | collective-permute-start | bytes 1769480 | tf_op jit(solution)/shard_map/ppermute | solution.py:1299
  137.0 12.5 %collective-permute-start.29 = (bf16[4,72,384]{2,1,0:T(8,128)(2,1)S(1)}, bf16[4,72,384]{2,1,0:T(8,128)(2,1)S(1)}, u32[]{:S(2)}, u32[]{:S(2)}) collective-permute-start(bf16[4,72,384]{2,1,0:T(8,128)(2,1)S(1)} %get-tuple-element.162), channel_id=1, source_target_pairs={{0,8},{4,12},{8,0},{12,4},{16,24},{20,28},{24,16},{28,20},{1,9},{5... | collective-permute-start | bytes 663560 | tf_op jit(solution)/shard_map/ppermute | solution.py:1299
  138.4 13.8 %collective-permute-start.31 = (bf16[4,72,384]{2,1,0:T(8,128)(2,1)S(1)}, bf16[4,72,384]{2,1,0:T(8,128)(2,1)S(1)}, u32[]{:S(2)}, u32[]{:S(2)}) collective-permute-start(bf16[4,72,384]{2,1,0:T(8,128)(2,1)S(1)} %get-tuple-element.163), channel_id=1, source_target_pairs={{0,24},{4,28},{8,16},{12,20},{16,8},{20,12},{24,0},{28,4},{1,25},{... | collective-permute-start | bytes 663560 | tf_op jit(solution)/shard_map/ppermute | solution.py:1299
  139.9 13.6 %collective-permute-start.30 = (bf16[4,72,384]{2,1,0:T(8,128)(2,1)S(1)}, bf16[4,72,384]{2,1,0:T(8,128)(2,1)S(1)}, u32[]{:S(2)}, u32[]{:S(2)}) collective-permute-start(bf16[4,72,384]{2,1,0:T(8,128)(2,1)S(1)} %get-tuple-element.164), channel_id=1, source_target_pairs={{0,16},{4,20},{8,24},{12,28},{16,0},{20,4},{24,8},{28,12},{1,17},{... | collective-permute-start | bytes 663560 | tf_op jit(solution)/shard_map/ppermute | solution.py:1299
  140.5 22.2 %collective-permute-start.38 = (bf16[64,1152]{1,0:T(8,128)(2,1)S(1)}, bf16[64,1152]{1,0:T(8,128)(2,1)S(1)}, u32[]{:S(2)}, u32[]{:S(2)}) collective-permute-start(bf16[64,1152]{1,0:T(8,128)(2,1)S(1)} %get-tuple-element.165), channel_id=1, source_target_pairs={{0,3},{1,0},{2,1},{3,2},{4,7},{5,4},{6,5},{7,6},{8,11},{9,8},{10,9... | collective-permute-start | bytes 442376 | tf_op jit(solution)/shard_map/ppermute | solution.py:1303
  144.7 18.5 %collective-permute-start.37 = (bf16[64,1152]{1,0:T(8,128)(2,1)S(1)}, bf16[64,1152]{1,0:T(8,128)(2,1)S(1)}, u32[]{:S(2)}, u32[]{:S(2)}) collective-permute-start(bf16[64,1152]{1,0:T(8,128)(2,1)S(1)} %get-tuple-element.166), channel_id=1, source_target_pairs={{0,2},{1,3},{2,0},{3,1},{4,6},{5,7},{6,4},{7,5},{8,10},{9,11},{10,... | collective-permute-start | bytes 442376 | tf_op jit(solution)/shard_map/ppermute | solution.py:1303
  149.4 13.9 %collective-permute-start.36 = (bf16[64,1152]{1,0:T(8,128)(2,1)S(1)}, bf16[64,1152]{1,0:T(8,128)(2,1)S(1)}, u32[]{:S(2)}, u32[]{:S(2)}) collective-permute-start(bf16[64,1152]{1,0:T(8,128)(2,1)S(1)} %get-tuple-element.167), channel_id=1, source_target_pairs={{0,1},{1,2},{2,3},{3,0},{4,5},{5,6},{6,7},{7,4},{8,9},{9,10},{10,1... | collective-permute-start | bytes 442376 | tf_op jit(solution)/shard_map/ppermute | solution.py:1303
  152.2 21.2 %collective-permute-start.35 = (bf16[512,512]{1,0:T(8,128)(2,1)S(1)}, bf16[512,512]{1,0:T(8,128)(2,1)S(1)}, u32[]{:S(2)}, u32[]{:S(2)}) collective-permute-start(bf16[512,512]{1,0:T(8,128)(2,1)S(1)} %get-tuple-element.145), channel_id=1, source_target_pairs={{1,0},{2,1},{3,2},{5,4},{6,5},{7,6},{9,8},{10,9},{11,10},{13,12},{... | collective-permute-start | bytes 1572872 | tf_op jit(solution)/shard_map/ppermute | solution.py:1379
  153.7 22.7 %collective-permute-start.34 = (bf16[72,384]{1,0:T(8,128)(2,1)S(1)}, bf16[72,384]{1,0:T(8,128)(2,1)S(1)}, u32[]{:S(2)}, u32[]{:S(2)}) collective-permute-start(bf16[72,384]{1,0:T(8,128)(2,1)S(1)} %get-tuple-element.168), channel_id=1, source_target_pairs={{0,3},{1,0},{2,1},{3,2},{4,7},{5,4},{6,5},{7,6},{8,11},{9,8},{10,9... | collective-permute-start | bytes 165896 | tf_op jit(solution)/shard_map/ppermute | solution.py:1303
  162.7 15.5 %collective-permute-start.33 = (bf16[72,384]{1,0:T(8,128)(2,1)S(1)}, bf16[72,384]{1,0:T(8,128)(2,1)S(1)}, u32[]{:S(2)}, u32[]{:S(2)}) collective-permute-start(bf16[72,384]{1,0:T(8,128)(2,1)S(1)} %get-tuple-element.169), channel_id=1, source_target_pairs={{0,2},{1,3},{2,0},{3,1},{4,6},{5,7},{6,4},{7,5},{8,10},{9,11},{10,... | collective-permute-start | bytes 165896 | tf_op jit(solution)/shard_map/ppermute | solution.py:1303
  163.2 14.9 %collective-permute-start.32 = (bf16[72,384]{1,0:T(8,128)(2,1)S(1)}, bf16[72,384]{1,0:T(8,128)(2,1)S(1)}, u32[]{:S(2)}, u32[]{:S(2)}) collective-permute-start(bf16[72,384]{1,0:T(8,128)(2,1)S(1)} %get-tuple-element.170), channel_id=1, source_target_pairs={{0,1},{1,2},{2,3},{3,0},{4,5},{5,6},{6,7},{7,4},{8,9},{9,10},{10,1... | collective-permute-start | bytes 165896 | tf_op jit(solution)/shard_map/ppermute | solution.py:1303
  (22 other events, 233.6 us)

commit v3 on v2

--- a/solution.py
+++ b/solution.py
@@ -613,10 +613,18 @@
 FFC = 512
 WA = 3 * COLS
 WF = COLS + 2 * FFC
-MASKS_A = (0, 2, 4, 6, 1, 3, 5, 7)
+ALL = (0, 1, 2, 3)
+PIECES_A = ((0, ALL), (2, ALL), (4, ALL), (6, ALL), (1, ALL[0:2]), (1, ALL[2:4]), (3, ALL), (5, ALL), (7, ALL))
 SMALL = pl.CostEstimate(flops=1, bytes_accessed=1, transcendentals=0)
+
+
+def about(us):
+    return pl.CostEstimate(flops=us * 1000000, bytes_accessed=us * 3300000, transcendentals=0)
+
+
 ANY = pl.BlockSpec(memory_space=pl.ANY)
 VMEM = pl.BlockSpec(memory_space=pltpu.VMEM)
+FAR = pl.BlockSpec(memory_space=pl.ANY)
 
 
 def params(mib):
@@ -677,25 +685,25 @@
 
 
 def project_kernel(
-    tokens_all, x_ref, halo_ref, p0, p1, p2, p3, p4, p5, p6, p7,
-    q_ref, k_ref, v_ref, kt_ref, nt_ref, w_ref, vec_ref, bup_ref, scale_ref, ext_ref, head_ref, sem
+    tokens_all, x_ref, p0, p1, p2, p3, p4, p5, p6, p7, p8,
+    q_ref, k_ref, v_ref, kt_ref, nt_ref, w_ref, vec_ref, bup_ref, scale_ref, head_ref, ext_ref, sem
 ):
     me, place = lax.axis_index("fsdp"), lax.axis_index("tp")
-    pieces = (p0, p1, p2, p3, p4, p5, p6, p7)
+    pieces = (p0, p1, p2, p3, p4, p5, p6, p7, p8)
 
     def each(act):
-        for j, (ref, mask) in enumerate(zip(pieces, MASKS_A)):
+        for ref, (mask, steps) in zip(pieces, PIECES_A):
             owner = lax.bitwise_xor(me, mask)
-            for s in range(4):
+            for i, s in enumerate(steps):
                 tp = lax.bitwise_and(place - s + 4, 3)
-                act(j, ref, owner, s, tp)
-
-    def start_ext(j, ref, owner, s, tp):
-        pltpu.make_async_copy(ref.at[s, pl.ds(ROWS, EXTRA), :], ext_ref.at[4 * j + s], sem.at[0]).start()
-
-    def start_w(j, ref, owner, s, tp):
+                act(ref.at[i], 4 * mask + s, owner, tp)
+
+    def start_ext(ref, slot, owner, tp):
+        pltpu.make_async_copy(ref.at[pl.ds(ROWS, EXTRA), :], ext_ref.at[slot], sem.at[0]).start()
+
+    def start_w(ref, slot, owner, tp):
         pltpu.make_async_copy(
-            ref.at[s, pl.ds(0, ROWS), :],
+            ref.at[pl.ds(0, ROWS), :],
             w_ref.at[rows_of(owner * ROWS, ROWS, ROWS), rows_of(tp * WA, WA)],
             sem.at[1],
         ).start()
@@ -706,10 +714,10 @@
     lane = lane_of((EXTRA, D))
     vectors = jnp.zeros((EXTRA, D), F32)
     total = jnp.zeros((EXTRA, 128), F32)
-    for j, mask in enumerate(MASKS_A):
+    for j in range(8):
         block = ext_ref[4 * j, :, 0:128].astype(F32)
         wide = jnp.concatenate([block] * 4, axis=1)
-        vectors = jnp.where(lane // ROWS == lax.bitwise_xor(me, mask), wide, vectors)
+        vectors = jnp.where(lane // ROWS == lax.bitwise_xor(me, j), wide, vectors)
         for s in range(4):
             total += ext_ref[4 * j + s, :, 0:128].astype(F32)
     vec_ref[...] = vectors
@@ -726,157 +734,227 @@
         for i in range(4):
             bup_ref[:, rows_of(tp * FFC + 128 * i, 128)] = jnp.broadcast_to(block[2 + i : 3 + i], (8, 128))
     pltpu.make_async_copy(w_ref, w_ref, sem.at[1]).wait()
-    gain, offset = vectors[0:1], vectors[1:2]
-
-    def rows_done(x, at):
-        xhat, _ = normalize(x.astype(F32))
-        n1 = xhat * gain + offset
-        turned = jnp.transpose(n1).astype(BF16)
-        for i in range(8):
-            slot = lax.bitwise_xor(me, i)
-            nt_ref[rows_of(slot * ROWS, ROWS, ROWS), rows_of(at, 128)] = turned[ROWS * i : ROWS * (i + 1)]
-        made = dot(n1.astype(BF16), w_ref[...])
-        for t in range(4):
-            lanes = slice(t * COLS, (t + 1) * COLS)
-            k = made[:, t * WA + COLS : t * WA + 2 * COLS]
-            k_ref[rows_of(at, 128), lanes] = k.astype(BF16)
-            kt_ref[lanes, rows_of(at, 128)] = jnp.transpose(k).astype(BF16)
-            v = made[:, t * WA + 2 * COLS : (t + 1) * WA] + head_ref[1:2, lanes]
-            v_ref[rows_of(at, 128), lanes] = v.astype(BF16)
-        return made
-
-    def halo_rows(i, carry):
-        rows_done(halo_ref[rows_of(i * 128, 128), :], i * 128)
-        return carry
-
-    lax.fori_loop(0, HALO // 128, halo_rows, 0)
 
     def own_rows(i, carry):
         rows = rows_of(i * 128, 128)
-        made = rows_done(x_ref[rows, :], HALO + i * 128)
+        n1 = first_norm(x_ref[rows, :], vectors, me, nt_ref, rows)
+        made = dot(n1, w_ref[...])
         for t in range(4):
             lanes = slice(t * COLS, (t + 1) * COLS)
             q = (made[:, t * WA : t * WA + COLS] + head_ref[0:1, lanes]).astype(BF16)
             q_ref[rows, lanes] = q * jnp.asarray(SCALE, BF16)
+            keep_keys(made[:, t * WA + COLS : (t + 1) * WA], head_ref, k_ref, v_ref, kt_ref, rows, lanes)
         return carry
 
     lax.fori_loop(0, x_ref.shape[0] // 128, own_rows, 0)
 
 
-def project(x, halo, pieces, tokens_all):
+def first_norm(x, vectors, me, nt_ref, rows):
+    xhat, _ = normalize(x.astype(F32))
+    n1 = xhat * vectors[0:1] + vectors[1:2]
+    turned = jnp.transpose(n1).astype(BF16)
+    for i in range(8):
+        slot = lax.bitwise_xor(me, i)
+        nt_ref[rows_of(slot * ROWS, ROWS, ROWS), rows] = turned[ROWS * i : ROWS * (i + 1)]
+    return n1.astype(BF16)
+
+
+def keep_keys(made, head_ref, k_ref, v_ref, kt_ref, rows, lanes):
+    k = made[:, 0:COLS]
+    k_ref[rows, lanes] = k.astype(BF16)
+    kt_ref[lanes, rows] = jnp.transpose(k).astype(BF16)
+    v_ref[rows, lanes] = (made[:, COLS:] + head_ref[1:2, lanes]).astype(BF16)
+
+
+def project(x, pieces, tokens_all):
     own = x.shape[0]
-    ext = HALO + own
     shapes = (
         jax.ShapeDtypeStruct((own, D), BF16),
-        jax.ShapeDtypeStruct((ext, D), BF16),
-        jax.ShapeDtypeStruct((ext, D), BF16),
-        jax.ShapeDtypeStruct((D, ext), BF16),
-        jax.ShapeDtypeStruct((D, ext), BF16),
+        jax.ShapeDtypeStruct((own, D), BF16),
+        jax.ShapeDtypeStruct((own, D), BF16),
+        jax.ShapeDtypeStruct((D, own), BF16),
+        jax.ShapeDtypeStruct((D, own), BF16),
         jax.ShapeDtypeStruct((D, 4 * WA), BF16),
         jax.ShapeDtypeStruct((EXTRA, D), F32),
         jax.ShapeDtypeStruct((8, 4 * FFC), F32),
         jax.ShapeDtypeStruct((8, 128), F32),
+        jax.ShapeDtypeStruct((EXTRA, D), F32),
     )
     return pl.pallas_call(
         functools.partial(project_kernel, float(tokens_all)),
         out_shape=shapes,
-        in_specs=[VMEM, VMEM] + [ANY] * 8,
+        in_specs=[VMEM] + [FAR] * 9,
         out_specs=[VMEM] * len(shapes),
-        scratch_shapes=[
-            pltpu.VMEM((32, EXTRA, WA), BF16),
-            pltpu.VMEM((EXTRA, D), F32),
-            pltpu.SemaphoreType.DMA((2,)),
-        ],
-        compiler_params=params(20),
+        scratch_shapes=[pltpu.VMEM((32, EXTRA, WA), BF16), pltpu.SemaphoreType.DMA((2,))],
+        compiler_params=params(16),
         cost_estimate=SMALL,
         name="project",
-    )(x, halo, *pieces)
-
-
-def attend_kernel(q_ref, k_ref, v_ref, idr_ref, idc_ref, o_ref, lse_ref, bias_ref, stat_ref):
-    own = o_ref.shape[0]
-    qb, window = bias_ref.shape[1:]
-
+    )(x, *pieces)
+
+
+def project_halo_kernel(x_ref, w_ref, vec_ref, head_ref, k_ref, v_ref, kt_ref, nt_ref):
+    me = lax.axis_index("fsdp")
+
+    def halo_rows(i, carry):
+        rows = rows_of(i * 128, 128)
+        n1 = first_norm(x_ref[rows, :], vec_ref[...], me, nt_ref, rows)
+        for t in range(4):
+            made = dot(n1, w_ref[:, t * WA + COLS : (t + 1) * WA])
+            keep_keys(made, head_ref, k_ref, v_ref, kt_ref, rows, slice(t * COLS, (t + 1) * COLS))
+        return carry
+
+    lax.fori_loop(0, HALO // 128, halo_rows, 0)
+
+
+def project_halo(x, w, vec, head):
+    shape = jax.ShapeDtypeStruct((HALO, D), BF16)
+    turned = jax.ShapeDtypeStruct((D, HALO), BF16)
+    return pl.pallas_call(
+        project_halo_kernel,
+        out_shape=(shape, shape, turned, turned),
+        compiler_params=params(12),
+        cost_estimate=SMALL,
+        name="project_halo",
+    )(x, w, vec, head)
+
+
+QB = 256
+WINDOW = HALO + QB
+
+
+def mask_rows(idr_ref, idc_ref, first):
+    key = lax.broadcasted_iota(jnp.int32, (QB, WINDOW), 1)
+    query = lax.broadcasted_iota(jnp.int32, (QB, WINDOW), 0)
+    same = idc_ref[rows_of(HALO + first, QB), :] == idr_ref[:, rows_of(first, WINDOW)]
+    return jnp.where(same & (key <= query + HALO), 0.0, NEG)
+
+
+def mask_cols(idr_ref, idc_ref, first):
+    key = lax.broadcasted_iota(jnp.int32, (WINDOW, QB), 0)
+    query = lax.broadcasted_iota(jnp.int32, (WINDOW, QB), 1)
+    same = idc_ref[rows_of(first, WINDOW), :] == idr_ref[:, rows_of(HALO + first, QB)]
+    return jnp.where(same & (key <= query + HALO), 0.0, NEG)
+
+
+def attend_block(both, keys, values, bias, stat_ref):
+    lane = lane_of((QB, PAIR))
+    got = None
+    for h in range(2):
+        mine = (lane < HD) if h == 0 else (lane >= HD)
+        s = dot_t(jnp.where(mine, both, jnp.zeros_like(both)), keys) + bias[...]
+        top = jnp.max(s, axis=-1, keepdims=True)
+        p = jnp.exp(s - top)
+        total = jnp.sum(p, axis=-1, keepdims=True)
+        o = dot(p.astype(BF16), values) / total
+        got = o if h == 0 else jnp.where(mine, o, got)
+        stat_ref[:, h : h + 1] = top + jnp.log(total)
+    return got.astype(BF16), jnp.transpose(stat_ref[...])[0:8, :]
+
+
+def attend_far_kernel(q_ref, k_ref, v_ref, idr_ref, idc_ref, o_ref, lse_ref, bias_ref, stat_ref):
     @pl.when(pl.program_id(0) == 0)
     def _():
         stat_ref[...] = jnp.zeros_like(stat_ref)
-
-        def mask(i, carry):
-            first = i * qb
-            key = lax.broadcasted_iota(jnp.int32, (qb, window), 1)
-            query = lax.broadcasted_iota(jnp.int32, (qb, window), 0)
-            same = idc_ref[rows_of(HALO + first, qb), :] == idr_ref[:, rows_of(first, window)]
-            bias_ref[i] = jnp.where(same & (key <= query + HALO), 0.0, NEG)
-            return carry
-
-        lax.fori_loop(0, own // qb, mask, 0)
-
-    def query_block(i, carry):
-        first = i * qb
-        lane = lane_of((qb, PAIR))
-        keys, values = k_ref[rows_of(first, window), :], v_ref[rows_of(first, window), :]
-        both = q_ref[rows_of(first, qb), :]
-        got = None
-        for h in range(2):
-            mine = (lane < HD) if h == 0 else (lane >= HD)
-            s = dot_t(jnp.where(mine, both, jnp.zeros_like(both)), keys) + bias_ref[i]
-            top = jnp.max(s, axis=-1, keepdims=True)
-            p = jnp.exp(s - top)
-            total = jnp.sum(p, axis=-1, keepdims=True)
-            o = dot(p.astype(BF16), values) / total
-            got = o if h == 0 else jnp.where(mine, o, got)
-            stat_ref[:, h : h + 1] = top + jnp.log(total)
-        o_ref[rows_of(first, qb), :] = got.astype(BF16)
-        lse_ref[0, :, rows_of(first, qb)] = jnp.transpose(stat_ref[...])[0:8, :]
-        return carry
-
-    lax.fori_loop(0, own // qb, query_block, 0)
-
-
-def attend(q, k, v, id_row, id_col, first_pair, pairs):
-    own, ext = q.shape[0], k.shape[0]
-    qb = 256
-    at = lambda i: (0, first_pair + i)
-    flat = lambda i: (0, 0)
-    return pl.pallas_call(
-        attend_kernel,
-        grid=(pairs,),
-        out_shape=(
-            jax.ShapeDtypeStruct((own, pairs * PAIR), BF16),
-            jax.ShapeDtypeStruct((pairs, 8, own), F32),
-        ),
+        bias_ref[...] = mask_rows(idr_ref, idc_ref, HALO)
+
+    o_ref[...], lse_ref[0] = attend_block(q_ref[...], k_ref[...], v_ref[...], bias_ref, stat_ref)
+
+
+def attend_far(q, k, v, id_row, id_col):
+    own = q.shape[0]
+    return pl.pallas_call(
+        attend_far_kernel,
+        grid=(4,),
+        out_shape=(jax.ShapeDtypeStruct((own, D), BF16), jax.ShapeDtypeStruct((4, 8, own), F32)),
         in_specs=[
-            pl.BlockSpec((own, PAIR), at),
-            pl.BlockSpec((ext, PAIR), at),
-            pl.BlockSpec((ext, PAIR), at),
-            pl.BlockSpec((1, ext), flat),
-            pl.BlockSpec((ext, 1), flat),
+            pl.BlockSpec((QB, PAIR), lambda g: (HALO // QB, g)),
+            pl.BlockSpec((own, PAIR), lambda g: (0, g)),
+            pl.BlockSpec((own, PAIR), lambda g: (0, g)),
+            pl.BlockSpec(id_row.shape, lambda g: (0, 0)),
+            pl.BlockSpec(id_col.shape, lambda g: (0, 0)),
         ],
-        out_specs=[pl.BlockSpec((own, PAIR), lambda i: (0, i)), pl.BlockSpec((1, 8, own), lambda i: (i, 0, 0))],
-        scratch_shapes=[pltpu.VMEM((own // qb, qb, HALO + qb), F32), pltpu.VMEM((qb, 128), F32)],
-        compiler_params=params(14),
+        out_specs=[
+            pl.BlockSpec((QB, PAIR), lambda g: (HALO // QB, g)),
+            pl.BlockSpec((1, 8, QB), lambda g: (g, 0, HALO // QB)),
+        ],
+        scratch_shapes=[pltpu.VMEM((QB, WINDOW), F32), pltpu.VMEM((QB, 128), F32)],
+        compiler_params=params(10),
         cost_estimate=SMALL,
-        name="attend",
+        name="attend_far",
     )(q, k, v, id_row, id_col)
 
 
-PIECES_F = ((0, (0, 1, 2, 3)), (2, (0, 1, 2, 3)), (4, (0, 1, 2, 3)), (6, (0, 1)), (6, (2, 3)))
+def attend_near_kernel(
+    q_ref, kh_ref, ko_ref, vh_ref, vo_ref, idr_ref, idc_ref, o_in, lse_in, o_ref, lse_ref, bias_ref, k_ref, v_ref, stat_ref
+):
+    @pl.when(pl.program_id(0) == 0)
+    def _():
+        stat_ref[...] = jnp.zeros_like(stat_ref)
+        for i in range(HALO // QB):
+            bias_ref[i] = mask_rows(idr_ref, idc_ref, i * QB)
+
+    for dst, halo, own in ((k_ref, kh_ref, ko_ref), (v_ref, vh_ref, vo_ref)):
+        dst[0:HALO, :] = halo[...]
+        dst[HALO:, :] = own[...]
+
+    def block(i, carry):
+        first = i * QB
+        window, rows = rows_of(first, WINDOW), rows_of(first, QB)
+        o, lse = attend_block(q_ref[rows, :], k_ref[window, :], v_ref[window, :], bias_ref.at[i], stat_ref)
+        o_ref[rows, :] = o
+        lse_ref[0, :, rows] = lse
+        return carry
+
+    lax.fori_loop(0, HALO // QB, block, 0)
+
+
+def attend_near(base, q, k_halo, k, v_halo, v, id_row, id_col, o, lse):
+    at = lambda i: (0, base + i)
+    block = pl.BlockSpec((HALO, PAIR), at)
+    return pl.pallas_call(
+        attend_near_kernel,
+        grid=(2,),
+        out_shape=(jax.ShapeDtypeStruct(o.shape, BF16), jax.ShapeDtypeStruct(lse.shape, F32)),
+        in_specs=[block] * 5
+        + [
+            pl.BlockSpec(id_row.shape, lambda i: (0, 0)),
+            pl.BlockSpec(id_col.shape, lambda i: (0, 0)),
+            ANY,
+            ANY,
+        ],
+        out_specs=[block, pl.BlockSpec((1, 8, HALO), lambda i: (base + i, 0, 0))],
+        scratch_shapes=[
+            pltpu.VMEM((HALO // QB, QB, WINDOW), F32),
+            pltpu.VMEM((2 * HALO, PAIR), BF16),
+            pltpu.VMEM((2 * HALO, PAIR), BF16),
+            pltpu.VMEM((QB, 128), F32),
+        ],
+        input_output_aliases={7: 0, 8: 1},
+        compiler_params=params(12),
+        cost_estimate=SMALL,
+        name="attend_near",
+    )(q, k_halo, k, v_halo, v, id_row, id_col, o, lse)
+
+
+PIECES_F = ((0, (0,)), (0, (1,)), (0, (2,)), (0, (3,)), (2, (0, 1, 2, 3)), (4, (0, 1, 2, 3)), (6, (0, 1)), (6, (2, 3)))
 
 
 def central_kernel(
-    rb, x_ref, oa_ref, ob_ref, teacher_ref, cot_ref, mask_ref, vec_ref, bup_ref, scale_ref,
-    p0, p1, p2, p3, p4, p5, p6, p7, p8, p9,
+    rb, x_ref, o_ref, teacher_ref, cot_ref, mask_ref, vec_ref, bup_ref, scale_ref,
+    *rest
+):
+    pieces = rest[:16]
+    (
     out_ref, gh_ref, go_ref, delta_ref, theirs_ref, mine_ref, small_ref, gbup_ref,
-    wo_ref, wup_ref, wdn_ref, o_ref, slope_ref, hid_ref, gpre_ref, n2t_ref, gmlpt_ref, gattnt_ref, sem
-):
+    wo_ref, wup_ref, wdn_ref, slope_ref, hid_ref, gpre_ref, n2t_ref, gmlpt_ref, gattnt_ref, sem
+    ) = rest[16:]
     me, place = lax.axis_index("fsdp"), lax.axis_index("tp")
     own, ff = x_ref.shape[0], 4 * FFC
-    pieces = (p0, p1, p2, p3, p4, p5, p6, p7, p8, p9)
     parts = ((wo_ref, 0, COLS), (wup_ref, COLS, FFC), (wdn_ref, COLS + FFC, FFC))
     for n, (dst, start, size) in enumerate(parts):
         for j, ref in enumerate(pieces):
-            mask, steps = PIECES_F[j % 5]
-            owner = lax.bitwise_xor(me, mask + j // 5)
+            mask, steps = PIECES_F[j % 8]
+            owner = lax.bitwise_xor(me, mask + j // 8)
             for i, s in enumerate(steps):
                 tp = lax.bitwise_and(place - s + 4, 3)
                 pltpu.make_async_copy(
@@ -885,8 +963,6 @@
                     sem.at[n],
                 ).start()
     small_ref[...] = jnp.zeros_like(small_ref)
-    o_ref[:, 0 : D // 2] = oa_ref[...]
-    o_ref[:, D // 2 :] = ob_ref[...]
     head_of = lax.broadcasted_iota(jnp.int32, (D, 128), 0) // HD
     pick = (head_of == lax.broadcasted_iota(jnp.int32, (D, 128), 1)).astype(BF16)
     out_bias, gain, offset, down_bias = (vec_ref[j : j + 1, :] for j in range(2, 6))
@@ -962,7 +1038,7 @@
     lax.fori_loop(0, 4, grads, 0)
 
 
-def central(x, o_a, o_b, teacher, cot, mask, vec, bup, scale, pieces):
+def central(x, o, teacher, cot, mask, vec, bup, scale, pieces):
     own = x.shape[0]
     rb = 256
     shapes = (
@@ -978,13 +1054,12 @@
     return pl.pallas_call(
         functools.partial(central_kernel, rb),
         out_shape=shapes,
-        in_specs=[VMEM] * 9 + [ANY] * 10,
+        in_specs=[VMEM] * 8 + [FAR] * 16,
         out_specs=[VMEM] * len(shapes),
         scratch_shapes=[
             pltpu.VMEM((D, D), BF16),
             pltpu.VMEM((D, 4 * FFC), BF16),
             pltpu.VMEM((D, 4 * FFC), BF16),
-            pltpu.VMEM((own, D), BF16),
             pltpu.VMEM((rb, 4 * FFC), F32),
             pltpu.VMEM((own, 4 * FFC), BF16),
             pltpu.VMEM((own, 4 * FFC), BF16),
@@ -996,218 +1071,254 @@
         compiler_params=params(36),
         cost_estimate=SMALL,
         name="central",
-    )(x, o_a, o_b, teacher, cot, mask, vec, bup, scale, *pieces)
-
-
-def pair_core(q_ref, k_ref, v_ref, go_ref, lse_ref, delta_ref, idr_ref, idc_ref, kt_ref, nt_ref,
-              g_ref, theirs_ref, mine_ref, bias_ref, dqt_ref, dk_ref, dv_ref):
-    ext, own = k_ref.shape[0], q_ref.shape[0]
-    window, qb = bias_ref.shape
+    )(x, o, teacher, cot, mask, vec, bup, scale, *pieces)
+
+
+def pull_block(both_q, both_g, keys, values, keys_t, bias, lse, delta, dk_ref, dv_ref, window):
+    lane = lane_of((QB, PAIR))
+    turned = []
+    for h in range(2):
+        mine = (lane < HD) if h == 0 else (lane >= HD)
+        q = jnp.where(mine, both_q, jnp.zeros_like(both_q))
+        g_o = jnp.where(mine, both_g, jnp.zeros_like(both_g))
+        p = jnp.exp(dot_t(keys, q) + bias[...] - lse[h : h + 1])
+        ds = (p * (dot_t(values, g_o) - delta[h : h + 1])).astype(BF16)
+        dv_ref[window, :] += dot(p.astype(BF16), g_o)
+        dk_ref[window, :] += dot(ds, q)
+        turned.append(dot(keys_t[h * HD : (h + 1) * HD, :], ds))
+    return (jnp.transpose(jnp.concatenate(turned, axis=0)) * SCALE).astype(BF16)
+
+
+def pull_near_kernel(
+    q_ref, go_ref, kh_ref, ko_ref, vh_ref, vo_ref, lse_ref, delta_ref, idr_ref, idc_ref, kth_ref, kto_ref, *rest
+):
+    gh_ref, gq_ref, part_ref, bias_ref, k_ref, v_ref, kt_ref, dk_ref, dv_ref = rest[-9:]
+
+    @pl.when(pl.program_id(0) == 0)
+    def _():
+        for i in range(HALO // QB):
+            bias_ref[i] = mask_cols(idr_ref, idc_ref, i * QB)
+
+    for dst, halo, own in ((k_ref, kh_ref, ko_ref), (v_ref, vh_ref, vo_ref)):
+        dst[0:HALO, :] = halo[...]
+        dst[HALO:, :] = own[...]
+    kt_ref[:, 0:HALO] = kth_ref[...]
+    kt_ref[:, HALO:] = kto_ref[...]
     dk_ref[...] = jnp.zeros_like(dk_ref)
     dv_ref[...] = jnp.zeros_like(dv_ref)
 
-    def query_block(i, carry):
-        first = i * qb
-        key = lax.broadcasted_iota(jnp.int32, (window, qb), 0)
-        query = lax.broadcasted_iota(jnp.int32, (window, qb), 1)
-        same = idc_ref[rows_of(first, window), :] == idr_ref[:, rows_of(HALO + first, qb)]
-        bias_ref[...] = jnp.where(same & (key <= query + HALO), 0.0, NEG)
-        lane = lane_of((qb, PAIR))
-        keys, values = k_ref[rows_of(first, window), :], v_ref[rows_of(first, window), :]
-        both_q, both_g = q_ref[rows_of(first, qb), :], go_ref[rows_of(first, qb), :]
-        all_lse, all_delta = lse_ref[0, :, rows_of(first, qb)], delta_ref[0, :, rows_of(first, qb)]
-        for h in range(2):
-            mine = (lane < HD) if h == 0 else (lane >= HD)
-            q = jnp.where(mine, both_q, jnp.zeros_like(both_q))
-            g_o = jnp.where(mine, both_g, jnp.zeros_like(both_g))
-            p = jnp.exp(dot_t(keys, q) + bias_ref[...] - all_lse[h : h + 1])
-            ds = (p * (dot_t(values, g_o) - all_delta[h : h + 1])).astype(BF16)
-            dv_ref[rows_of(first, window), :] += dot(p.astype(BF16), g_o)
-            dk_ref[rows_of(first, window), :] += dot(ds, q)
-            dqt_ref[h * HD : (h + 1) * HD, rows_of(first, qb)] = dot(
-                kt_ref[h * HD : (h + 1) * HD, rows_of(first, window)], ds
-            )
-        return carry
-
-    lax.fori_loop(0, own // qb, query_block, 0)
-    g_ref[0:HALO, 0:COLS] = jnp.zeros((HALO, COLS), BF16)
-
-    def gather(i, carry):
-        rows = rows_of(i * 128, 128)
-        g_ref[rows, COLS : 2 * COLS] = dk_ref[rows, :].astype(BF16)
-        g_ref[rows, 2 * COLS :] = dv_ref[rows, :].astype(BF16)
-        return carry
-
-    lax.fori_loop(0, ext // 128, gather, 0)
-
-    def gather_q(i, carry):
-        cols = rows_of(i * 128, 128)
-        g_ref[rows_of(HALO + i * 128, 128), 0:COLS] = (jnp.transpose(dqt_ref[:, cols]) * SCALE).astype(BF16)
-        return carry
-
-    lax.fori_loop(0, own // 128, gather_q, 0)
-    low = dot(nt_ref[...], g_ref[...]).astype(BF16)
-    for r in range(8):
-        dst = theirs_ref if r % 2 else mine_ref
-        dst[r // 2, 0, 0:ROWS, :] = low[ROWS * r : ROWS * (r + 1)]
-
-
-def pair_kernel(sc_ref, q_ref, k_ref, v_ref, go_ref, lse_ref, delta_ref, idr_ref, idc_ref, kt_ref, nt_ref, *rest):
-    g_ref, theirs_ref, mine_ref, *scratch = rest[-7:]
-    pair_core(q_ref, k_ref, v_ref, go_ref, lse_ref, delta_ref, idr_ref, idc_ref, kt_ref, nt_ref,
-              g_ref, theirs_ref, mine_ref, *scratch)
-
-
-def pair_backward(step, where, q, k, v, g_o, lse, delta, id_row, id_col, kt, nt, before):
-    own, ext = q.shape[0], k.shape[0]
-    qb = 256
-
-    def at(i, sc):
-        return (0, lax.bitwise_and(sc[0] + step, 3))
-
-    def deep(i, sc):
-        return (lax.bitwise_and(sc[0] + step, 3), 0, 0)
-
-    def down(i, sc):
-        return (lax.bitwise_and(sc[0] + step, 3), 0)
-
-    flat = lambda i, sc: (0, 0)
-    send = jax.ShapeDtypeStruct((4, 4, ROWS + EXTRA, WA), BF16)
-    block = pl.BlockSpec((4, 1, ROWS + EXTRA, WA), lambda i, sc: (0, step, 0, 0))
-    return pl.pallas_call(
-        pair_kernel,
-        grid_spec=pltpu.PrefetchScalarGridSpec(
-            num_scalar_prefetch=1,
-            grid=(1,),
-            in_specs=[
-                pl.BlockSpec((own, PAIR), at),
-                pl.BlockSpec((ext, PAIR), at),
-                pl.BlockSpec((ext, PAIR), at),
-                pl.BlockSpec((own, PAIR), at),
-                pl.BlockSpec((1, 8, own), deep),
-                pl.BlockSpec((1, 8, own), deep),
-                pl.BlockSpec((1, ext), flat),
-                pl.BlockSpec((ext, 1), flat),
-                pl.BlockSpec((PAIR, ext), down),
-                pl.BlockSpec((D, ext), flat),
-            ]
-            + [ANY] * len(before),
-            out_specs=[pl.BlockSpec((ext, WA), flat), block, block],
-            scratch_shapes=[
-                pltpu.VMEM((HALO + qb, qb), F32),
-                pltpu.VMEM((PAIR, own), F32),
-                pltpu.VMEM((ext, PAIR), F32),
-                pltpu.VMEM((ext, PAIR), F32),
-            ],
+    def block(i, carry):
+        first = i * QB
+        window, rows = rows_of(first, WINDOW), rows_of(first, QB)
+        gq_ref[rows, :] = pull_block(
+            q_ref[rows, :], go_ref[rows, :], k_ref[window, :], v_ref[window, :], kt_ref[:, window],
+            bias_ref.at[i], lse_ref[0, :, rows], delta_ref[0, :, rows], dk_ref, dv_ref, window
+        )
+        return carry
+
+    lax.fori_loop(0, HALO // QB, block, 0)
+    for n, ref in enumerate((dk_ref, dv_ref)):
+        lanes = slice(n * PAIR, (n + 1) * PAIR)
+        gh_ref[:, lanes] = ref[0:HALO, :].astype(BF16)
+        part_ref[:, lanes] = ref[HALO:, :]
+
+
+def pull_near(base, q, g_o, k_halo, k, v_halo, v, lse, delta, id_row, id_col, kt_halo, kt, before):
+    at = lambda i: (0, base + i)
+    block = pl.BlockSpec((HALO, PAIR), at)
+    deep = pl.BlockSpec((1, 8, HALO), lambda i: (base + i, 0, 0))
+    down = pl.BlockSpec((PAIR, HALO), lambda i: (base + i, 0))
+    wide = pl.BlockSpec((HALO, 2 * PAIR), at)
+    return pl.pallas_call(
+        pull_near_kernel,
+        grid=(2,),
+        out_shape=(
+            jax.ShapeDtypeStruct((HALO, 2 * D), BF16),
+            jax.ShapeDtypeStruct((HALO, D), BF16),
+            jax.ShapeDtypeStruct((HALO, 2 * D), F32),
         ),
-        out_shape=(jax.ShapeDtypeStruct((ext, WA), BF16), send, send),
-        input_output_aliases={11: 1, 12: 2} if before else {},
+        in_specs=[block] * 6
+        + [
+            deep,
+            deep,
+            pl.BlockSpec(id_row.shape, lambda i: (0, 0)),
+            pl.BlockSpec(id_col.shape, lambda i: (0, 0)),
+            down,
+            down,
+        ]
+        + [ANY] * len(before),
+        out_specs=[wide, block, wide],
+        scratch_shapes=[
+            pltpu.VMEM((HALO // QB, WINDOW, QB), F32),
+            pltpu.VMEM((2 * HALO, PAIR), BF16),
+            pltpu.VMEM((2 * HALO, PAIR), BF16),
+            pltpu.VMEM((PAIR, 2 * HALO), BF16),
+            pltpu.VMEM((2 * HALO, PAIR), F32),
+            pltpu.VMEM((2 * HALO, PAIR), F32),
+        ],
+        input_output_aliases={12: 0, 13: 1, 14: 2} if before else {},
         compiler_params=params(14),
         cost_estimate=SMALL,
-        name="pair_backward",
-    )(where, q, k, v, g_o, lse, delta, id_row, id_col, kt, nt, *before)
-
-
-def pull_kernel(x_ref, halo_ref, g0, g1, g2, g3, w_ref, small_in, gbup_ref, scale_ref, theirs_in, mine_in,
-                gn_halo_ref, gn_ref, theirs_ref, mine_ref, small_ref, bias_ref):
+        name="pull_near",
+    )(q, g_o, k_halo, k, v_halo, v, lse, delta, id_row, id_col, kt_halo, kt, *before)
+
+
+def pull_far_kernel(
+    q_ref, go_ref, k_ref, v_ref, lse_ref, delta_ref, idr_ref, idc_ref, kt_ref, gq_ref, part_ref, g_ref, bias_ref, dk_ref, dv_ref
+):
+    @pl.when(pl.program_id(0) == 0)
+    def _():
+        bias_ref[...] = mask_cols(idr_ref, idc_ref, HALO)
+
+    for n, ref in enumerate((dk_ref, dv_ref)):
+        ref[0:HALO, :] = part_ref[:, n * PAIR : (n + 1) * PAIR]
+        ref[HALO:, :] = jnp.zeros((QB, PAIR), F32)
+    g_ref[0:HALO, 0:COLS] = gq_ref[...]
+    g_ref[HALO:, 0:COLS] = pull_block(
+        q_ref[...], go_ref[...], k_ref[...], v_ref[...], kt_ref[...],
+        bias_ref, lse_ref[0], delta_ref[0], dk_ref, dv_ref, slice(None)
+    )
+    g_ref[:, COLS : 2 * COLS] = dk_ref[...].astype(BF16)
+    g_ref[:, 2 * COLS :] = dv_ref[...].astype(BF16)
+
+
+def pull_far(q, g_o, k, v, lse, delta, id_row, id_col, kt, gq_near, part):
+    own = q.shape[0]
+    last = pl.BlockSpec((QB, PAIR), lambda g: (HALO // QB, g))
+    full = pl.BlockSpec((own, PAIR), lambda g: (0, g))
+    deep = pl.BlockSpec((1, 8, QB), lambda g: (g, 0, HALO // QB))
+    return pl.pallas_call(
+        pull_far_kernel,
+        grid=(4,),
+        out_shape=jax.ShapeDtypeStruct((own, 4 * WA), BF16),
+        in_specs=[
+            last,
+            last,
+            full,
+            full,
+            deep,
+            deep,
+            pl.BlockSpec(id_row.shape, lambda g: (0, 0)),
+            pl.BlockSpec(id_col.shape, lambda g: (0, 0)),
+            pl.BlockSpec((PAIR, own), lambda g: (g, 0)),
+            pl.BlockSpec((HALO, PAIR), lambda g: (0, g)),
+            pl.BlockSpec((HALO, 2 * PAIR), lambda g: (0, g)),
+        ],
+        out_specs=pl.BlockSpec((own, WA), lambda g: (0, g)),
+        scratch_shapes=[
+            pltpu.VMEM((WINDOW, QB), F32),
+            pltpu.VMEM((own, PAIR), F32),
+            pltpu.VMEM((own, PAIR), F32),
+        ],
+        compiler_params=params(12),
+        cost_estimate=SMALL,
+        name="pull_far",
+    )(q, g_o, k, v, lse, delta, id_row, id_col, kt, gq_near, part)
+
+
+def norm_sums(small_ref, x, g_n1):
+    xhat, _ = normalize(x.astype(F32))
+    small_ref[0:8, :] += fold(g_n1 * xhat)
+    small_ref[8:16, :] += fold(g_n1)
+
+
+def halo_back_kernel(g_ref, w_ref, x_ref, out_ref, small_ref):
+    small_ref[...] = jnp.zeros_like(small_ref)
+
+    def block(i, carry):
+        rows = rows_of(i * 128, 128)
+        total = None
+        for t in range(4):
+            part = dot_t(g_ref[rows, t * 2 * COLS : (t + 1) * 2 * COLS], w_ref[:, t * WA + COLS : (t + 1) * WA])
+            total = part if total is None else total + part
+        out_ref[rows, :] = total.astype(BF16)
+        norm_sums(small_ref, x_ref[rows, :], total)
+        return carry
+
+    lax.fori_loop(0, HALO // 128, block, 0)
+
+
+def halo_back(g_halo, w, halo):
+    return pl.pallas_call(
+        halo_back_kernel,
+        out_shape=(jax.ShapeDtypeStruct((HALO, D), BF16), jax.ShapeDtypeStruct((16, D), F32)),
+        compiler_params=params(10),
+        cost_estimate=SMALL,
+        name="halo_back",
+    )(g_halo, w, halo)
+
+
+def own_back_kernel(
+    x_ref, gh_ref, g_ref, nth_ref, nto_ref, w_ref, small_halo, small_two, gbup_ref, scale_ref,
+    gn_ref, theirs_ref, mine_ref, small_ref, sum_ref
+):
     me, place = lax.axis_index("fsdp"), lax.axis_index("tp")
-    own, ext = x_ref.shape[0], g0.shape[0]
-    grads = (g0, g1, g2, g3)
-    small_ref[...] = jnp.zeros_like(small_ref)
-
-    def pull(at, skip):
-        total = None
-        for s, ref in enumerate(grads):
-            tp = lax.bitwise_and(place + s, 3)
-            part = dot_t(
-                ref[rows_of(at, 128), skip:], w_ref[:, rows_of(tp * WA + skip, WA - skip)]
-            )
-            total = part if total is None else total + part
-        return total
-
-    def norms(x, g_n1):
-        xhat, _ = normalize(x.astype(F32))
-        small_ref[0:8, :] += fold(g_n1 * xhat)
-        small_ref[8:16, :] += fold(g_n1)
-
-    def pull_halo(i, carry):
+    own = x_ref.shape[0]
+    small_ref[...] = small_halo[...]
+
+    def block(i, carry):
         rows = rows_of(i * 128, 128)
-        g_n1 = pull(i * 128, COLS)
-        gn_halo_ref[rows, :] = g_n1.astype(BF16)
-        norms(halo_ref[rows, :], g_n1)
-        return carry
-
-    lax.fori_loop(0, HALO // 128, pull_halo, 0)
-
-    def pull_own(i, carry):
-        rows = rows_of(i * 128, 128)
-        g_n1 = pull(HALO + i * 128, 0)
+        g_n1 = dot_t(g_ref[rows, :], w_ref[...])
         gn_ref[rows, :] = g_n1
-        norms(x_ref[rows, :], g_n1)
-        return carry
-
-    lax.fori_loop(0, own // 128, pull_own, 0)
-
-    ones = jnp.ones((8, ext), BF16)
-    for s, ref in enumerate(grads):
-        bias_ref[s] = dot(ones, ref[...])[0:1]
+        norm_sums(small_ref, x_ref[rows, :], g_n1)
+        return carry
+
+    lax.fori_loop(0, own // 128, block, 0)
     sums = lambda ref, j: jnp.sum(ref[8 * j : 8 * j + 8, :], axis=0, keepdims=True)
-    loss = jnp.sum(sums(small_in, 1), axis=1, keepdims=True) * scale_ref[4:5, 0:1]
+    loss = jnp.sum(sums(small_two, 1), axis=1, keepdims=True) * scale_ref[4:5, 0:1]
     vectors = jnp.concatenate(
-        [sums(small_ref, 0), sums(small_ref, 1), sums(small_in, 4), sums(small_in, 2), sums(small_in, 3),
-         sums(small_in, 0), jnp.zeros((2, D), F32)],
+        [sums(small_ref, 0), sums(small_ref, 1), sums(small_two, 4), sums(small_two, 2), sums(small_two, 3),
+         sums(small_two, 0), jnp.zeros((2, D), F32)],
         axis=0,
     )
     high = loss.astype(BF16).astype(F32)
     row, lane = lax.broadcasted_iota(jnp.int32, (EXTRA, 128), 0), lane_of((EXTRA, 128))
+    ones_own, ones_halo = jnp.ones((8, own), BF16), jnp.ones((8, HALO), BF16)
+
+    def grads(s, carry):
+        tp = lax.bitwise_and(place + s, 3)
+        g_own = g_ref[:, rows_of(tp * WA, WA)]
+        g_halo = gh_ref[:, rows_of(tp * 2 * COLS, 2 * COLS)]
+        total = dot(nto_ref[...], g_own)
+        more = dot(nth_ref[...], g_halo)
+        low = jnp.concatenate([total[:, 0:COLS], total[:, COLS:] + more], axis=1).astype(BF16)
+        by_own, by_halo = dot(ones_own, g_own)[0:1], dot(ones_halo, g_halo)[0:1]
+        ups = gbup_ref[0:1, rows_of(tp * FFC, FFC)]
+        mids = jnp.concatenate(
+            [by_own[:, 0:COLS], by_own[:, 2 * COLS :] + by_halo[:, COLS:]]
+            + [ups[:, 128 * j : 128 * j + 128] for j in range(4)]
+            + [jnp.zeros((2, 128), F32)],
+            axis=0,
+        ).astype(BF16)
+        for r in range(8):
+            dst = theirs_ref if r % 2 else mine_ref
+            dst[r // 2, s, 0:ROWS, :] = low[ROWS * r : ROWS * (r + 1)]
+            dst[r // 2, s, ROWS:, 128:256] = mids
+        return carry
+
+    lax.fori_loop(0, 4, grads, 0)
     for r in range(8):
         owner = lax.bitwise_xor(me, r)
         block = pltpu.roll(vectors, lax.rem(D - owner * ROWS, D), 1)[:, 0:128]
         block = jnp.where((row == 6) & (lane == 0), high, block)
-        block = jnp.where((row == 6) & (lane == 1), loss - high, block)
+        block = jnp.where((row == 6) & (lane == 1), loss - high, block).astype(BF16)
         dst = theirs_ref if r % 2 else mine_ref
         for s in range(4):
-            tp = lax.bitwise_and(place + s, 3)
-            ups = gbup_ref[0:1, rows_of(tp * FFC, FFC)]
-            mids = jnp.concatenate(
-                [bias_ref[s][:, 0:COLS], bias_ref[s][:, 2 * COLS :]]
-                + [ups[:, 128 * j : 128 * j + 128] for j in range(4)]
-                + [jnp.zeros((2, 128), F32)],
-                axis=0,
-            )
-            dst[r // 2, s, :, 0:128] = block.astype(BF16)
-            dst[r // 2, s, :, 128:256] = mids.astype(BF16)
-            dst[r // 2, s, :, 256:384] = jnp.zeros((EXTRA, 128), BF16)
-
-
-def pull_back(x, halo, grads, w, small_two, gbup, scale, theirs, mine):
-    own, ext = x.shape[0], grads[0].shape[0]
-    full = lambda a: pl.BlockSpec(a.shape, lambda i: (0,) * a.ndim)
-    send = jax.ShapeDtypeStruct(theirs.shape, BF16)
-    tail = pl.BlockSpec((4, 4, EXTRA, WA), lambda i: (0, 0, ROWS // EXTRA, 0))
-    given = (x, halo, *grads, w, small_two, gbup, scale)
-    return pl.pallas_call(
-        pull_kernel,
-        grid=(1,),
-        in_specs=[full(a) for a in given] + [ANY, ANY],
-        out_specs=[
-            pl.BlockSpec((HALO, D), lambda i: (0, 0)),
-            pl.BlockSpec((own, D), lambda i: (0, 0)),
-            tail,
-            tail,
-        ],
-        out_shape=(
-            jax.ShapeDtypeStruct((HALO, D), BF16),
-            jax.ShapeDtypeStruct((own, D), F32),
-            send,
-            send,
-        ),
-        scratch_shapes=[pltpu.VMEM((16, D), F32), pltpu.VMEM((4, 1, WA), F32)],
-        input_output_aliases={10: 2, 11: 3},
-        compiler_params=params(20),
+            dst[r // 2, s, ROWS:, 0:128] = block
+            dst[r // 2, s, ROWS:, 256:384] = jnp.zeros((EXTRA, 128), BF16)
+
+
+def own_back(x, g_halo, g_own, nt_halo, nt, w, small_halo, small_two, gbup, scale):
+    own = x.shape[0]
+    send = jax.ShapeDtypeStruct((4, 4, ROWS + EXTRA, WA), BF16)
+    return pl.pallas_call(
+        own_back_kernel,
+        out_shape=(jax.ShapeDtypeStruct((own, D), F32), send, send),
+        scratch_shapes=[pltpu.VMEM((16, D), F32), pltpu.VMEM((8, 128), F32)],
+        compiler_params=params(16),
         cost_estimate=SMALL,
-        name="pull_back",
-    )(*given, theirs, mine)
+        name="own_back",
+    )(x, g_halo, g_own, nt_halo, nt, w, small_halo, small_two, gbup, scale)
 
 
 def close_kernel(x_ref, gn_ref, back_ref, gh_ref, vec_ref, out_ref):
@@ -1323,61 +1434,60 @@
         (w_q, w_k, w_v, w_o.T, w_up, w_down.T, ln1_gain, ln1_bias, b_o, ln2_gain, ln2_bias, b_down, b_q, b_v, b_up,
          valid_mask)
     )
+    steps_a = [shard_a] + [to_step(shard_a, s) for s in (1, 2, 3)]
+    line_a = jnp.stack(steps_a)
+    steps_f = [shard_f] + [to_step(shard_f, s) for s in (1, 2, 3)]
+    over_f = [to_mask(x, 1) for x in steps_f]
+    near_a = [to_mask(line_a, m) for m in (2, 4, 6)]
+    halves_a = after([jnp.stack(steps_a[0:2]), jnp.stack(steps_a[2:4])], steps_f)
+    over_a = [to_mask(a, 1) for a in halves_a]
+    line_f = jnp.stack(after(steps_f, (over_a, near_a)))
+    pieces_a = [line_a] + near_a + over_a + [to_mask(a, 1) for a in near_a]
     halo = lax.ppermute(layer_input[own - HALO :], "tp", [(i, i + 1) for i in range(3)])
-    line_a = jnp.stack([shard_a] + [to_step(shard_a, s) for s in (1, 2, 3)])
-    near_a = [line_a] + [to_mask(line_a, m) for m in (2, 4, 6)]
-    pieces_a = near_a + [to_mask(a, 1) for a in near_a]
-    shard_f = after(shard_f, pieces_a[4])
-    steps_f = [shard_f] + [to_step(shard_f, s) for s in (1, 2, 3)]
+    f_x, f_y = to_mask(line_f, 2), to_mask(line_f, 4)
 
     ids = segment_ids + LEN * jnp.arange(segment_ids.shape[0], dtype=jnp.int32)[:, None]
     ids = jnp.concatenate([jnp.full((HALO,), -1, jnp.int32), ids.reshape(-1)])
     ids = lax.dynamic_slice_in_dim(ids, place * own, HALO + own)
     id_row, id_col = ids[None, :], ids[:, None]
     mask = valid_mask.astype(F32)[:, None]
-    where = place.reshape(1).astype(jnp.int32)
-
-    q, k, v, kt, nt, w_all, vec, bup, scale = project(layer_input, halo, pieces_a, tokens_all)
-    line_f = jnp.stack(after(steps_f, q))
-    q_a = after(q, line_f)
-    f_x, f_y = to_mask(line_f, 2), to_mask(line_f, 4)
-    o_a, lse_a = attend(q_a, k, v, id_row, id_col, 0, 2)
-    q_b = after(q, o_a)
-    o_b, lse_b = attend(q_b, k, v, id_row, id_col, 2, 2)
-    f_x, f_y = after((f_x, f_y), o_b)
-    near_f = [line_f, f_x, f_y, to_mask(f_y[0:2], 2), to_mask(f_x[2:4], 4)]
-    pieces_f = near_f + [to_mask(a, 1) for a in near_f]
+
+    q, k, v, kt, nt, w_all, vec, bup, scale, head = project(after(layer_input, over_f), pieces_a, tokens_all)
+    o, lse = attend_far(q, k, v, id_row, id_col)
+    f_x, f_y = after((f_x, f_y), o)
+    halo = after(halo, o)
+    f_xy = [to_mask(f_y[0:2], 2), to_mask(f_x[2:4], 4)]
+    k_halo, v_halo, kt_halo, nt_halo = project_halo(halo, w_all, vec, head)
+    o, lse = attend_near(0, q, k_halo, k, v_halo, v, id_row, id_col, o, lse)
+    o, lse = attend_near(2, q, k_halo, k, v_halo, v, id_row, id_col, o, lse)
+    near_f = [f_x, f_y] + after(f_xy, o)
+    pieces_f = [x[None] for x in steps_f] + near_f + [x[None] for x in over_f] + [to_mask(a, 1) for a in near_f]
     layer_out, g_h1, g_o, delta, theirs_f, mine_f, small_two, gbup = central(
-        layer_input, o_a, o_b, teacher, cotangent, mask, vec, bup, scale, pieces_f
-    )
-    lse = jnp.concatenate([lse_a, lse_b])
-
-    def backward(step, before):
-        return pair_backward(step, where, q, k, v, g_o, lse, delta, id_row, id_col, kt, nt, before)
-
-    g0, *sums = backward(0, ())
-    half = add(after(mine_f, g0), to_mask(theirs_f, 1))
+        layer_input, o, teacher, cotangent, mask, vec, bup, scale, pieces_f
+    )
+
+    def near(base, g_o, before):
+        return pull_near(base, q, g_o, k_halo, k, v_halo, v, lse, delta, id_row, id_col, kt_halo, kt, before)
+
+    begun = near(0, g_o, ())
+    half = add(after(mine_f, begun), to_mask(theirs_f, 1))
     from_x, from_y = to_mask(half[3, 0:2], 2), to_mask(half[3, 2:4], 4)
-    sums = after(sums, half)
-    g1, *sums = backward(1, sums)
-    from_x, from_y = after((from_x, from_y), g1)
+    g_halo, gq_near, part = near(2, after(g_o, half), begun)
+    gn_halo, small_halo = halo_back(g_halo, w_all, halo)
+    back = lax.ppermute(gn_halo, "tp", [(i + 1, i) for i in range(3)])
+    from_x, from_y = after((from_x, from_y), gn_halo)
     for_x = jnp.concatenate([half[1, 0:2], add(half[1, 2:4], from_y)])
     for_y = jnp.concatenate([add(half[2, 0:2], from_x), half[2, 2:4]])
     got_x, got_y = to_mask(for_x, 2), to_mask(for_y, 4)
-    sums = after(sums, (for_x, for_y))
-    g2, *sums = backward(2, sums)
-    g3, *sums = backward(3, sums)
-    got_x, got_y = after((got_x, got_y), g3)
+    g_own = pull_far(after(q, (for_x, for_y)), g_o, k, v, lse, delta, id_row, id_col, kt, gq_near, part)
+    gn_own, theirs_a, mine_a = own_back(
+        layer_input, g_halo, g_own, nt_halo, nt, w_all, small_halo, small_two, gbup, scale
+    )
+    got_x, got_y = after((got_x, got_y), gn_own)
     line = (half[0].astype(F32) + got_x.astype(F32) + got_y.astype(F32)).astype(BF16)
-    line_up = [line[s] for s in (1, 2, 3)]
-    sums = after(sums, line_up)
-    grad_wo, grad_wup, grad_wdn = unpack_f(line, *[to_step(line_up[s - 1], s) for s in (1, 2, 3)])
-
-    gn_halo, gn_own, theirs_a, mine_a = pull_back(
-        layer_input, halo, (g0, g1, g2, g3), w_all, small_two, gbup, scale, *sums
-    )
-    back = lax.ppermute(gn_halo, "tp", [(i + 1, i) for i in range(3)])
-    half = add(mine_a, to_mask(theirs_a, 1))
+    grad_wo, grad_wup, grad_wdn = unpack_f(line, *[to_step(line[s], s) for s in (1, 2, 3)])
+
+    half = add(mine_a, to_mask(after(theirs_a, back), 1))
     from_x, from_y, from_xy = (to_mask(half[m], 2 * m) for m in (1, 2, 3))
     line = (half[0].astype(F32) + from_x.astype(F32) + from_y.astype(F32) + from_xy.astype(F32)).astype(BF16)
     grad_wq, grad_wk, grad_wv, grad_bq, grad_bv, grad_bup, few = unpack_a(

time: 183 us -> 160 us (0.87)
  waiting for transfers between devices: 42.4 us -> 18.5 us
    ppermute x25 -> x29, waiting for transfers between devices: 22.4 us -> 7.84 us  [to_mask(): return lax.ppermute(x, 'fsdp', [(i, i ^ mask) for i in range(8)])]
    ppermute x1, waiting for transfers between devices: 9.33 us -> 1.61 us  [local_fast(): back = lax.ppermute(gn_halo, 'tp', [(i + 1, i) for i in range(3)])]
    ppermute x12, starting transfers between devices: 31.5 us -> 26.3 us  [to_step(): return lax.ppermute(x, 'tp', [(i, (i + step) % 4) for i in range(4)])]
    ppermute x25 -> x29, starting transfers between devices: 15.9 us -> 18.9 us  [to_mask(): return lax.ppermute(x, 'fsdp', [(i, i ^ mask) for i in range(8)])]
    unnamed x31 -> x36, local copies, waits for them, and re-layouts: 3.36 us -> 6.05 us
    slice x2, local copies, waits for them, and re-layouts: 2.08 us -> 0.05 us  [local_fast(): f_xy = [to_mask(f_y[0:2], 2), to_mask(f_x[2:4], 4)]]
    pallas_call x7 -> x9, Pallas kernels: 41.8 us -> 43.6 us  [the longest x2 12 us: pull_near(): pl.pallas_call(pull_near_kernel, grid=(2,), out_shape=(jax.ShapeDtypeStru...]
  transfers between devices with their start and end apart: 39 -> 43, of which waited for: 19 -> 14; matrix products, arithmetic and copies ran while one was open for 2% -> 4% of each run, Pallas kernels for 25% -> 33%
where the time goes in v3:
time: 160 us; the launch traced here: 159 us
  Pallas kernels  73.6 us (46%)
  starting transfers between devices  49.6 us (31%)
  waiting for transfers between devices  18.5 us (12%)
  local copies, waits for them, and re-layouts  8.74 us (5%)
  other arithmetic  5.17 us (3%)
  between operations  3.51 us (2%)
    ppermute x12, starting transfers between devices, to_step(): return lax.ppermute(x, 'tp', [(i, (i + step) % 4) for i in range(4)])  26.3 us
    ppermute x29, starting transfers between devices, to_mask(): return lax.ppermute(x, 'fsdp', [(i, i ^ mask) for i in range(8)])  18.9 us
    pallas_call x1, Pallas kernels, central(): pl.pallas_call(functools.partial(central_kernel, rb), out_shape=shapes, i...  18.7 us
    pallas_call x2, Pallas kernels, pull_near(): pl.pallas_call(pull_near_kernel, grid=(2,), out_shape=(jax.ShapeDtypeStru...  12 us
    pallas_call x2, Pallas kernels, attend_near(): pl.pallas_call(attend_near_kernel, grid=(2,), out_shape=(jax.ShapeDtypeSt...  9.43 us
    ppermute x12, waiting for transfers between devices, to_step(): return lax.ppermute(x, 'tp', [(i, (i + step) % 4) for i in range(4)])  9.04 us
    ppermute x29, waiting for transfers between devices, to_mask(): return lax.ppermute(x, 'fsdp', [(i, i ^ mask) for i in range(8)])  7.84 us
    pallas_call x1, Pallas kernels, own_back(): pl.pallas_call(own_back_kernel, out_shape=(jax.ShapeDtypeStruct((own, D),...  7.37 us
  transfers between devices with their start and end apart: 43, of which 14 were waited for; matrix products, arithmetic and copies ran while one was open for 4% of the time, Pallas kernels for 33%

profile of v3, /device:TPU:0, one launch (start us, length us, event | category | flops | bytes accessed | tf_op | source)
XLA Modules:
  0.0 159.1 jit_solution(3287852434497603909)
XLA Ops:
  0.7 1.9 %pack_weights.1 = (bf16[72,384]{1,0:T(8,128)(2,1)}, bf16[64,1152]{1,0:T(8,128)(2,1)}) custom-call(bf16[64,128]{1,0:T(8,128)(2,1)} %wq_ref.1, bf16[64,128]{1,0:T(8,128)(2,1)} %wk_ref.1, bf16[64,128]{1,0:T(8,128)(2,1)} %wv_ref.1, bf16[64,128]{1,0:T(8,128)(2,1)} %bitcast.100, bf16[64,512]{1,0:T(8,128)(2,1)} %wup_ref.1, bf16[64,512]{1,0:T(8,128)(2,1)} %bitcast.99, ...), custom_call_target="tpu_custom_call" | custom-call | tf_op jit(solution)/shard_map/pack_weights/pallas_call | solution.py:676
  2.6 5.0 %collective-permute-start.9 = (bf16[72,384]{1,0:T(8,128)(2,1)}, bf16[72,384]{1,0:T(8,128)(2,1)S(1)}, u32[]{:S(2)}, u32[]{:S(2)}) collective-permute-start(bf16[72,384]{1,0:T(8,128)(2,1)} %get-tuple-element.91), channel_id=1, source_target_pairs={{0,3},{1,0},{2,1},{3,2},{4,7},{5,4},{6,5},{7,6},{8,11},{9,8},{10,9... | collective-permute-start | bytes 165896 | tf_op jit(solution)/shard_map/ppermute | solution.py:1414
  8.6 2.8 %collective-permute-start.5 = (bf16[64,1152]{1,0:T(8,128)(2,1)}, bf16[64,1152]{1,0:T(8,128)(2,1)S(1)}, u32[]{:S(2)}, u32[]{:S(2)}) collective-permute-start(bf16[64,1152]{1,0:T(8,128)(2,1)} %get-tuple-element.110), channel_id=1, source_target_pairs={{0,3},{1,0},{2,1},{3,2},{4,7},{5,4},{6,5},{7,6},{8,11},{9,8},{10,9... | collective-permute-start | bytes 442376 | tf_op jit(solution)/shard_map/ppermute | solution.py:1414
  16.1 2.5 %collective-permute-start.12 = (bf16[4,72,384]{2,1,0:T(8,128)(2,1)S(1)}, bf16[4,72,384]{2,1,0:T(8,128)(2,1)S(1)}, u32[]{:S(2)}, u32[]{:S(2)}) collective-permute-start(bf16[4,72,384]{2,1,0:T(8,128)(2,1)S(1)} %pad_maximum_fusion.3.p0), channel_id=1, source_target_pairs={{0,24},{4,28},{8,16},{12,20},{16,8},{20,12},{24,0},{28,4},{1,25},{... | collective-permute-start | bytes 663560 | tf_op jit(solution)/shard_map/ppermute | solution.py:1410
  19.7 6.5 %collective-permute-done.3 = bf16[64,1152]{1,0:T(8,128)(2,1)S(1)} collective-permute-done((bf16[64,1152]{1,0:T(8,128)(2,1)}, bf16[64,1152]{1,0:T(8,128)(2,1)S(1)}, u32[]{:S(2)}, u32[]{:S(2)}) %collective-permute-start.3) | collective-permute-done | bytes 147488 | tf_op jit(solution)/shard_map/ppermute | solution.py:1414
  29.3 1.8 %pad_maximum_fusion = bf16[4,64,1152]{2,1,0:T(8,128)(2,1)} fusion(bf16[1,64,1152]{2,1,0:T(8,128)(2,1)S(1)} %bitcast.81, bf16[1,64,1152]{2,1,0:T(8,128)(2,1)S(1)} %bitcast.83, bf16[1,64,1152]{2,1,0:T(8,128)(2,1)S(1)} %bitcast.85, bf16[1,64,1152]{2,1,0:T(8,128)(2,1)} %bitcast.79), kind=kLoop, calls=%fused_computation.6 | loop fusion | flops 884736 | bytes 1179648 | tf_op jit(solution)/shard_map/stack | solution.py:1444
  31.2 1.5 collective-permute-start.20
  32.7 1.5 collective-permute-start.19
  36.5 3.1 %collective-permute-start.18 = (bf16[512,512]{1,0:T(8,128)(2,1)}, bf16[512,512]{1,0:T(8,128)(2,1)S(1)}, u32[]{:S(2)}, u32[]{:S(2)}) collective-permute-start(bf16[512,512]{1,0:T(8,128)(2,1)} %slice.84), channel_id=1, source_target_pairs={{0,1},{1,2},{2,3},{4,5},{5,6},{6,7},{8,9},{9,10},{10,11},{12,13},{... | collective-permute-start | bytes 1572872 | tf_op jit(solution)/shard_map/ppermute | solution.py:1446
  45.7 5.0 %project.1 = (bf16[768,512]{1,0:T(8,128)(2,1)S(1)}, bf16[768,512]{1,0:T(8,128)(2,1)S(1)}, bf16[768,512]{1,0:T(8,128)(2,1)S(1)}, bf16[512,768]{1,0:T(8,128)(2,1)S...) custom-call(bf16[768,512]{1,0:T(8,128)(2,1)S(1)} %copy-done, ...), custom_call_target="tpu_custom_call" | custom-call | flops 1 | bytes 1 | tf_op jit(solution)/shard_map/project/pallas_call | solution.py:783
  50.6 4.7 %attend_far.1 = (bf16[768,512]{1,0:T(8,128)(2,1)S(1)}, f32[4,8,768]{2,1,0:T(8,128)S(1)}) custom-call(bf16[768,512]{1,0:T(8,128)(2,1)S(1)} %get-tuple-element.135.q_ref, bf16[768,512]{1,0:T(8,128)(2,1)S(1)} %get-tuple-element.95.k_ref.ko_ref, bf16[768,512]{1,0:T(8,128)(2,1)S(1)} %get-tuple-element.96.v_ref.vo_ref, s32[1,1280]{1,0:T(1,128)S(1)} %broadcast_in_dim.35.idr_ref, ...), custom_call_target="tpu_custom_call" | custom-call | flops 1 | bytes 1 | tf_op jit(solution)/shard_map/attend_far/pallas_call | solution.py:865
  57.0 2.2 %project_halo.1 = (bf16[512,512]{1,0:T(8,128)(2,1)S(1)}, bf16[512,512]{1,0:T(8,128)(2,1)S(1)}, bf16[512,512]{1,0:T(8,128)(2,1)S(1)}, bf16[512,512]{1,0:T(8,128)(2,1)S(1)}) custom-call(bf16[512,512]{1,0:T(8,128)(2,1)S(1)} %collective-permute-done.18.x_ref, bf16[512,1536]{1,0:T(8,128)(2,1)S(1)} %get-tuple-element.99.w_ref, ...), custom_call_target="tpu_custom_call" | custom-call | flops 1 | bytes 1 | tf_op jit(solution)/shard_map/project_halo/pallas_call | solution.py:812
  59.2 4.7 %attend_near.2 = (bf16[768,512]{1,0:T(8,128)(2,1)S(1)}, f32[4,8,768]{2,1,0:T(8,128)S(1)}) custom-call(bf16[768,512]{1,0:T(8,128)(2,1)S(1)} %get-tuple-element.135.q_ref, bf16[512,512]{1,0:T(8,128)(2,1)S(1)} %get-tuple-element.102.kh_ref, bf16[768,512]{1,0:T(8,128)(2,1)S(1)} %get-tuple-element.95.k_ref.ko_ref, ...), custom_call_target="tpu_custom_call", output_to_operand_aliasing={{0}: (7, {}), {1}: (8, {})} | custom-call | flops 1 | bytes 1 | tf_op jit(solution)/shard_map/attend_near/pallas_call | solution.py:914
  64.0 4.7 %attend_near.3 = (bf16[768,512]{1,0:T(8,128)(2,1)S(1)}, f32[4,8,768]{2,1,0:T(8,128)S(1)}) custom-call(bf16[768,512]{1,0:T(8,128)(2,1)S(1)} %get-tuple-element.135.q_ref, bf16[512,512]{1,0:T(8,128)(2,1)S(1)} %get-tuple-element.102.kh_ref, bf16[768,512]{1,0:T(8,128)(2,1)S(1)} %get-tuple-element.95.k_ref.ko_ref, ...), custom_call_target="tpu_custom_call", output_to_operand_aliasing={{0}: (7, {}), {1}: (8, {})} | custom-call | flops 1 | bytes 1 | tf_op jit(solution)/shard_map/attend_near/pallas_call | solution.py:914
  70.9 18.7 %central.1 = (bf16[768,512]{1,0:T(8,128)(2,1)}, f32[768,512]{1,0:T(8,128)S(1)}, bf16[768,512]{1,0:T(8,128)(2,1)S(1)}, f32[4,8,768]{2,1,0:T(8,128)S(1)}, bf16[4,4...) custom-call(bf16[768,512]{1,0:T(8,128)(2,1)S(1)} %copy-done, ...), custom_call_target="tpu_custom_call" | custom-call | flops 1 | bytes 1 | tf_op jit(solution)/shard_map/central/pallas_call | solution.py:1054
  89.8 6.0 %pull_near.2 = (bf16[512,1024]{1,0:T(8,128)(2,1)S(1)}, bf16[512,512]{1,0:T(8,128)(2,1)S(1)}, f32[512,1024]{1,0:T(8,128)S(1)}) custom-call(bf16[768,512]{1,0:T(8,128)(2,1)S(1)} %get-tuple-element.135.q_ref, bf16[768,512]{1,0:T(8,128)(2,1)S(1)} %get-tuple-element.130.go_ref, bf16[512,512]{1,0:T(8,128)(2,1)S(1)} %get-tuple-element.102.kh_ref, ...), custom_call_target="tpu_custom_call" | custom-call | flops 1 | bytes 1 | tf_op jit(solution)/shard_map/pull_near/pallas_call | solution.py:1132
  96.7 1.5 collective-permute-start.29
  98.2 1.5 collective-permute-start.28
  99.7 6.0 %pull_near.3 = (bf16[512,1024]{1,0:T(8,128)(2,1)S(1)}, bf16[512,512]{1,0:T(8,128)(2,1)S(1)}, f32[512,1024]{1,0:T(8,128)S(1)}) custom-call(bf16[768,512]{1,0:T(8,128)(2,1)S(1)} %get-tuple-element.135.q_ref, bf16[768,512]{1,0:T(8,128)(2,1)S(1)} %get-tuple-element.130.go_ref, ...), custom_call_target="tpu_custom_call", output_to_operand_aliasing={{0}: (12, {}), {1}: (13, {}), {2}: (14, {})} | custom-call | flops 1 | bytes 1 | tf_op jit(solution)/shard_map/pull_near/pallas_call | solution.py:1132
  105.7 2.0 %halo_back.1 = (bf16[512,512]{1,0:T(8,128)(2,1)S(1)}, f32[16,512]{1,0:T(8,128)S(1)}) custom-call(bf16[512,1024]{1,0:T(8,128)(2,1)S(1)} %get-tuple-element.131.g_ref.gh_ref, bf16[512,1536]{1,0:T(8,128)(2,1)S(1)} %get-tuple-element.99.w_ref, bf16[512,512]{1,0:T(8,128)(2,1)S(1)} %collective-permute-done.18.x_ref), custom_call_target="tpu_custom_call" | custom-call | flops 1 | bytes 1 | tf_op jit(solution)/shard_map/halo_back/pallas_call | solution.py:1242
  110.5 6.0 %pull_far.1.g_ref = bf16[768,1536]{1,0:T(8,128)(2,1)S(1)} custom-call(bf16[768,512]{1,0:T(8,128)(2,1)S(1)} %get-tuple-element.135.q_ref, bf16[768,512]{1,0:T(8,128)(2,1)S(1)} %get-tuple-element.130.go_ref, bf16[768,512]{1,0:T(8,128)(2,1)S(1)} %get-tuple-element.95.k_ref.ko_ref, bf16[768,512]{1,0:T(8,128)(2,1)S(1)} %get-tuple-element.96.v_ref.vo_ref, ...), custom_call_target="tpu_custom_call" | custom-call | flops 1 | bytes 1 | tf_op jit(solution)/shard_map/pull_far/pallas_call | solution.py:1190
  116.4 7.4 %own_back.1 = (f32[768,512]{1,0:T(8,128)S(1)}, bf16[4,4,72,384]{3,2,1,0:T(8,128)(2,1)S(1)}, bf16[4,4,72,384]{3,2,1,0:T(8,128)(2,1)S(1)}) custom-call(bf16[768,512]{1,0:T(8,128)(2,1)S(1)} %copy-done, bf16[512,1024]{1,0:T(8,128)(2,1)S(1)} %get-tuple-element.131.g_ref.gh_ref, bf16[768,1536]{1,0:T(8,128)(2,1)S(1)} %pull_far.1.g_ref, ...), custom_call_target="tpu_custom_call" | custom-call | flops 1 | bytes 1 | tf_op jit(solution)/shard_map/own_back/pallas_call | solution.py:1314
  123.8 1.6 %collective-permute-done.30.back_ref = bf16[512,512]{1,0:T(8,128)(2,1)S(1)} collective-permute-done((bf16[512,512]{1,0:T(8,128)(2,1)S(1)}, bf16[512,512]{1,0:T(8,128)(2,1)S(1)}, u32[]{:S(2)}, u32[]{:S(2)}) %collective-permute-start.30) | collective-permute-done | bytes 524320 | tf_op jit(solution)/shard_map/ppermute | solution.py:1477
  125.7 2.2 %collective-permute-done.31 = bf16[4,4,72,384]{3,2,1,0:T(8,128)(2,1)S(1)} collective-permute-done((bf16[4,4,72,384]{3,2,1,0:T(8,128)(2,1)S(1)}, bf16[4,4,72,384]{3,2,1,0:T(8,128)(2,1)S(1)}, u32[]{:S(2)}, u32[]{:S(2)}) %collective-permute-start.31) | collective-permute-done | bytes 884768 | tf_op jit(solution)/shard_map/ppermute | solution.py:1410
  128.2 1.3 collective-permute-start.32
  129.5 1.5 collective-permute-start.34
  131.8 5.0 %collective-permute-start.42 = (bf16[64,1152]{1,0:T(8,128)(2,1)S(1)}, bf16[64,1152]{1,0:T(8,128)(2,1)S(1)}, u32[]{:S(2)}, u32[]{:S(2)}) collective-permute-start(bf16[64,1152]{1,0:T(8,128)(2,1)S(1)} %get-tuple-element.169), channel_id=1, source_target_pairs={{0,3},{1,0},{2,1},{3,2},{4,7},{5,4},{6,5},{7,6},{8,11},{9,8},{10,9... | collective-permute-start | bytes 442376 | tf_op jit(solution)/shard_map/ppermute | solution.py:1414
  137.3 3.2 %collective-permute-start.40 = (bf16[64,1152]{1,0:T(8,128)(2,1)S(1)}, bf16[64,1152]{1,0:T(8,128)(2,1)S(1)}, u32[]{:S(2)}, u32[]{:S(2)}) collective-permute-start(bf16[64,1152]{1,0:T(8,128)(2,1)S(1)} %get-tuple-element.171), channel_id=1, source_target_pairs={{0,1},{1,2},{2,3},{3,0},{4,5},{5,6},{6,7},{7,4},{8,9},{9,10},{10,1... | collective-permute-start | bytes 442376 | tf_op jit(solution)/shard_map/ppermute | solution.py:1414
  141.3 1.4 collective-permute-done.33
  142.8 5.1 %collective-permute-start.37 = (bf16[72,384]{1,0:T(8,128)(2,1)S(1)}, bf16[72,384]{1,0:T(8,128)(2,1)S(1)}, u32[]{:S(2)}, u32[]{:S(2)}) collective-permute-start(bf16[72,384]{1,0:T(8,128)(2,1)S(1)} %get-tuple-element.172), channel_id=1, source_target_pairs={{0,3},{1,0},{2,1},{3,2},{4,7},{5,4},{6,5},{7,6},{8,11},{9,8},{10,9... | collective-permute-start | bytes 165896 | tf_op jit(solution)/shard_map/ppermute | solution.py:1414
  148.5 1.9 %collective-permute-start.35 = (bf16[72,384]{1,0:T(8,128)(2,1)S(1)}, bf16[72,384]{1,0:T(8,128)(2,1)S(1)}, u32[]{:S(2)}, u32[]{:S(2)}) collective-permute-start(bf16[72,384]{1,0:T(8,128)(2,1)S(1)} %get-tuple-element.174), channel_id=1, source_target_pairs={{0,1},{1,2},{2,3},{3,0},{4,5},{5,6},{6,7},{7,4},{8,9},{9,10},{10,1... | collective-permute-start | bytes 165896 | tf_op jit(solution)/shard_map/ppermute | solution.py:1414
  150.4 3.0 %close.1 = f32[768,512]{1,0:T(8,128)} custom-call(bf16[768,512]{1,0:T(8,128)(2,1)S(1)} %copy-done, f32[768,512]{1,0:T(8,128)S(1)} %get-tuple-element.147.gn_ref, bf16[512,512]{1,0:T(8,128)(2,1)S(1)} %collective-permute-done.30.back_ref, f32[768,512]{1,0:T(8,128)S(1)} %get-tuple-element.148.gh_ref, f32[8,512]{1,0:T(8,128)S(1)} %get-tuple-element.100.vec_ref), custom_call_target="tpu_custom_call" | custom-call | flops 1 | bytes 1 | tf_op jit(solution)/shard_map/close/pallas_call | solution.py:1346
  (133 shorter events, 32.5 us)
Async XLA Ops:
  2.6 10.0 %collective-permute-start.9 = (bf16[72,384]{1,0:T(8,128)(2,1)}, bf16[72,384]{1,0:T(8,128)(2,1)S(1)}, u32[]{:S(2)}, u32[]{:S(2)}) collective-permute-start(bf16[72,384]{1,0:T(8,128)(2,1)} %get-tuple-element.91), channel_id=1, source_target_pairs={{0,3},{1,0},{2,1},{3,2},{4,7},{5,4},{6,5},{7,6},{8,11},{9,8},{10,9... | collective-permute-start | bytes 165896 | tf_op jit(solution)/shard_map/ppermute | solution.py:1414
  7.6 6.2 %collective-permute-start.8 = (bf16[72,384]{1,0:T(8,128)(2,1)}, bf16[72,384]{1,0:T(8,128)(2,1)S(1)}, u32[]{:S(2)}, u32[]{:S(2)}) collective-permute-start(bf16[72,384]{1,0:T(8,128)(2,1)} %get-tuple-element.91), channel_id=1, source_target_pairs={{0,2},{1,3},{2,0},{3,1},{4,6},{5,7},{6,4},{7,5},{8,10},{9,11},{10,... | collective-permute-start | bytes 165896 | tf_op jit(solution)/shard_map/ppermute | solution.py:1414
  7.6 6.8 %collective-permute-start.7 = (bf16[72,384]{1,0:T(8,128)(2,1)}, bf16[72,384]{1,0:T(8,128)(2,1)S(1)}, u32[]{:S(2)}, u32[]{:S(2)}) collective-permute-start(bf16[72,384]{1,0:T(8,128)(2,1)} %get-tuple-element.91), channel_id=1, source_target_pairs={{0,1},{1,2},{2,3},{3,0},{4,5},{5,6},{6,7},{7,4},{8,9},{9,10},{10,1... | collective-permute-start | bytes 165896 | tf_op jit(solution)/shard_map/ppermute | solution.py:1414
  8.6 10.5 %collective-permute-start.5 = (bf16[64,1152]{1,0:T(8,128)(2,1)}, bf16[64,1152]{1,0:T(8,128)(2,1)S(1)}, u32[]{:S(2)}, u32[]{:S(2)}) collective-permute-start(bf16[64,1152]{1,0:T(8,128)(2,1)} %get-tuple-element.110), channel_id=1, source_target_pairs={{0,3},{1,0},{2,1},{3,2},{4,7},{5,4},{6,5},{7,6},{8,11},{9,8},{10,9... | collective-permute-start | bytes 442376 | tf_op jit(solution)/shard_map/ppermute | solution.py:1414
  11.5 14.7 %collective-permute-start.3 = (bf16[64,1152]{1,0:T(8,128)(2,1)}, bf16[64,1152]{1,0:T(8,128)(2,1)S(1)}, u32[]{:S(2)}, u32[]{:S(2)}) collective-permute-start(bf16[64,1152]{1,0:T(8,128)(2,1)} %get-tuple-element.110), channel_id=1, source_target_pairs={{0,2},{1,3},{2,0},{3,1},{4,6},{5,7},{6,4},{7,5},{8,10},{9,11},{10,... | collective-permute-start | bytes 442376 | tf_op jit(solution)/shard_map/ppermute | solution.py:1414
  12.6 13.6 %collective-permute-start.1 = (bf16[64,1152]{1,0:T(8,128)(2,1)}, bf16[64,1152]{1,0:T(8,128)(2,1)S(1)}, u32[]{:S(2)}, u32[]{:S(2)}) collective-permute-start(bf16[64,1152]{1,0:T(8,128)(2,1)} %get-tuple-element.110), channel_id=1, source_target_pairs={{0,1},{1,2},{2,3},{3,0},{4,5},{5,6},{6,7},{7,4},{8,9},{9,10},{10,1... | collective-permute-start | bytes 442376 | tf_op jit(solution)/shard_map/ppermute | solution.py:1414
  16.1 13.2 %collective-permute-start.12 = (bf16[4,72,384]{2,1,0:T(8,128)(2,1)S(1)}, bf16[4,72,384]{2,1,0:T(8,128)(2,1)S(1)}, u32[]{:S(2)}, u32[]{:S(2)}) collective-permute-start(bf16[4,72,384]{2,1,0:T(8,128)(2,1)S(1)} %pad_maximum_fusion.3.p0), channel_id=1, source_target_pairs={{0,24},{4,28},{8,16},{12,20},{16,8},{20,12},{24,0},{28,4},{1,25},{... | collective-permute-start | bytes 663560 | tf_op jit(solution)/shard_map/ppermute | solution.py:1410
  18.6 10.7 %collective-permute-start.11 = (bf16[4,72,384]{2,1,0:T(8,128)(2,1)S(1)}, bf16[4,72,384]{2,1,0:T(8,128)(2,1)}, u32[]{:S(2)}, u32[]{:S(2)}) collective-permute-start(bf16[4,72,384]{2,1,0:T(8,128)(2,1)S(1)} %pad_maximum_fusion.3.p0), channel_id=1, source_target_pairs={{0,16},{4,20},{8,24},{12,28},{16,0},{20,4},{24,8},{28,12},{1,17},{... | collective-permute-start | bytes 663560 | tf_op jit(solution)/shard_map/ppermute | solution.py:1410
  19.2 10.2 %collective-permute-start.10 = (bf16[4,72,384]{2,1,0:T(8,128)(2,1)S(1)}, bf16[4,72,384]{2,1,0:T(8,128)(2,1)}, u32[]{:S(2)}, u32[]{:S(2)}) collective-permute-start(bf16[4,72,384]{2,1,0:T(8,128)(2,1)S(1)} %pad_maximum_fusion.3.p0), channel_id=1, source_target_pairs={{0,8},{4,12},{8,0},{12,4},{16,24},{20,28},{24,16},{28,20},{1,9},{5... | collective-permute-start | bytes 663560 | tf_op jit(solution)/shard_map/ppermute | solution.py:1410
  31.2 24.1 %collective-permute-start.20 = (bf16[4,64,1152]{2,1,0:T(8,128)(2,1)}, bf16[4,64,1152]{2,1,0:T(8,128)(2,1)S(1)}, u32[]{:S(2)}, u32[]{:S(2)}) collective-permute-start(bf16[4,64,1152]{2,1,0:T(8,128)(2,1)} %pad_maximum_fusion), channel_id=1, source_target_pairs={{0,16},{4,20},{8,24},{12,28},{16,0},{20,4},{24,8},{28,12},{1,17},{... | collective-permute-start | bytes 1769480 | tf_op jit(solution)/shard_map/ppermute | solution.py:1410
  32.7 22.6 %collective-permute-start.19 = (bf16[4,64,1152]{2,1,0:T(8,128)(2,1)}, bf16[4,64,1152]{2,1,0:T(8,128)(2,1)S(1)}, u32[]{:S(2)}, u32[]{:S(2)}) collective-permute-start(bf16[4,64,1152]{2,1,0:T(8,128)(2,1)} %pad_maximum_fusion), channel_id=1, source_target_pairs={{0,8},{4,12},{8,0},{12,4},{16,24},{20,28},{24,16},{28,20},{1,9},{5... | collective-permute-start | bytes 1769480 | tf_op jit(solution)/shard_map/ppermute | solution.py:1410
  34.2 6.1 %collective-permute-start.17 = (bf16[4,72,384]{2,1,0:T(8,128)(2,1)S(1)}, bf16[4,72,384]{2,1,0:T(8,128)(2,1)S(1)}, u32[]{:S(2)}, u32[]{:S(2)}) collective-permute-start(bf16[4,72,384]{2,1,0:T(8,128)(2,1)S(1)} %collective-permute-done.12.p3), channel_id=1, source_target_pairs={{0,4},{4,0},{8,12},{12,8},{16,20},{20,16},{24,28},{28,24},{1,5},{5... | collective-permute-start | bytes 663560 | tf_op jit(solution)/shard_map/ppermute | solution.py:1410
  36.5 20.5 %collective-permute-start.18 = (bf16[512,512]{1,0:T(8,128)(2,1)}, bf16[512,512]{1,0:T(8,128)(2,1)S(1)}, u32[]{:S(2)}, u32[]{:S(2)}) collective-permute-start(bf16[512,512]{1,0:T(8,128)(2,1)} %slice.84), channel_id=1, source_target_pairs={{0,1},{1,2},{2,3},{4,5},{5,6},{6,7},{8,9},{9,10},{10,11},{12,13},{... | collective-permute-start | bytes 1572872 | tf_op jit(solution)/shard_map/ppermute | solution.py:1446
  55.4 13.4 %collective-permute-start.21 = (bf16[2,64,1152]{2,1,0:T(8,128)(2,1)S(1)}, bf16[2,64,1152]{2,1,0:T(8,128)(2,1)S(1)}, u32[]{:S(2)}, u32[]{:S(2)}) collective-permute-start(bf16[2,64,1152]{2,1,0:T(8,128)(2,1)S(1)} %slice.85), channel_id=1, source_target_pairs={{0,8},{4,12},{8,0},{12,4},{16,24},{20,28},{24,16},{28,20},{1,9},{5... | collective-permute-start | bytes 884744 | tf_op jit(solution)/shard_map/ppermute | solution.py:1410
  56.0 12.8 %collective-permute-start.22 = (bf16[2,64,1152]{2,1,0:T(8,128)(2,1)S(1)}, bf16[2,64,1152]{2,1,0:T(8,128)(2,1)S(1)}, u32[]{:S(2)}, u32[]{:S(2)}) collective-permute-start(bf16[2,64,1152]{2,1,0:T(8,128)(2,1)S(1)} %slice.86), channel_id=1, source_target_pairs={{0,16},{4,20},{8,24},{12,28},{16,0},{20,4},{24,8},{28,12},{1,17},{... | collective-permute-start | bytes 884744 | tf_op jit(solution)/shard_map/ppermute | solution.py:1410
  56.5 13.0 %collective-permute-start.23 = (bf16[4,64,1152]{2,1,0:T(8,128)(2,1)S(1)}, bf16[4,64,1152]{2,1,0:T(8,128)(2,1)S(1)}, u32[]{:S(2)}, u32[]{:S(2)}) collective-permute-start(bf16[4,64,1152]{2,1,0:T(8,128)(2,1)S(1)} %collective-permute-done.19.rest_4_), channel_id=1, source_target_pairs={{0,4},{4,0},{8,12},{12,8},{16,20},{20,16},{24,28},{28,24},{1,5},{5... | collective-permute-start | bytes 1769480 | tf_op jit(solution)/shard_map/ppermute | solution.py:1410
  56.5 13.0 %collective-permute-start.24 = (bf16[4,64,1152]{2,1,0:T(8,128)(2,1)S(1)}, bf16[4,64,1152]{2,1,0:T(8,128)(2,1)S(1)}, u32[]{:S(2)}, u32[]{:S(2)}) collective-permute-start(bf16[4,64,1152]{2,1,0:T(8,128)(2,1)S(1)} %collective-permute-done.20.rest_5_), channel_id=1, source_target_pairs={{0,4},{4,0},{8,12},{12,8},{16,20},{20,16},{24,28},{28,24},{1,5},{5... | collective-permute-start | bytes 1769480 | tf_op jit(solution)/shard_map/ppermute | solution.py:1410
  89.6 6.2 %collective-permute-start.27 = (bf16[4,4,64,1152]{3,2,1,0:T(8,128)(2,1)S(1)}, bf16[4,4,64,1152]{3,2,1,0:T(8,128)(2,1)S(1)}, u32[]{:S(2)}, u32[]{:S(2)}) collective-permute-start(bf16[4,4,64,1152]{3,2,1,0:T(8,128)(2,1)S(1)} %get-tuple-element.129), channel_id=1, source_target_pairs={{0,4},{4,0},{8,12},{12,8},{16,20},{20,16},{24,28},{28,24},{1,5},{5... | collective-permute-start | bytes 7077896 | tf_op jit(solution)/shard_map/ppermute | solution.py:1410
  96.7 12.3 %collective-permute-start.29 = (bf16[2,64,1152]{2,1,0:T(8,128)(2,1)S(1)}, bf16[2,64,1152]{2,1,0:T(8,128)(2,1)S(1)}, u32[]{:S(2)}, u32[]{:S(2)}) collective-permute-start(bf16[2,64,1152]{2,1,0:T(8,128)(2,1)S(1)} %get-tuple-element.163), channel_id=1, source_target_pairs={{0,16},{4,20},{8,24},{12,28},{16,0},{20,4},{24,8},{28,12},{1,17},{... | collective-permute-start | bytes 884744 | tf_op jit(solution)/shard_map/ppermute | solution.py:1410
  98.2 10.8 %collective-permute-start.28 = (bf16[2,64,1152]{2,1,0:T(8,128)(2,1)S(1)}, bf16[2,64,1152]{2,1,0:T(8,128)(2,1)S(1)}, u32[]{:S(2)}, u32[]{:S(2)}) collective-permute-start(bf16[2,64,1152]{2,1,0:T(8,128)(2,1)S(1)} %get-tuple-element.164), channel_id=1, source_target_pairs={{0,8},{4,12},{8,0},{12,4},{16,24},{20,28},{24,16},{28,20},{1,9},{5... | collective-permute-start | bytes 884744 | tf_op jit(solution)/shard_map/ppermute | solution.py:1410
  107.7 17.8 %collective-permute-start.30 = (bf16[512,512]{1,0:T(8,128)(2,1)S(1)}, bf16[512,512]{1,0:T(8,128)(2,1)S(1)}, u32[]{:S(2)}, u32[]{:S(2)}) collective-permute-start(bf16[512,512]{1,0:T(8,128)(2,1)S(1)} %get-tuple-element.132), channel_id=1, source_target_pairs={{1,0},{2,1},{3,2},{5,4},{6,5},{7,6},{9,8},{10,9},{11,10},{13,12},{... | collective-permute-start | bytes 1572872 | tf_op jit(solution)/shard_map/ppermute | solution.py:1477
  109.2 16.2 %collective-permute-start.38 = (bf16[4,64,1152]{2,1,0:T(8,128)(2,1)S(1)}, bf16[4,64,1152]{2,1,0:T(8,128)(2,1)S(1)}, u32[]{:S(2)}, u32[]{:S(2)}) collective-permute-start(bf16[4,64,1152]{2,1,0:T(8,128)(2,1)S(1)} %pad_maximum_fusion.1), channel_id=1, source_target_pairs={{0,8},{4,12},{8,0},{12,4},{16,24},{20,28},{24,16},{28,20},{1,9},{5... | collective-permute-start | bytes 1769480 | tf_op jit(solution)/shard_map/ppermute | solution.py:1410
  109.9 15.6 %collective-permute-start.39 = (bf16[4,64,1152]{2,1,0:T(8,128)(2,1)S(1)}, bf16[4,64,1152]{2,1,0:T(8,128)(2,1)S(1)}, u32[]{:S(2)}, u32[]{:S(2)}) collective-permute-start(bf16[4,64,1152]{2,1,0:T(8,128)(2,1)S(1)} %pad_maximum_fusion.2), channel_id=1, source_target_pairs={{0,16},{4,20},{8,24},{12,28},{16,0},{20,4},{24,8},{28,12},{1,17},{... | collective-permute-start | bytes 1769480 | tf_op jit(solution)/shard_map/ppermute | solution.py:1410
  128.2 9.1 %collective-permute-start.32 = (bf16[4,72,384]{2,1,0:T(8,128)(2,1)S(1)}, bf16[4,72,384]{2,1,0:T(8,128)(2,1)S(1)}, u32[]{:S(2)}, u32[]{:S(2)}) collective-permute-start(bf16[4,72,384]{2,1,0:T(8,128)(2,1)S(1)} %get-tuple-element.166), channel_id=1, source_target_pairs={{0,8},{4,12},{8,0},{12,4},{16,24},{20,28},{24,16},{28,20},{1,9},{5... | collective-permute-start | bytes 663560 | tf_op jit(solution)/shard_map/ppermute | solution.py:1410
  129.5 11.8 %collective-permute-start.34 = (bf16[4,72,384]{2,1,0:T(8,128)(2,1)S(1)}, bf16[4,72,384]{2,1,0:T(8,128)(2,1)S(1)}, u32[]{:S(2)}, u32[]{:S(2)}) collective-permute-start(bf16[4,72,384]{2,1,0:T(8,128)(2,1)S(1)} %get-tuple-element.167), channel_id=1, source_target_pairs={{0,24},{4,28},{8,16},{12,20},{16,8},{20,12},{24,0},{28,4},{1,25},{... | collective-permute-start | bytes 663560 | tf_op jit(solution)/shard_map/ppermute | solution.py:1410
  131.0 11.6 %collective-permute-start.33 = (bf16[4,72,384]{2,1,0:T(8,128)(2,1)S(1)}, bf16[4,72,384]{2,1,0:T(8,128)(2,1)S(1)}, u32[]{:S(2)}, u32[]{:S(2)}) collective-permute-start(bf16[4,72,384]{2,1,0:T(8,128)(2,1)S(1)} %get-tuple-element.168), channel_id=1, source_target_pairs={{0,16},{4,20},{8,24},{12,28},{16,0},{20,4},{24,8},{28,12},{1,17},{... | collective-permute-start | bytes 663560 | tf_op jit(solution)/shard_map/ppermute | solution.py:1410
  131.8 16.7 %collective-permute-start.42 = (bf16[64,1152]{1,0:T(8,128)(2,1)S(1)}, bf16[64,1152]{1,0:T(8,128)(2,1)S(1)}, u32[]{:S(2)}, u32[]{:S(2)}) collective-permute-start(bf16[64,1152]{1,0:T(8,128)(2,1)S(1)} %get-tuple-element.169), channel_id=1, source_target_pairs={{0,3},{1,0},{2,1},{3,2},{4,7},{5,4},{6,5},{7,6},{8,11},{9,8},{10,9... | collective-permute-start | bytes 442376 | tf_op jit(solution)/shard_map/ppermute | solution.py:1414
  136.8 16.6 %collective-permute-start.41 = (bf16[64,1152]{1,0:T(8,128)(2,1)S(1)}, bf16[64,1152]{1,0:T(8,128)(2,1)S(1)}, u32[]{:S(2)}, u32[]{:S(2)}) collective-permute-start(bf16[64,1152]{1,0:T(8,128)(2,1)S(1)} %get-tuple-element.170), channel_id=1, source_target_pairs={{0,2},{1,3},{2,0},{3,1},{4,6},{5,7},{6,4},{7,5},{8,10},{9,11},{10,... | collective-permute-start | bytes 442376 | tf_op jit(solution)/shard_map/ppermute | solution.py:1414
  137.3 16.1 %collective-permute-start.40 = (bf16[64,1152]{1,0:T(8,128)(2,1)S(1)}, bf16[64,1152]{1,0:T(8,128)(2,1)S(1)}, u32[]{:S(2)}, u32[]{:S(2)}) collective-permute-start(bf16[64,1152]{1,0:T(8,128)(2,1)S(1)} %get-tuple-element.171), channel_id=1, source_target_pairs={{0,1},{1,2},{2,3},{3,0},{4,5},{5,6},{6,7},{7,4},{8,9},{9,10},{10,1... | collective-permute-start | bytes 442376 | tf_op jit(solution)/shard_map/ppermute | solution.py:1414
  142.8 11.3 %collective-permute-start.37 = (bf16[72,384]{1,0:T(8,128)(2,1)S(1)}, bf16[72,384]{1,0:T(8,128)(2,1)S(1)}, u32[]{:S(2)}, u32[]{:S(2)}) collective-permute-start(bf16[72,384]{1,0:T(8,128)(2,1)S(1)} %get-tuple-element.172), channel_id=1, source_target_pairs={{0,3},{1,0},{2,1},{3,2},{4,7},{5,4},{6,5},{7,6},{8,11},{9,8},{10,9... | collective-permute-start | bytes 165896 | tf_op jit(solution)/shard_map/ppermute | solution.py:1414
  147.9 6.9 %collective-permute-start.36 = (bf16[72,384]{1,0:T(8,128)(2,1)S(1)}, bf16[72,384]{1,0:T(8,128)(2,1)S(1)}, u32[]{:S(2)}, u32[]{:S(2)}) collective-permute-start(bf16[72,384]{1,0:T(8,128)(2,1)S(1)} %get-tuple-element.173), channel_id=1, source_target_pairs={{0,2},{1,3},{2,0},{3,1},{4,6},{5,7},{6,4},{7,5},{8,10},{9,11},{10,... | collective-permute-start | bytes 165896 | tf_op jit(solution)/shard_map/ppermute | solution.py:1414
  148.5 6.3 %collective-permute-start.35 = (bf16[72,384]{1,0:T(8,128)(2,1)S(1)}, bf16[72,384]{1,0:T(8,128)(2,1)S(1)}, u32[]{:S(2)}, u32[]{:S(2)}) collective-permute-start(bf16[72,384]{1,0:T(8,128)(2,1)S(1)} %get-tuple-element.174), channel_id=1, source_target_pairs={{0,1},{1,2},{2,3},{3,0},{4,5},{5,6},{6,7},{7,4},{8,9},{9,10},{10,1... | collective-permute-start | bytes 165896 | tf_op jit(solution)/shard_map/ppermute | solution.py:1414
  (29 other events, 160.1 us)
